TPU v7x, 512 devices: a whole 4x8x8 slice. The times are simulated.
512 devices in a mesh: slab: 32 (over y, x), band: 16 (over z, core).
Axes of the slice: x: 4, y: 8, z: 8, core: 2. Of those that a mesh axis runs over, the one named last changes fastest.
Arguments:
- basis: float32 [3, 512, 49152], P(None, 'slab', 'band')
- offsets: float32 [3, 512, 256], P(None, 'slab', 'band'), may hold values from -0.45 to 0.45
- bond_modulus: float32 [512, 256], P('slab', 'band'), may hold values from 0.5 to 2
- bulk_modulus: float32 [512, 256], P('slab', 'band'), may hold values from 0.5 to 2
- springs: float32 [512, 256], P('slab', 'band'), may hold values from 0.5 to 2
- intact: int32 [32, 32, 9], P('slab', 'band'), may hold values from 0 to 1, as said below
Outputs:
- new_modes: float32 [3, 512, 16384], P(None, 'slab', 'band')
- new_images: float32 [3, 512, 16384], P(None, 'slab', 'band')
- reduced: float32 [64, 64], replicated
Inputs may be any that keep to these rules, and one draw needn't show every extreme that they name: intact[i, j, 3 (dx + 1) + (dy + 1)] is 1 where the bonds between block (i, j) and block (i + dx, j + dy) are intact, and 0 where they are broken or that block lies outside the plate; the entry for (0, 0) is always 1, and the entry for (dx, dy) of one block equals the entry for (-dx, -dy) of the other.
All inputs are finite; a program needn't handle non-finite values.
Results may differ from a plain program's by a relative error of at most 0.0003.
Values sent between devices are 32-bit elements; how exact they have to be, the bound alone decides.
No kernel may reach another device: no remote copies, remote signals or barrier semaphores. Data moves between devices by JAX's collectives and lax.ppermute only.
A program may use at most 128 MiB of HBM per device.

v0:
```python
import jax
import jax.numpy as jnp
from jax import lax
from jax.sharding import PartitionSpec as P

BLOCK_X = 16
BLOCK_Y = 8
REACH = 3
MODES = 64
NCOL = 192


horizon_square = 9.0
bond_scale = 1.0 / 18.0
dilation_scale = 1.0 / 27.0
highest = lax.Precision.HIGHEST


def padded(value, sides, width):
    for axis, dim in sides:
        size, length = (lax.axis_size(axis), value.shape[dim])
        up = [(i, (i + 1) % size) for i in range(size - 1)]
        down = [(j, i) for i, j in up]
        last = lax.slice_in_dim(value, length - width, length, axis=dim)
        first = lax.slice_in_dim(value, 0, width, axis=dim)
        before = lax.ppermute(last, axis, up)
        after = lax.ppermute(first, axis, down)
        value = jnp.concatenate([before, value, after], axis=dim)
    return value


def window(array, margin, region):
    start_x, count_x, start_y, count_y = region
    piece = array[
        :,
        start_x + margin : start_x + margin + count_x,
        start_y + margin : start_y + margin + count_y,
    ]
    return piece.reshape((piece.shape[0], count_x * count_y) + piece.shape[3:])


def widened(region):
    start_x, count_x, start_y, count_y = region
    return (start_x - REACH, count_x + 2 * REACH, start_y - REACH, count_y + 2 * REACH)


def lattice(region):
    start_x, count_x, start_y, count_y = region
    along_x = jnp.repeat(jnp.arange(start_x, start_x + count_x, dtype=jnp.int32), count_y)
    along_y = jnp.tile(jnp.arange(start_y, start_y + count_y, dtype=jnp.int32), count_x)
    return (along_x, along_y)


def pair_geometry(geometry, margin, region, bond_table, table_shift):
    home_geometry = window(geometry, margin, region)
    far_geometry = window(geometry, margin, widened(region))
    home_x, home_y = lattice(region)
    far_x, far_y = lattice(widened(region))
    home_block_x = jnp.floor_divide(home_x, BLOCK_X)
    home_block_y = jnp.floor_divide(home_y, BLOCK_Y)
    offset_code = 3 * (jnp.floor_divide(far_x, BLOCK_X)[None, :] - home_block_x[:, None] + 1) + (
        jnp.floor_divide(far_y, BLOCK_Y)[None, :] - home_block_y[:, None] + 1
    )
    select_rows = (
        home_block_x[:, None] + table_shift
        == jnp.arange(bond_table.shape[0], dtype=jnp.int32)[None, :]
    ).astype(jnp.float32)
    select_cols = (
        home_block_y[:, None] + table_shift
        == jnp.arange(bond_table.shape[1], dtype=jnp.int32)[None, :]
    ).astype(jnp.float32)
    home_bonds = jnp.einsum(
        "na,nb,abo->no", select_rows, select_cols, bond_table.astype(jnp.float32), precision=highest
    )
    intact_mask = jnp.zeros(offset_code.shape, jnp.float32)
    for offset in range(9):
        intact_mask = intact_mask + jnp.where(
            offset_code == offset, home_bonds[:, offset][:, None], 0.0
        )
    bond_vector = jnp.stack(
        [
            (far_x[None, :] - home_x[:, None]).astype(jnp.float32)
            + far_geometry[0][None, :]
            - home_geometry[0][:, None],
            (far_y[None, :] - home_y[:, None]).astype(jnp.float32)
            + far_geometry[1][None, :]
            - home_geometry[1][:, None],
            far_geometry[2][None, :] - home_geometry[2][:, None],
        ],
        axis=1,
    )
    distance = jnp.sum(bond_vector * bond_vector, axis=1)
    weight = jnp.maximum(1.0 - distance / horizon_square, 0.0) * intact_mask
    return (bond_vector, weight, home_geometry, far_geometry)


def volume_terms(tile_set, home_field, far_field):
    bond_vector, weight, home_geometry, far_geometry = tile_set
    home_count = bond_vector.shape[0]
    far_count = bond_vector.shape[2]
    weighted = weight[:, None, :] * bond_vector
    far_flat = far_field.reshape(3 * far_count, home_field.shape[2])
    volume_change = jnp.dot(
        weighted.reshape(home_count, 3 * far_count), far_flat, precision=highest
    )
    return volume_change - jnp.einsum(
        "nc,cnk->nk", jnp.sum(weighted, axis=2), home_field, precision=highest
    )


def bond_terms(tile_set, home_field, far_field):
    bond_vector, weight, home_geometry, far_geometry = tile_set
    home_count = bond_vector.shape[0]
    far_count = bond_vector.shape[2]
    column_count = home_field.shape[2]
    far_flat = far_field.reshape(3 * far_count, column_count)
    coupling = weight * (home_geometry[3][:, None] + far_geometry[3][None, :]) * bond_scale
    leading = jnp.transpose(bond_vector, (1, 0, 2))
    tensor = coupling[None, :, None, :] * leading[:, :, None, :] * bond_vector[None, :, :, :]
    bond_force = jnp.einsum("cnd,dnk->cnk", jnp.sum(tensor, axis=3), home_field, precision=highest)
    return bond_force - jnp.dot(
        tensor.reshape(3 * home_count, 3 * far_count), far_flat, precision=highest
    ).reshape(3, home_count, column_count)


def dilatation_terms(tile_set, home_value, far_value):
    bond_vector, weight, home_geometry, far_geometry = tile_set
    home_count = bond_vector.shape[0]
    weighted = jnp.transpose(weight[:, None, :] * bond_vector, (1, 0, 2))
    remote = jnp.dot(weighted.reshape(3 * home_count, -1), far_value, precision=highest).reshape(
        3, home_count, far_value.shape[1]
    )
    return -(remote + jnp.sum(weighted, axis=2)[:, :, None] * home_value[None, :, :])


def rotation(mass_gram, stiff_gram, mode_count):
    mass_factor = jnp.linalg.cholesky(mass_gram)
    left_solved = lax.linalg.triangular_solve(mass_factor, stiff_gram, left_side=True, lower=True)
    projected = lax.linalg.triangular_solve(mass_factor, left_solved.T, left_side=True, lower=True)
    projected = 0.5 * (projected + projected.T)
    stiff_factor = jnp.linalg.cholesky(projected)
    target = jnp.eye(stiff_gram.shape[0], mode_count, dtype=stiff_gram.dtype)
    forward = lax.linalg.triangular_solve(stiff_factor, target, left_side=True, lower=True)
    inverse = lax.linalg.triangular_solve(
        stiff_factor, forward, left_side=True, lower=True, transpose_a=True
    )
    normal = jnp.linalg.cholesky(jnp.dot(inverse.T, inverse, precision=highest))
    lifted = lax.linalg.triangular_solve(
        mass_factor, inverse, left_side=True, lower=True, transpose_a=True
    )
    return lax.linalg.triangular_solve(
        normal, lifted, left_side=False, lower=True, transpose_a=True
    )


def local(basis, offsets, bond_modulus, bulk_modulus, springs, intact):
    size_x = offsets.shape[1]
    size_y = offsets.shape[2]
    column_count = NCOL
    basis = basis.reshape(3, size_x, size_y, column_count)
    strip_count = intact.shape[0]
    strip_x = size_x // strip_count
    total_rows = float(3 * size_x * size_y * lax.axis_size("slab") * lax.axis_size("band"))
    flat_basis = basis.reshape(-1, column_count)
    strips = [(0, strip_x, 0, size_y)]
    margin = REACH
    geometry = jnp.concatenate([offsets, bond_modulus[None]], axis=0)
    wide_field, wide_geometry = (
        padded(basis, (("slab", 1), ("band", 2)), margin),
        padded(geometry, (("slab", 1), ("band", 2)), margin),
    )
    table_shift = 0
    tile_sets = [
        pair_geometry(wide_geometry, margin, region, intact, table_shift) for region in strips
    ]
    volumes = []
    forces = []
    for region, tile_set in zip(strips, tile_sets):
        home_field = window(wide_field, margin, region)
        far_field = window(wide_field, margin, widened(region))
        volumes.append(volume_terms(tile_set, home_field, far_field))
        forces.append(bond_terms(tile_set, home_field, far_field))
    volume_grid = jnp.concatenate(
        [volume.reshape(strip_x, size_y, column_count) for volume in volumes], axis=0
    )
    dilatation = dilation_scale * bulk_modulus[:, :, None] * volume_grid
    wide_dilatation = padded(dilatation, (("slab", 0), ("band", 1)), REACH)
    images = []
    for region, tile_set, bond_force in zip(strips, tile_sets, forces):
        home_value = window(wide_dilatation[None], REACH, region)[0]
        far_value = window(wide_dilatation[None], REACH, widened(region))[0]
        home_field = window(basis, 0, region)
        stiffness = window(springs[None], 0, region)[0]
        image_strip = (
            bond_force
            + dilatation_terms(tile_set, home_value, far_value)
            + stiffness[None, :, None] * home_field
        )
        images.append(image_strip.reshape(3, strip_x, size_y, column_count))
    image_grid = images[0]
    flat_images = image_grid.reshape(-1, column_count)
    stiff_part = jnp.einsum("rk,rl->kl", flat_basis, flat_images, precision=highest)
    mass_part = jnp.einsum("rk,rl->kl", flat_basis, flat_basis, precision=highest)
    mass_total, stiff_total = lax.psum((mass_part, stiff_part), ("slab", "band"))
    mass_gram = mass_total / total_rows
    stiff_gram = stiff_total / total_rows
    stiff_gram = 0.5 * (stiff_gram + stiff_gram.T)
    rotate = rotation(mass_gram, stiff_gram, MODES)
    new_modes = jnp.einsum("cxyk,km->cxym", basis, rotate, precision=highest)
    new_images = jnp.einsum("cxyk,km->cxym", image_grid, rotate, precision=highest)
    reduced = (
        lax.psum(
            jnp.einsum("cxym,cxyn->mn", new_modes, new_images, precision=highest), ("slab", "band")
        )
        / total_rows
    )
    return (
        new_modes.reshape(3, size_x, size_y * MODES),
        new_images.reshape(3, size_x, size_y * MODES),
        reduced,
    )


def solution(mesh):
    in_specs = (
        P(None, "slab", "band"),
        P(None, "slab", "band"),
        P("slab", "band"),
        P("slab", "band"),
        P("slab", "band"),
        P("slab", "band", None),
    )
    out_specs = (P(None, "slab", "band"), P(None, "slab", "band"), P())
    return jax.shard_map(local, mesh=mesh, in_specs=in_specs, out_specs=out_specs, check_vma=False)
```

profile of v0, /device:TPU:1, one launch (start us, length us, event | category | flops | bytes accessed | tf_op | source)
XLA Modules:
  0.0 619.2 jit_solution(15690530505633483698)
XLA Ops:
  9.4 4.6 collective-permute-start
  16.1 3.4 collective-permute-start.4
  27.8 7.3 %collective-permute-start.3 = (f32[4,22,3]{2,1,0:T(8,128)}, f32[4,22,3]{2,1,0:T(8,128)S(1)}, u32[]{:S(2)}, u32[]{:S(2)}) collective-permute-start(f32[4,22,3]{2,1,0:T(8,128)} %get-tuple-element.109), channel_id=1, source_target_pairs={{1,0},{2,1},{3,2},{4,3},{5,4},{6,5},{7,6},{8,7},{9,8},{10,9},{11,1... | collective-permute-start | bytes 3176 | tf_op jit(solution)/shard_map/ppermute | solution.py:27
  48.9 3.0 collective-permute-start.7
  58.1 2.8 pad_maximum_fusion
  63.5 4.4 convolution_subtract_fusion
  71.8 4.9 collective-permute-start.8
  76.7 4.3 fusion.87
  84.6 4.8 collective-permute-start.10
  89.5 4.3 fusion.19
  93.8 5.4 mul.174
  107.9 6.6 %fusion.10 = f32[3,256,192]{1,2,0:T(8,128)S(1)} fusion(f32[3,256,192]{1,2,0:T(8,128)S(1)} %fusion.16, f32[3,256,1452]{1,2,0:T(8,128)} %mul.174, f32[1452,192]{1,0:T(8,128)S(1)} %copy-done, f32[256,3,192]{0,2,1:T(8,128)S(1)} %copy-done.5, f32[3,256,192]{1,2,0:T(8,128)S(1)} %copy-done.6, f32[256]{0:T(256)S(1)} %copy-done.23), kind=kOutput, calls=%fused_computation.12 | convolution fusion | flops 2569863168 | bytes 7936000 | tf_op jit(solution)/shard_map/dot_general | solution.py:121
  117.0 275.1 %all-reduce.10.cloned.1.call-done = (f32[192,192]{1,0:T(8,128)}, f32[192,192]{1,0:T(8,128)}) async-done(((f32[192,192]{1,0:T(8,128)}, f32[192,192]{1,0:T(8,128)}), (f32[192,192]{1,0:T(8,128)}, f32[192,192]{1,0:T(8,128)})) %all-reduce.10.cloned.1.call-update) | async-done | bytes 294928 | tf_op jit(solution)/shard_map/psum | solution.py:204
  394.3 11.7 %cholesky.171 = f32[128,128]{1,0:T(8,128)S(1)} custom-call(f32[128,128]{1,0:T(8,128)S(1)} %copy.93), custom_call_target="Cholesky" | custom-call | tf_op jit(solution)/shard_map/jit(cholesky)/cholesky | solution.py:137
  406.1 10.2 %custom-call.28 = f32[1,128,128]{1,2,0:T(8,128)S(1)} custom-call(f32[1,128,128]{2,1,0:T(8,128)S(1)} %get-tuple-element.103), custom_call_target="InvertDiagBlocksLowerTriangular" | custom-call | tf_op jit(solution)/shard_map/jit(cholesky)/cholesky | solution.py:137
  416.8 5.9 cholesky.191
  425.6 19.7 %custom-call.33 = f32[2,128,128]{1,2,0:T(8,128)S(1)} custom-call(f32[2,128,128]{2,1,0:T(8,128)S(1)} %pad_maximum_fusion.4), custom_call_target="InvertDiagBlocksLowerTriangular" | custom-call | tf_op jit(solution)/shard_map/triangular_solve/custom-call.6 | solution.py:148
  447.5 11.7 %cholesky.209 = f32[128,128]{1,0:T(8,128)S(1)} custom-call(f32[128,128]{1,0:T(8,128)S(1)} %cholesky.246), custom_call_target="Cholesky" | custom-call | tf_op jit(solution)/shard_map/jit(cholesky)/cholesky | solution.py:141
  459.2 9.8 %custom-call.31 = f32[1,128,128]{1,2,0:T(8,128)S(1)} custom-call(f32[1,128,128]{2,1,0:T(8,128)S(1)} %get-tuple-element.101), custom_call_target="InvertDiagBlocksLowerTriangular" | custom-call | tf_op jit(solution)/shard_map/jit(cholesky)/cholesky | solution.py:141
  469.4 5.8 cholesky.229
  478.1 19.8 %custom-call.32 = f32[2,128,128]{1,2,0:T(8,128)S(1)} custom-call(f32[2,128,128]{2,1,0:T(8,128)S(1)} %pad_maximum_fusion.5), custom_call_target="InvertDiagBlocksLowerTriangular" | custom-call | tf_op jit(solution)/shard_map/triangular_solve/custom-call.6 | solution.py:144
  500.1 5.8 cholesky.98
  507.3 4.9 custom-call.24
  516.5 95.0 %psum.23 = f32[64,64]{1,0:T(8,128)S(1)} all-reduce(f32[64,64]{1,0:T(8,128)S(1)} %convolution_bitcast_fusion.3), channel_id=1, replica_groups=mesh['slab'=32,'band'=16] {'slab','band'}, use_global_device_ids=true, to_apply=%region_12.16 | all-reduce | flops 4096 | bytes 32768 | tf_op jit(solution)/shard_map/psum | solution.py:212
  (233 shorter events, 69.8 us)
Async XLA Ops:
  7.2 13.6 %copy-start.8 = (f32[3,16,16]{2,1,0:T(8,128)S(1)}, f32[3,16,16]{2,1,0:T(8,128)}, u32[]{:S(2)}) copy-start(f32[3,16,16]{2,1,0:T(8,128)} %param.12) | copy-start | bytes 9220
  7.2 14.2 %copy-start.3 = (f32[3,16,3072]{2,1,0:T(8,128)S(1)}, f32[3,16,3072]{2,1,0:T(8,128)}, u32[]{:S(2)}) copy-start(f32[3,16,3072]{2,1,0:T(8,128)} %param.11) | copy-start | bytes 1769476
  7.2 384.9 %all-reduce.10.cloned.1.call-start = ((), (), s32[]{:S(2)}) async-start(), calls=%async_computation | async-start | bytes 786432 | tf_op jit(solution)/shard_map/psum | solution.py:204
  8.1 19.1 %collective-permute-start.1 = (f32[4,3,16]{2,1,0:T(4,128)S(1)}, f32[4,3,16]{2,1,0:T(4,128)S(1)}, u32[]{:S(2)}, u32[]{:S(2)}) collective-permute-start(f32[4,3,16]{2,1,0:T(4,128)S(1)} %get-tuple-element.115), channel_id=1, source_target_pairs={{16,0},{32,16},{48,32},{64,48},{80,64},{96,80},{112,96},{128,112},... | collective-permute-start | bytes 2312 | tf_op jit(solution)/shard_map/ppermute | solution.py:27
  9.3 13.5 %copy-start.37 = (s32[1,2,9]{2,1,0:T(2,128)S(1)}, s32[1,2,9]{2,1,0:T(2,128)}, u32[]{:S(2)}) copy-start(s32[1,2,9]{2,1,0:T(2,128)} %param.16) | copy-start | bytes 220
  9.3 14.5 %copy-start.22 = (f32[16,16]{1,0:T(8,128)S(1)}, f32[16,16]{1,0:T(8,128)}, u32[]{:S(2)}) copy-start(f32[16,16]{1,0:T(8,128)} %param.14) | copy-start | bytes 3076
  9.4 17.8 %collective-permute-start = (f32[4,3,16]{2,1,0:T(4,128)S(1)}, f32[4,3,16]{2,1,0:T(4,128)S(1)}, u32[]{:S(2)}, u32[]{:S(2)}) collective-permute-start(f32[4,3,16]{2,1,0:T(4,128)S(1)} %get-tuple-element.114), channel_id=1, source_target_pairs={{0,16},{16,32},{32,48},{48,64},{64,80},{80,96},{96,112},{112,128},... | collective-permute-start | bytes 2312 | tf_op jit(solution)/shard_map/ppermute | solution.py:26
  15.4 32.4 %copy-start.1 = (f32[3,16,16,192]{3,2,1,0:T(8,128)}, f32[3,16,16,192]{3,2,1,0:T(8,128)S(1)}, u32[]{:S(2)}) copy-start(f32[3,16,16,192]{3,2,1,0:T(8,128)S(1)} %reshape.1000) | copy-start | bytes 1769476
  16.1 31.6 %collective-permute-start.4 = (f32[3,3,16,192]{3,2,1,0:T(8,128)}, f32[3,3,16,192]{3,2,1,0:T(8,128)S(1)}, u32[]{:S(2)}, u32[]{:S(2)}) collective-permute-start(f32[3,3,16,192]{3,2,1,0:T(8,128)} %get-tuple-element.93), channel_id=1, source_target_pairs={{0,16},{16,32},{32,48},{48,64},{64,80},{80,96},{96,112},{112,128},... | collective-permute-start | bytes 331784 | tf_op jit(solution)/shard_map/ppermute | solution.py:26
  19.5 28.3 %collective-permute-start.5 = (f32[3,3,16,192]{3,2,1,0:T(8,128)S(1)}, f32[3,3,16,192]{3,2,1,0:T(8,128)S(1)}, u32[]{:S(2)}, u32[]{:S(2)}) collective-permute-start(f32[3,3,16,192]{3,2,1,0:T(8,128)S(1)} %get-tuple-element.92), channel_id=1, source_target_pairs={{16,0},{32,16},{48,32},{64,48},{80,64},{96,80},{112,96},{128,112},... | collective-permute-start | bytes 331784 | tf_op jit(solution)/shard_map/ppermute | solution.py:27
  27.8 15.1 %collective-permute-start.3 = (f32[4,22,3]{2,1,0:T(8,128)}, f32[4,22,3]{2,1,0:T(8,128)S(1)}, u32[]{:S(2)}, u32[]{:S(2)}) collective-permute-start(f32[4,22,3]{2,1,0:T(8,128)} %get-tuple-element.109), channel_id=1, source_target_pairs={{1,0},{2,1},{3,2},{4,3},{5,4},{6,5},{7,6},{8,7},{9,8},{10,9},{11,1... | collective-permute-start | bytes 3176 | tf_op jit(solution)/shard_map/ppermute | solution.py:27
  35.1 7.7 %collective-permute-start.2 = (f32[4,22,3]{2,1,0:T(8,128)S(1)}, f32[4,22,3]{2,1,0:T(8,128)}, u32[]{:S(2)}, u32[]{:S(2)}) collective-permute-start(f32[4,22,3]{2,1,0:T(8,128)S(1)} %get-tuple-element.108), channel_id=1, source_target_pairs={{0,1},{1,2},{2,3},{3,4},{4,5},{5,6},{6,7},{7,8},{8,9},{9,10},{10,1... | collective-permute-start | bytes 3176 | tf_op jit(solution)/shard_map/ppermute | solution.py:26
  38.1 6.3 %copy-start.12 = (s32[484]{0:T(512)S(1)}, s32[484]{0:T(512)}, u32[]{:S(2)}) copy-start(s32[484]{0:T(512)} %copy-done.11) | copy-start | bytes 5812
  38.1 6.3 %copy-start.14 = (s32[484]{0:T(512)S(1)}, s32[484]{0:T(512)}, u32[]{:S(2)}) copy-start(s32[484]{0:T(512)} %copy-done.13) | copy-start | bytes 5812
  38.1 6.3 %copy-start.17 = (s32[256]{0:T(256)S(1)}, s32[256]{0:T(256)}, u32[]{:S(2)}) copy-start(s32[256]{0:T(256)} %copy-done.16) | copy-start | bytes 3076
  47.9 6.6 %copy-start.4 = (f32[3,22,16,192]{3,2,1,0:T(8,128)}, f32[3,22,16,192]{3,2,1,0:T(8,128)S(1)}, u32[]{:S(2)}) copy-start(f32[3,22,16,192]{3,2,1,0:T(8,128)S(1)} %constant_dynamic-update-slice_fusion) | copy-start | bytes 2433028
  48.9 8.1 %collective-permute-start.7 = (f32[3,22,3,192]{3,2,1,0:T(4,128)}, f32[3,22,3,192]{3,2,1,0:T(4,128)}, u32[]{:S(2)}, u32[]{:S(2)}) collective-permute-start(f32[3,22,3,192]{3,2,1,0:T(4,128)} %get-tuple-element.91), channel_id=1, source_target_pairs={{1,0},{2,1},{3,2},{4,3},{5,4},{6,5},{7,6},{8,7},{9,8},{10,9},{11,1... | collective-permute-start | bytes 456200 | tf_op jit(solution)/shard_map/ppermute | solution.py:27
  51.9 6.3 %collective-permute-start.6 = (f32[3,22,3,192]{3,2,1,0:T(4,128)}, f32[3,22,3,192]{3,2,1,0:T(4,128)}, u32[]{:S(2)}, u32[]{:S(2)}) collective-permute-start(f32[3,22,3,192]{3,2,1,0:T(4,128)} %get-tuple-element.90), channel_id=1, source_target_pairs={{0,1},{1,2},{2,3},{3,4},{4,5},{5,6},{6,7},{7,8},{8,9},{9,10},{10,1... | collective-permute-start | bytes 456200 | tf_op jit(solution)/shard_map/ppermute | solution.py:26
  70.5 11.5 %collective-permute-start.9 = (f32[3,16,192]{2,1,0:T(8,128)}, f32[3,16,192]{2,1,0:T(8,128)S(1)}, u32[]{:S(2)}, u32[]{:S(2)}) collective-permute-start(f32[3,16,192]{2,1,0:T(8,128)} %get-tuple-element.99), channel_id=1, source_target_pairs={{16,0},{32,16},{48,32},{64,48},{80,64},{96,80},{112,96},{128,112},... | collective-permute-start | bytes 110600 | tf_op jit(solution)/shard_map/ppermute | solution.py:27
  71.8 10.2 %collective-permute-start.8 = (f32[3,16,192]{2,1,0:T(8,128)S(1)}, f32[3,16,192]{2,1,0:T(8,128)S(1)}, u32[]{:S(2)}, u32[]{:S(2)}) collective-permute-start(f32[3,16,192]{2,1,0:T(8,128)S(1)} %get-tuple-element.98), channel_id=1, source_target_pairs={{0,16},{16,32},{32,48},{48,64},{64,80},{80,96},{96,112},{112,128},... | collective-permute-start | bytes 110600 | tf_op jit(solution)/shard_map/ppermute | solution.py:26
  82.7 18.8 %collective-permute-start.11 = (f32[22,3,192]{2,1,0:T(4,128)}, f32[22,3,192]{2,1,0:T(4,128)S(1)}, u32[]{:S(2)}, u32[]{:S(2)}) collective-permute-start(f32[22,3,192]{2,1,0:T(4,128)} %get-tuple-element.97), channel_id=1, source_target_pairs={{1,0},{2,1},{3,2},{4,3},{5,4},{6,5},{7,6},{8,7},{9,8},{10,9},{11,1... | collective-permute-start | bytes 152072 | tf_op jit(solution)/shard_map/ppermute | solution.py:27
  84.6 16.9 %collective-permute-start.10 = (f32[22,3,192]{2,1,0:T(4,128)}, f32[22,3,192]{2,1,0:T(4,128)}, u32[]{:S(2)}, u32[]{:S(2)}) collective-permute-start(f32[22,3,192]{2,1,0:T(4,128)} %get-tuple-element.96), channel_id=1, source_target_pairs={{0,1},{1,2},{2,3},{3,4},{4,5},{5,6},{6,7},{7,8},{8,9},{9,10},{10,1... | collective-permute-start | bytes 152072 | tf_op jit(solution)/shard_map/ppermute | solution.py:26
  392.1 33.2 %copy-start.7 = (f32[192,192]{1,0:T(8,128)S(1)}, f32[192,192]{1,0:T(8,128)}, u32[]{:S(2)}) copy-start(f32[192,192]{1,0:T(8,128)} %get-tuple-element.78) | copy-start | bytes 442372
  459.2 53.3 %copy-start.2 = (f32[3,16,16,192]{3,2,1,0:T(8,128)S(1)}, f32[3,16,16,192]{3,2,1,0:T(8,128)}, u32[]{:S(2)}) copy-start(f32[3,16,16,192]{3,2,1,0:T(8,128)} %copy-done.1) | copy-start | bytes 1769476
  (27 other events, 64.1 us)
Sparse Core Ops, SparseCore 0:
  116.8 275.2 all-reduce.9
where the time goes:
time: 628 us; the launch traced here: 619 us
  waiting for transfers between devices  276 us (44%)
  other arithmetic  131 us (21%)
  blocking collectives  95 us (15%)
  starting transfers between devices  38.3 us (6%)
  local copies, waits for them, and re-layouts  31.2 us (5%)
  matrix products  29.5 us (5%)
  between operations  18 us (3%)
    psum x1, waiting for transfers between devices, local(): lax.psum((mass_part, stiff_part), ('slab', 'band'))  275 us
    psum x1, blocking collectives, local(): lax.psum(jnp.einsum('cxym,cxyn->mn', new_modes, new_images, precision=hig...  95 us
    another operation x7, other arithmetic, rotation(): mass_factor = jnp.linalg.cholesky(mass_gram)  29.1 us
    another operation x7, other arithmetic, rotation(): stiff_factor = jnp.linalg.cholesky(projected)  28.7 us
    ppermute x6, starting transfers between devices, padded(): before = lax.ppermute(last, axis, up)  22.2 us
    another operation x4, other arithmetic, rotation(): lax.linalg.triangular_solve(stiff_factor, forward, left_side=True, lower=...  20 us
    another operation x6, other arithmetic, rotation(): lax.linalg.triangular_solve(mass_factor, inverse, left_side=True, lower=T...  19.8 us
    ppermute x6, starting transfers between devices, padded(): after = lax.ppermute(first, axis, down)  16.1 us
  transfers between devices with their start and end apart: 13, of which 2 were waited for; matrix products, arithmetic and copies ran while one was open for 6% of the time, Pallas kernels for 0%

commit v1 on v0

v1 whole, which is shorter than its diff:
```python
import jax
import jax.numpy as jnp
from jax import lax
from jax.experimental import pallas as pl
from jax.experimental.pallas import tpu as pltpu
from jax.sharding import PartitionSpec as P


MODES = 64
NCOL = 192
SIDE = 16
HALO = 6
GROUP = 32
STRIPS = 12
FAR = 256
highest = lax.Precision.HIGHEST
f32 = jnp.float32
bf16 = jnp.bfloat16

VMEM = pl.BlockSpec(memory_space=pltpu.VMEM)
PARAMS = pltpu.CompilerParams(vmem_limit_bytes=56 * 1024 * 1024)


def call(kernel, outs, scratch, args, flops, name):
    size = sum(a.size for a in args) + sum(o[0] * o[1] * (o[2] if len(o) > 2 else 1) for o in outs)
    return pl.pallas_call(
        kernel,
        out_shape=[jax.ShapeDtypeStruct(o, f32) for o in outs],
        in_specs=[VMEM] * len(args),
        out_specs=[VMEM] * len(outs),
        scratch_shapes=scratch,
        compiler_params=PARAMS,
        cost_estimate=pl.CostEstimate(flops=flops, bytes_accessed=4 * size, transcendentals=0),
        name=name,
    )(*args)


def pack_x(basis, geo, up, down):
    for out, first, lane in ((up, SIDE - HALO, 256), (down, 0, 384)):
        for c in range(3):
            for j in range(4):
                row = j * 18 + c * 6
                out[row : row + 6, :] = basis[c, first : first + 6, j * 768 : (j + 1) * 768]
        out[72:80, :] = jnp.zeros((8, 768), f32)
        out[72:80, 0:128] = geo[:, lane : lane + 128]


def pack_y(basis, geo, left, right, up, down, own):
    own[...] = jnp.zeros((8, 512), f32)
    for y in range(SIDE):
        at = GROUP * y
        own[:, at : at + 16] = geo[:, 16 * y : 16 * y + 16]
        own[:, at + 16 : at + 22] = left[72:80, 8 * y : 8 * y + 6]
        own[:, at + 22 : at + 28] = right[72:80, 8 * y : 8 * y + 6]
    for out, first in ((up, SIDE - HALO), (down, 0)):
        pieces = ((2, 384, 768, 0), (3, 0, 768, 384)) if first else ((0, 0, 768, 0), (1, 0, 384, 768))
        for c in range(3):
            row = GROUP * c
            out[row : row + 16, :] = basis[c, :, first * NCOL : (first + HALO) * NCOL]
            for j, start, stop, lane in pieces:
                src = j * 18 + c * 6
                width = stop - start
                out[row + 16 : row + 22, lane : lane + width] = left[src : src + 6, start:stop]
                out[row + 22 : row + 28, lane : lane + width] = right[src : src + 6, start:stop]
            out[row + 28 : row + 32, :] = jnp.zeros((4, 1152), f32)
        lanes = slice(first * GROUP, (first + HALO) * GROUP)
        out[28:32, 0:192] = own[0:4, lanes]
        out[60:64, 0:192] = own[4:8, lanes]


def split(value):
    high = value.astype(bf16)
    return high, (value - high.astype(f32)).astype(bf16)


def product(left, right_high, right_low):
    high, low = split(left)
    return (
        jnp.dot(high, right_high, preferred_element_type=f32)
        + jnp.dot(high, right_low, preferred_element_type=f32)
        + jnp.dot(low, right_high, preferred_element_type=f32)
    )


def block_masks(s, table):
    y0 = 2 * s - 4
    lane = lax.broadcasted_iota(jnp.int32, (32, FAR), 1)
    row = lax.broadcasted_iota(jnp.int32, (32, FAR), 0)
    xi = lane & 31
    far_x = jnp.where(xi < 16, 0, jnp.where(xi < 22, -1, 1))
    far_y = ((y0 - 3 + (lane >> 5)) >> 3) - (y0 >> 3)
    home_x = jnp.where(row < 16, 0, jnp.where(row < 22, -1, 1))
    entry = row - jnp.where(row < 16, 0, jnp.where(row < 22, 16, 22))
    entry = jnp.where(entry < 6, entry, -100)
    code = 3 * (far_x - home_x + 1) + far_y + 1
    value = jnp.where(code == entry, table[:, 7:8], 0.0)
    value = value + jnp.where(code == entry + 6, table[:, 6:7], 0.0)
    middle = jnp.sum(value[0:8], axis=0, keepdims=True)
    rest = value[16:32]
    at = lax.broadcasted_iota(jnp.int32, (16, FAR), 0)
    before = jnp.sum(jnp.where(at < 6, rest, 0.0), axis=0, keepdims=True)
    after = jnp.sum(jnp.where(at >= 6, rest, 0.0), axis=0, keepdims=True)
    return middle, before, after


def bonds(far, home):
    vector = [far[j : j + 1, :] - home[:, j : j + 1] for j in range(3)]
    square = vector[0] * vector[0] + vector[1] * vector[1] + vector[2] * vector[2]
    return vector, jnp.maximum(1.0 - square * (1.0 / 9.0), 0.0)


def stiffness(
    basis, left, right, own, below, above, images, grams,
    geo, geo_cols, geo_far, field, high, low, dil_high, dil_low, result,
):
    geo[...] = jnp.zeros((8, 1024), f32)
    geo[:, 256:768] = own[...]
    for part, lane in ((below, 64), (above, 768)):
        geo[0:4, lane : lane + 192] = part[28:32, 0:192]
        geo[4:8, lane : lane + 192] = part[60:64, 0:192]
    lane = lax.broadcasted_iota(jnp.int32, (8, 1024), 1)
    channel = lax.broadcasted_iota(jnp.int32, (8, 1024), 0)
    xi = lane & 31
    at_x = jnp.where(xi < 16, xi, jnp.where(xi < 22, xi - 22, xi - 6))
    at_y = (lane >> 5) - 8
    place = jnp.where(channel == 0, at_x, jnp.where(channel == 1, at_y, 0)).astype(f32)
    placed = geo[...] + place
    geo[...] = placed
    geo_cols[...] = placed.T
    for s in range(STRIPS):
        start = GROUP * (2 * s + 1)
        geo_far[s] = geo[:, start : start + FAR]

    for c in range(3):
        for y in range(SIDE):
            j, t = divmod(y, 4)
            src = j * 18 + c * 6
            row = GROUP * y
            field[c, row : row + 16, :] = basis[c, :, y * NCOL : (y + 1) * NCOL]
            field[c, row + 16 : row + 22, :] = left[src : src + 6, t * NCOL : (t + 1) * NCOL]
            field[c, row + 22 : row + 28, :] = right[src : src + 6, t * NCOL : (t + 1) * NCOL]
            field[c, row + 28 : row + 32, :] = jnp.zeros((4, NCOL), f32)
        for y in range(SIDE):
            row = GROUP * y
            parts = split(field[c, row : row + 32, :])
            high[c, 256 + row : 288 + row, :] = parts[0]
            low[c, 256 + row : 288 + row, :] = parts[1]
        for j in range(HALO):
            for part, first in ((below, 2), (above, 24)):
                row = GROUP * (first + j)
                parts = split(part[GROUP * c : GROUP * (c + 1), j * NCOL : (j + 1) * NCOL])
                high[c, row : row + 32, :] = parts[0]
                low[c, row : row + 32, :] = parts[1]
        for row in (0, 960):
            for ref in (high, low):
                ref[c, row : row + 64, :] = jnp.zeros((64, NCOL), bf16)

    row = lax.broadcasted_iota(jnp.int32, (64, FAR), 0)
    lane = lax.broadcasted_iota(jnp.int32, (64, FAR), 1)
    at_self = lane == row + 96
    home_row = row & 31

    def dilatations(s, carry):
        near = pl.multiple_of(GROUP * (2 * s + 4), 64)
        start = pl.multiple_of(GROUP * (2 * s + 1), 32)
        home = geo_cols[pl.ds(near, 64), :]
        middle, before, after = block_masks(s, home[0:32])
        vector, weight = bonds(geo_far[s], home)
        weight = weight * jnp.where(home_row < 16, middle, jnp.where(home_row < 22, before, after))
        total = jnp.zeros((64, NCOL), f32)
        for j in range(3):
            matrix = weight * vector[j]
            matrix = jnp.where(at_self, -jnp.sum(matrix, axis=1, keepdims=True), matrix)
            total = total + product(
                matrix, high[j, pl.ds(start, FAR), :], low[j, pl.ds(start, FAR), :]
            )
        parts = split(total * (home[:, 4:5] * (1.0 / 27.0)))
        dil_high[pl.ds(near, 64), :] = parts[0]
        dil_low[pl.ds(near, 64), :] = parts[1]
        return carry

    lax.fori_loop(0, STRIPS, dilatations, 0)

    row = lax.broadcasted_iota(jnp.int32, (32, FAR), 0)
    lane = lax.broadcasted_iota(jnp.int32, (32, FAR), 1)
    own_self = lane == row + jnp.where(row < 16, 96, 112)

    def forces(s, carry):
        near = pl.multiple_of(GROUP * (2 * s + 4), 64)
        start = pl.multiple_of(GROUP * (2 * s + 1), 32)
        first = geo_cols[pl.ds(near, 32), :]
        second = geo_cols[pl.ds(near + 32, 16), :]
        home = jnp.concatenate([first[0:16], second], axis=0)
        middle, _, _ = block_masks(s, first)
        far = geo_far[s]
        vector, weight = bonds(far, home)
        weight = weight * middle
        coupling = weight * ((home[:, 3:4] + far[3:4, :]) * (1.0 / 18.0))
        spring = home[:, 5:6]
        pairs = {}
        for i in range(3):
            side = coupling * vector[i]
            for j in range(i, 3):
                matrix = side * vector[j]
                total = jnp.sum(matrix, axis=1, keepdims=True)
                if i == j:
                    total = total + spring
                pairs[i, j] = pairs[j, i] = jnp.where(own_self, total, -matrix)
        image = jnp.zeros((96, NCOL), f32)
        for j in range(3):
            stacked = jnp.concatenate([pairs[i, j] for i in range(3)], axis=0)
            image = image + product(
                stacked, high[j, pl.ds(start, FAR), :], low[j, pl.ds(start, FAR), :]
            )
        sides = []
        for i in range(3):
            matrix = weight * vector[i]
            total = jnp.sum(matrix, axis=1, keepdims=True)
            sides.append(-jnp.where(own_self, total, matrix))
        image = image + product(
            jnp.concatenate(sides, axis=0),
            dil_high[pl.ds(start, FAR), :],
            dil_low[pl.ds(start, FAR), :],
        )
        at = pl.multiple_of(32 * (s - 2), 32)
        for i in range(3):
            result[i, pl.ds(at, 32), :] = image[32 * i : 32 * i + 32]
        return carry

    lax.fori_loop(2, 10, forces, 0)

    for c in range(3):
        for y in range(SIDE):
            images[c, :, y * NCOL : (y + 1) * NCOL] = result[c, 16 * y : 16 * y + 16, :]

    rows = field[...].reshape(3, SIDE, GROUP, NCOL)[:, :, 0:16, :].reshape(768, NCOL)
    image = result[...].reshape(768, NCOL)

    def gram(a, b):
        return lax.dot_general(
            a, b, (((0,), (0,)), ((), ())), precision=highest, preferred_element_type=f32
        )

    mass = gram(rows, rows)
    stiff = gram(rows, image)
    mirror = gram(image, rows)
    at_row = lax.broadcasted_iota(jnp.int32, (NCOL, NCOL), 0)
    at_col = lax.broadcasted_iota(jnp.int32, (NCOL, NCOL), 1)
    grams[0:192, :] = jnp.where(at_row >= at_col, mass, 0.5 * (stiff + mirror))
    diagonal = jnp.sum(jnp.where(at_row == at_col, stiff, 0.0), axis=0, keepdims=True)
    grams[192:200, :] = jnp.broadcast_to(diagonal, (8, NCOL))
    grams[200:256, :] = jnp.zeros((56, NCOL), f32)


def eliminate(ref, step, capture):
    base = 8 * step
    panel = ref[base : base + 8, :]
    columns = [ref[:, base + i : base + i + 1] for i in range(8)]
    at = lax.broadcasted_iota(jnp.int32, panel.shape, 0)
    caught = panel
    for i in range(8):
        pivot = panel[i : i + 1, base + i : base + i + 1]
        row = panel[i : i + 1, :]
        scaled = row * (1.0 / pivot)
        if capture:
            root = lax.rsqrt(pivot)
            root = root * (1.5 - 0.5 * pivot * root * root)
            caught = jnp.where(at == i, row * root, caught)
        panel = jnp.where(at == i, scaled, panel - panel[:, base + i : base + i + 1] * scaled)
    rest = ref[...]
    for i in range(8):
        rest = rest - columns[i] * panel[i : i + 1, :]
    ref[...] = rest
    ref[base : base + 8, :] = panel
    return caught


def rotation(scale, grams, basis, images, modes, mode_images, reduced, square, work, small, factor):
    packed = grams[0:192, :] * scale
    diagonal = grams[192:193, :] * scale
    square[...] = jnp.zeros((256, 256), f32)
    square[0:192, 0:192] = packed
    flipped = square[...].T[0:192, 0:192]
    at_row = lax.broadcasted_iota(jnp.int32, (NCOL, NCOL), 0)
    at_col = lax.broadcasted_iota(jnp.int32, (NCOL, NCOL), 1)
    mass = jnp.where(at_row >= at_col, packed, flipped)
    stiff = jnp.where(at_row < at_col, packed, jnp.where(at_row > at_col, flipped, diagonal))
    work[:, 0:192] = stiff
    work[:, 192:256] = mass[:, 0:64]
    for step in range(24):
        eliminate(work, step, False)
    solved = work[:, 192:256]
    weighted = jnp.dot(mass, solved, precision=highest, preferred_element_type=f32)
    square[0:192, 0:64] = solved
    turned = square[...].T[0:64, 0:192]
    small[:, 0:64] = jnp.dot(turned, weighted, precision=highest, preferred_element_type=f32)
    small[:, 64:256] = turned
    factor[...] = jnp.zeros((128, 384), f32)
    for step in range(8):
        caught = eliminate(small, step, True)[:, 64:256]
        factor[8 * step : 8 * step + 8, 0:192] = caught
        factor[64 + 8 * step : 72 + 8 * step, 192:384] = caught
    rotate = factor[0:64, 0:192]
    across = (((1,), (1,)), ((), ()))
    lifted = lax.dot_general(stiff, rotate, across, precision=highest, preferred_element_type=f32)
    reduced[...] = jnp.dot(rotate, lifted, precision=highest, preferred_element_type=f32)
    both = factor[...]
    for source, out in ((basis, modes), (images, mode_images)):
        for y in range(SIDE // 2):
            value = source[:, :, y * 384 : (y + 1) * 384].reshape(48, 384)
            value = lax.dot_general(value, both, across, precision=highest, preferred_element_type=f32)
            out[:, :, y * 128 : (y + 1) * 128] = value.reshape(3, SIDE, 128)


def exchange(up, down, axis):
    size = lax.axis_size(axis)
    forward = [(i, i + 1) for i in range(size - 1)]
    backward = [(i + 1, i) for i in range(size - 1)]
    return lax.ppermute(up, axis, forward), lax.ppermute(down, axis, backward)


def spread(value, axis):
    size = lax.axis_size(axis)
    return lax.all_to_all(jnp.broadcast_to(value[None], (size,) + value.shape), axis, 0, 0, tiled=True)


def local(basis, offsets, bond_modulus, bulk_modulus, springs, intact):
    slabs = lax.axis_size("slab")
    bands = lax.axis_size("band")
    total_rows = float(3 * SIDE * SIDE * slabs * bands)

    with jax.named_scope("geometry"):
        table = intact[0].astype(f32)
        table = jnp.stack([jnp.pad(table[:, 6:9], ((0, 0), (0, 3))), table[:, 0:6]])
        table = jnp.repeat(table, SIDE // 2, axis=1)
        points = jnp.concatenate(
            [offsets, bond_modulus[None], bulk_modulus[None], springs[None]], axis=0
        ).transpose(0, 2, 1)

        def lanes(part, width):
            pads = width - part.shape[2]
            part = jnp.concatenate(
                [
                    jnp.pad(part, ((0, 0), (0, 0), (0, pads))),
                    jnp.pad(table, ((0, 0), (0, 0), (0, width - 6))),
                ],
                axis=0,
            )
            return part.reshape(8, SIDE * width)

        geo = jnp.concatenate(
            [lanes(points, 16), lanes(points[:, :, SIDE - HALO :], 8), lanes(points[:, :, :HALO], 8)],
            axis=1,
        )

    with jax.named_scope("halo"):
        up, down = call(pack_x, [(80, 768)] * 2, [], (basis, geo), 1000, "pack_x")
        left, right = exchange(up, down, "slab")
        up, down, own = call(
            pack_y, [(96, 1152)] * 2 + [(8, 512)], [], (basis, geo, left, right), 1000, "pack_y"
        )
        below, above = exchange(up, down, "band")

    with jax.named_scope("stiffness"):
        images, grams = call(
            stiffness,
            [(3, SIDE, SIDE * NCOL), (256, NCOL)],
            [
                pltpu.VMEM((8, 1024), f32),
                pltpu.VMEM((1024, 8), f32),
                pltpu.VMEM((STRIPS, 8, FAR), f32),
                pltpu.VMEM((3, 512, NCOL), f32),
                pltpu.VMEM((3, 1024, NCOL), bf16),
                pltpu.VMEM((3, 1024, NCOL), bf16),
                pltpu.VMEM((1024, NCOL), bf16),
                pltpu.VMEM((1024, NCOL), bf16),
                pltpu.VMEM((3, 256, NCOL), f32),
            ],
            (basis, left, right, own, below, above),
            2 * 10**9,
            "stiffness",
        )

    with jax.named_scope("sums"):
        part = lax.all_to_all(grams.reshape(slabs, 256 // slabs, NCOL), "slab", 0, 0, tiled=True)
        part = spread(jnp.sum(part, axis=0), "band")
        part = spread(jnp.sum(part, axis=0), "slab")
        grams = part.reshape(256, NCOL)

    with jax.named_scope("rotation"):
        def kernel(*refs):
            rotation(1.0 / total_rows, *refs)

        modes, mode_images, reduced = call(
            kernel,
            [(3, SIDE, SIDE * MODES)] * 2 + [(MODES, MODES)],
            [
                pltpu.VMEM((256, 256), f32),
                pltpu.VMEM((192, 256), f32),
                pltpu.VMEM((64, 256), f32),
                pltpu.VMEM((128, 384), f32),
            ],
            (grams, basis, images),
            10**9,
            "rotation",
        )
    return modes, mode_images, reduced


def solution(mesh):
    in_specs = (
        P(None, "slab", "band"),
        P(None, "slab", "band"),
        P("slab", "band"),
        P("slab", "band"),
        P("slab", "band"),
        P("slab", "band", None),
    )
    out_specs = (P(None, "slab", "band"), P(None, "slab", "band"), P())
    return jax.shard_map(local, mesh=mesh, in_specs=in_specs, out_specs=out_specs, check_vma=False)
```

time: 628 us -> 152 us (0.24); the launches traced: 619 us -> 152 us
  waiting for transfers between devices: 276 us -> 13.8 us
  other arithmetic: 131 us -> 0.85 us
  Pallas kernels: 0 us -> 57.3 us
  blocking collectives: 95 us -> 60.6 us
  matrix products: 29.5 us -> 0 us
  local copies, waits for them, and re-layouts: 31.2 us -> 4.31 us
  starting transfers between devices: 38.3 us -> 14.4 us
  between operations: 18 us -> 0.77 us
    psum x1 -> x0, waiting for transfers between devices: 275 us -> none  [local(): lax.psum((mass_part, stiff_part), ('slab', 'band'))]
    another operation x31 -> x1, other arithmetic: 110 us -> 0.01 us  [local(): table = jnp.stack([jnp.pad(table[:, 6:9], ((0, 0), (0, 3))), table[:, 0:6]])]
    psum x1 -> x0, blocking collectives: 95 us -> none  [local(): lax.psum(jnp.einsum('cxym,cxyn->mn', new_modes, new_images, precision=hig...]
    all_to_all x0 -> x3, blocking collectives: none -> 60.6 us  [the longest x2 38.5 us: spread(): lax.all_to_all(jnp.broadcast_to(value[None], (size,) + value.shape), axis...]
    pallas_call x0 -> x4, Pallas kernels: none -> 57.3 us  [call(): pl.pallas_call(kernel, out_shape=[jax.ShapeDtypeStruct(o, f32) for o in o...]
    dot_general x11 -> x0, matrix products: 24.9 us -> none  [the longest x1 6.6 us: bond_terms(): jnp.dot(tensor.reshape(3 * home_count, 3 * far_count), far_flat, precisio...]
    ppermute x12 -> x4, starting transfers between devices: 38.2 us -> 14.4 us  [exchange(): return (lax.ppermute(up, axis, forward), lax.ppermute(down, axis, backward))]
    ppermute x12 -> x4, waiting for transfers between devices: 1.25 us -> 13.8 us  [exchange(): return (lax.ppermute(up, axis, forward), lax.ppermute(down, axis, backward))]
  transfers between devices with their start and end apart: 13 -> 4, of which waited for: 2 -> 4; matrix products, arithmetic and copies ran while one was open for 6% -> 0% of each run, Pallas kernels for 0% -> 0%
where the time goes in v1:
time: 152 us
  blocking collectives  60.6 us (40%)
  Pallas kernels  57.3 us (38%)
  starting transfers between devices  14.4 us (9%)
  waiting for transfers between devices  13.8 us (9%)
  local copies, waits for them, and re-layouts  4.31 us (3%)
    pallas_call x4, Pallas kernels, call(): pl.pallas_call(kernel, out_shape=[jax.ShapeDtypeStruct(o, f32) for o in o...  57.3 us
    all_to_all x2, blocking collectives, spread(): lax.all_to_all(jnp.broadcast_to(value[None], (size,) + value.shape), axis...  38.5 us
    all_to_all x1, blocking collectives, local(): lax.all_to_all(grams.reshape(slabs, 256 // slabs, NCOL), 'slab', 0, 0, ti...  22.1 us
    ppermute x4, starting transfers between devices, exchange(): return (lax.ppermute(up, axis, forward), lax.ppermute(down, axis, backward))  14.4 us
    ppermute x4, waiting for transfers between devices, exchange(): return (lax.ppermute(up, axis, forward), lax.ppermute(down, axis, backward))  13.8 us
    unnamed x23, local copies, waits for them, and re-layouts  3.42 us
  transfers between devices with their start and end apart: 4, of which 4 were waited for; matrix products, arithmetic and copies ran while one was open for 0% of the time, Pallas kernels for 0%

profile of v1, /device:TPU:1, one launch (start us, length us, event | category | flops | bytes accessed | tf_op | source)
XLA Modules:
  0.0 151.9 jit_solution(12862193557464746175)
XLA Ops:
  0.6 0.7 convert_bitcast_fusion
  1.4 0.1 copy.20
  1.7 0.6 copy-done.3
  2.4 0.6 copy-done.7
  3.4 0.1 reshape.30
  3.6 0.1 reshape.29
  3.7 0.6 copy-done.2
  4.3 1.9 %pack_x.1 = (f32[80,768]{1,0:T(8,128)}, f32[80,768]{1,0:T(8,128)}) custom-call(f32[3,16,3072]{2,1,0:T(8,128)} %refs_1_.1, f32[8,512]{1,0:T(8,128)} %copy-done.2), custom_call_target="tpu_custom_call" | custom-call | flops 1000 | bytes 1097728 | tf_op jit(solution)/shard_map/halo/pack_x/pallas_call | solution.py:26
  6.2 3.9 %collective-permute-start = (f32[80,768]{1,0:T(8,128)}, f32[80,768]{1,0:T(8,128)S(1)}, u32[]{:S(2)}, u32[]{:S(2)}) collective-permute-start(f32[80,768]{1,0:T(8,128)} %get-tuple-element.10), channel_id=1, source_target_pairs={{0,16},{16,32},{32,48},{48,64},{64,80},{80,96},{96,112},{112,128},... | collective-permute-start | bytes 737288 | tf_op jit(solution)/shard_map/halo/ppermute | solution.py:319
  10.2 1.3 collective-permute-start.1
  11.5 2.1 %collective-permute-done.left = f32[80,768]{1,0:T(8,128)S(1)} collective-permute-done((f32[80,768]{1,0:T(8,128)}, f32[80,768]{1,0:T(8,128)S(1)}, u32[]{:S(2)}, u32[]{:S(2)}) %collective-permute-start) | collective-permute-done | bytes 245792 | tf_op jit(solution)/shard_map/halo/ppermute | solution.py:319
  13.6 3.7 %collective-permute-done.1.right = f32[80,768]{1,0:T(8,128)S(1)} collective-permute-done((f32[80,768]{1,0:T(8,128)}, f32[80,768]{1,0:T(8,128)S(1)}, u32[]{:S(2)}, u32[]{:S(2)}) %collective-permute-start.1) | collective-permute-done | bytes 245792 | tf_op jit(solution)/shard_map/halo/ppermute | solution.py:319
  17.4 0.7 copy-done.1
  18.0 2.3 %pack_y.1 = (f32[96,1152]{1,0:T(8,128)}, f32[96,1152]{1,0:T(8,128)}, f32[8,512]{1,0:T(8,128)}) custom-call(f32[3,16,3072]{2,1,0:T(8,128)} %refs_1_.1, f32[8,512]{1,0:T(8,128)} %copy-done.2, f32[80,768]{1,0:T(8,128)} %copy-done, f32[80,768]{1,0:T(8,128)} %copy-done.1), custom_call_target="tpu_custom_call" | custom-call | flops 1000 | bytes 1998848 | tf_op jit(solution)/shard_map/halo/pack_y/pallas_call | solution.py:26
  20.3 7.2 %collective-permute-start.2 = (f32[96,1152]{1,0:T(8,128)}, f32[96,1152]{1,0:T(8,128)S(1)}, u32[]{:S(2)}, u32[]{:S(2)}) collective-permute-start(f32[96,1152]{1,0:T(8,128)} %get-tuple-element.13), channel_id=1, source_target_pairs={{0,1},{1,2},{2,3},{3,4},{4,5},{5,6},{6,7},{7,8},{8,9},{9,10},{10,1... | collective-permute-start | bytes 1327112 | tf_op jit(solution)/shard_map/halo/ppermute | solution.py:319
  27.5 1.9 %collective-permute-start.3 = (f32[96,1152]{1,0:T(8,128)}, f32[96,1152]{1,0:T(8,128)S(1)}, u32[]{:S(2)}, u32[]{:S(2)}) collective-permute-start(f32[96,1152]{1,0:T(8,128)} %get-tuple-element.14), channel_id=1, source_target_pairs={{1,0},{2,1},{3,2},{4,3},{5,4},{6,5},{7,6},{8,7},{9,8},{10,9},{11,1... | collective-permute-start | bytes 1327112 | tf_op jit(solution)/shard_map/halo/ppermute | solution.py:319
  29.4 3.6 %collective-permute-done.2.below = f32[96,1152]{1,0:T(8,128)S(1)} collective-permute-done((f32[96,1152]{1,0:T(8,128)}, f32[96,1152]{1,0:T(8,128)S(1)}, u32[]{:S(2)}, u32[]{:S(2)}) %collective-permute-start.2) | collective-permute-done | bytes 442400 | tf_op jit(solution)/shard_map/halo/ppermute | solution.py:319
  33.0 4.3 %collective-permute-done.3.above = f32[96,1152]{1,0:T(8,128)S(1)} collective-permute-done((f32[96,1152]{1,0:T(8,128)}, f32[96,1152]{1,0:T(8,128)S(1)}, u32[]{:S(2)}, u32[]{:S(2)}) %collective-permute-start.3) | collective-permute-done | bytes 442400 | tf_op jit(solution)/shard_map/halo/ppermute | solution.py:319
  37.3 0.8 copy-done.9
  38.1 15.7 %stiffness.1 = (f32[3,16,3072]{2,1,0:T(8,128)}, f32[256,192]{1,0:T(8,128)}) custom-call(f32[3,16,3072]{2,1,0:T(8,128)} %refs_1_.1, f32[80,768]{1,0:T(8,128)} %copy-done, f32[80,768]{1,0:T(8,128)} %copy-done.1, f32[8,512]{1,0:T(8,128)} %get-tuple-element.12.own, f32[96,1152]{1,0:T(8,128)} %copy-done.8, f32[96,1152]{1,0:T(8,128)} %copy-done.9), custom_call_target="tpu_custom_call" | custom-call | flops 2000000000 | bytes 2768896 | tf_op jit(solution)/shard_map/stiffness/stiffness/pallas_call | solution.py:26
  53.8 22.1 %all_to_all.15 = f32[32,8,192]{2,1,0:T(8,128)S(1)} all-to-all(f32[32,8,192]{2,1,0:T(8,128)} %bitcast.15), channel_id=1, replica_groups=mesh['slab'=32,'band'=16] {'slab'}, dimensions={0} | all-to-all | bytes 393216 | tf_op jit(solution)/shard_map/sums/all_to_all | solution.py:385
  76.0 21.9 %all_to_all.16 = f32[16,8,192]{2,1,0:T(8,128)S(1)} all-to-all(f32[16,8,192]{2,1,0:T(8,128)S(1)} %broadcast_in_dim.28), channel_id=1, replica_groups=mesh['slab'=32,'band'=16] {'band'}, dimensions={0} | all-to-all | bytes 196608 | tf_op jit(solution)/shard_map/sums/all_to_all | solution.py:324
  97.9 16.5 %all_to_all.17 = f32[32,8,192]{2,1,0:T(8,128)} all-to-all(f32[32,8,192]{2,1,0:T(8,128)S(1)} %broadcast_in_dim.29), channel_id=1, replica_groups=mesh['slab'=32,'band'=16] {'slab'}, dimensions={0} | all-to-all | bytes 393216 | tf_op jit(solution)/shard_map/sums/all_to_all | solution.py:324
  114.5 37.4 %rotation.1 = (f32[3,16,1024]{2,1,0:T(8,128)}, f32[3,16,1024]{2,1,0:T(8,128)}, f32[64,64]{1,0:T(8,128)}) custom-call(f32[256,192]{1,0:T(8,128)} %bitcast.16, f32[3,16,3072]{2,1,0:T(8,128)} %refs_1_.1, f32[3,16,3072]{2,1,0:T(8,128)} %get-tuple-element.16.refs_2_), custom_call_target="tpu_custom_call" | custom-call | flops 1000000000 | bytes 1785856 | tf_op jit(solution)/shard_map/rotation/rotation/pallas_call | solution.py:26
  (37 shorter events, 0.9 us)
Async XLA Ops:
  1.5 0.7 copy-start.3
  1.6 0.7 copy-start.6
  1.7 0.7 copy-start.4
  1.7 0.7 copy-start.5
  2.4 0.7 copy-start.7
  3.7 0.6 copy-start.2
  6.2 7.4 %collective-permute-start = (f32[80,768]{1,0:T(8,128)}, f32[80,768]{1,0:T(8,128)S(1)}, u32[]{:S(2)}, u32[]{:S(2)}) collective-permute-start(f32[80,768]{1,0:T(8,128)} %get-tuple-element.10), channel_id=1, source_target_pairs={{0,16},{16,32},{32,48},{48,64},{64,80},{80,96},{96,112},{112,128},... | collective-permute-start | bytes 737288 | tf_op jit(solution)/shard_map/halo/ppermute | solution.py:319
  10.2 7.2 %collective-permute-start.1 = (f32[80,768]{1,0:T(8,128)}, f32[80,768]{1,0:T(8,128)S(1)}, u32[]{:S(2)}, u32[]{:S(2)}) collective-permute-start(f32[80,768]{1,0:T(8,128)} %get-tuple-element.11), channel_id=1, source_target_pairs={{16,0},{32,16},{48,32},{64,48},{80,64},{96,80},{112,96},{128,112},... | collective-permute-start | bytes 737288 | tf_op jit(solution)/shard_map/halo/ppermute | solution.py:319
  13.6 3.7 %copy-start = (f32[80,768]{1,0:T(8,128)}, f32[80,768]{1,0:T(8,128)S(1)}, u32[]{:S(2)}) copy-start(f32[80,768]{1,0:T(8,128)S(1)} %collective-permute-done.left) | copy-start | bytes 737284
  17.4 0.7 copy-start.1
  20.3 12.7 %collective-permute-start.2 = (f32[96,1152]{1,0:T(8,128)}, f32[96,1152]{1,0:T(8,128)S(1)}, u32[]{:S(2)}, u32[]{:S(2)}) collective-permute-start(f32[96,1152]{1,0:T(8,128)} %get-tuple-element.13), channel_id=1, source_target_pairs={{0,1},{1,2},{2,3},{3,4},{4,5},{5,6},{6,7},{7,8},{8,9},{9,10},{10,1... | collective-permute-start | bytes 1327112 | tf_op jit(solution)/shard_map/halo/ppermute | solution.py:319
  27.5 9.8 %collective-permute-start.3 = (f32[96,1152]{1,0:T(8,128)}, f32[96,1152]{1,0:T(8,128)S(1)}, u32[]{:S(2)}, u32[]{:S(2)}) collective-permute-start(f32[96,1152]{1,0:T(8,128)} %get-tuple-element.14), channel_id=1, source_target_pairs={{1,0},{2,1},{3,2},{4,3},{5,4},{6,5},{7,6},{8,7},{9,8},{10,9},{11,1... | collective-permute-start | bytes 1327112 | tf_op jit(solution)/shard_map/halo/ppermute | solution.py:319
  33.0 4.3 %copy-start.8 = (f32[96,1152]{1,0:T(8,128)}, f32[96,1152]{1,0:T(8,128)S(1)}, u32[]{:S(2)}) copy-start(f32[96,1152]{1,0:T(8,128)S(1)} %collective-permute-done.2.below) | copy-start | bytes 1327108
  37.3 0.8 copy-start.9

commit v2 on v1

--- a/solution.py
+++ b/solution.py
@@ -252,27 +252,70 @@
     grams[200:256, :] = jnp.zeros((56, NCOL), f32)
 
 
-def eliminate(ref, step, capture):
-    base = 8 * step
-    panel = ref[base : base + 8, :]
-    columns = [ref[:, base + i : base + i + 1] for i in range(8)]
-    at = lax.broadcasted_iota(jnp.int32, panel.shape, 0)
-    caught = panel
-    for i in range(8):
-        pivot = panel[i : i + 1, base + i : base + i + 1]
-        row = panel[i : i + 1, :]
-        scaled = row * (1.0 / pivot)
-        if capture:
-            root = lax.rsqrt(pivot)
-            root = root * (1.5 - 0.5 * pivot * root * root)
-            caught = jnp.where(at == i, row * root, caught)
-        panel = jnp.where(at == i, scaled, panel - panel[:, base + i : base + i + 1] * scaled)
-    rest = ref[...]
-    for i in range(8):
-        rest = rest - columns[i] * panel[i : i + 1, :]
-    ref[...] = rest
-    ref[base : base + 8, :] = panel
-    return caught
+def lanes_of(tile, column):
+    half = tile[column // 128]
+    at = column % 128
+    return jnp.broadcast_to(half[:, at : at + 1], (8, 128))
+
+
+def row_of(value, row):
+    return jnp.broadcast_to(value[row : row + 1, :], (8, 128))
+
+
+def reduce_block(ref, row0, col0, out):
+    at = lax.broadcasted_iota(jnp.int32, (8, 128), 0)
+    tiles = []
+    for q in range(8):
+        row = row0 + 8 * q
+        tiles.append([ref[row : row + 8, 0:128], ref[row : row + 8, 128:256]])
+    pivots = [lanes_of(tiles[0], col0 + j) for j in range(8)]
+    for t in range(8):
+        first = col0 + 8 * t
+        others = [q for q in range(8) if q != t]
+        if out is not None:
+            others = [q for q in others if q > t]
+        columns = {q: [lanes_of(tiles[q], first + i) for i in range(8)] for q in others}
+        ahead, following = [], []
+        if t < 7:
+            ahead = [lanes_of(tiles[t], first + 8 + j) for j in range(8)]
+            following = [lanes_of(tiles[t + 1], first + 8 + j) for j in range(8)]
+        panel = tiles[t]
+        caught = list(panel)
+        for i in range(8):
+            pivot = row_of(pivots[i], i)
+            inverse = 1.0 / pivot
+            factor = pivots[i]
+            chosen = at == i
+
+            def step(value):
+                row = row_of(value, i) * inverse
+                return jnp.where(chosen, row, value - factor * row)
+
+            if out is not None:
+                root = lax.rsqrt(pivot)
+                root = root * (1.5 - 0.5 * pivot * root * root)
+                caught = [jnp.where(chosen, row_of(p, i) * root, c) for p, c in zip(panel, caught)]
+            pivots = [step(p) if j > i else p for j, p in enumerate(pivots)]
+            ahead = [step(p) for p in ahead]
+            panel = [step(p) for p in panel]
+        tiles[t] = panel
+        if out is not None:
+            out(t, caught)
+        if t < 7:
+            pivots = following
+            for i in range(8):
+                pivots = [
+                    p - columns[t + 1][i] * row_of(a, i) for p, a in zip(pivots, ahead)
+                ]
+        for i in range(8):
+            rows = [row_of(p, i) for p in panel]
+            for q in others:
+                tiles[q] = [v - columns[q][i] * r for v, r in zip(tiles[q], rows)]
+    if out is None:
+        for q in range(8):
+            row = row0 + 8 * q
+            ref[row : row + 8, 0:128] = tiles[q][0]
+            ref[row : row + 8, 128:256] = tiles[q][1]
 
 
 def rotation(scale, grams, basis, images, modes, mode_images, reduced, square, work, small, factor):
@@ -287,8 +330,19 @@
     stiff = jnp.where(at_row < at_col, packed, jnp.where(at_row > at_col, flipped, diagonal))
     work[:, 0:192] = stiff
     work[:, 192:256] = mass[:, 0:64]
-    for step in range(24):
-        eliminate(work, step, False)
+    for block in range(3):
+        base = 64 * block
+        reduce_block(work, base, base, None)
+        reduced_rows = work[base : base + 64, :]
+        for other in range(3):
+            if other != block:
+                rows = slice(64 * other, 64 * other + 64)
+                work[rows, :] = work[rows, :] - jnp.dot(
+                    work[rows, base : base + 64],
+                    reduced_rows,
+                    precision=highest,
+                    preferred_element_type=f32,
+                )
     solved = work[:, 192:256]
     weighted = jnp.dot(mass, solved, precision=highest, preferred_element_type=f32)
     square[0:192, 0:64] = solved
@@ -296,10 +350,13 @@
     small[:, 0:64] = jnp.dot(turned, weighted, precision=highest, preferred_element_type=f32)
     small[:, 64:256] = turned
     factor[...] = jnp.zeros((128, 384), f32)
-    for step in range(8):
-        caught = eliminate(small, step, True)[:, 64:256]
-        factor[8 * step : 8 * step + 8, 0:192] = caught
-        factor[64 + 8 * step : 72 + 8 * step, 192:384] = caught
+
+    def keep(t, caught):
+        value = jnp.concatenate(caught, axis=1)[:, 64:256]
+        factor[8 * t : 8 * t + 8, 0:192] = value
+        factor[64 + 8 * t : 72 + 8 * t, 192:384] = value
+
+    reduce_block(small, 0, 0, keep)
     rotate = factor[0:64, 0:192]
     across = (((1,), (1,)), ((), ()))
     lifted = lax.dot_general(stiff, rotate, across, precision=highest, preferred_element_type=f32)

time: 152 us -> 129 us (0.85)
  Pallas kernels: 57.3 us -> 34 us
    pallas_call x4, Pallas kernels: 57.3 us -> 34 us  [call(): pl.pallas_call(kernel, out_shape=[jax.ShapeDtypeStruct(o, f32) for o in o...]
where the time goes in v2:
time: 129 us
  blocking collectives  60.6 us (47%)
  Pallas kernels  34 us (26%)
  starting transfers between devices  14.4 us (11%)
  waiting for transfers between devices  13.8 us (11%)
  local copies, waits for them, and re-layouts  4.31 us (3%)
    all_to_all x2, blocking collectives, spread(): lax.all_to_all(jnp.broadcast_to(value[None], (size,) + value.shape), axis...  38.5 us
    pallas_call x4, Pallas kernels, call(): pl.pallas_call(kernel, out_shape=[jax.ShapeDtypeStruct(o, f32) for o in o...  34 us
    all_to_all x1, blocking collectives, local(): lax.all_to_all(grams.reshape(slabs, 256 // slabs, NCOL), 'slab', 0, 0, ti...  22.1 us
    ppermute x4, starting transfers between devices, exchange(): return (lax.ppermute(up, axis, forward), lax.ppermute(down, axis, backward))  14.4 us
    ppermute x4, waiting for transfers between devices, exchange(): return (lax.ppermute(up, axis, forward), lax.ppermute(down, axis, backward))  13.8 us
    unnamed x23, local copies, waits for them, and re-layouts  3.42 us
  transfers between devices with their start and end apart: 4, of which 4 were waited for; matrix products, arithmetic and copies ran while one was open for 0% of the time, Pallas kernels for 0%

profile of v2, /device:TPU:1, one launch (start us, length us, event | category | flops | bytes accessed | tf_op | source)
XLA Modules:
  0.0 128.6 jit_solution(8875356064428774445)
XLA Ops:
  0.6 0.7 convert_bitcast_fusion
  1.4 0.1 copy.20
  1.7 0.6 copy-done.3
  2.4 0.6 copy-done.7
  3.4 0.1 reshape.30
  3.6 0.1 reshape.29
  3.7 0.6 copy-done.2
  4.3 1.9 %pack_x.1 = (f32[80,768]{1,0:T(8,128)}, f32[80,768]{1,0:T(8,128)}) custom-call(f32[3,16,3072]{2,1,0:T(8,128)} %refs_1_.1, f32[8,512]{1,0:T(8,128)} %copy-done.2), custom_call_target="tpu_custom_call" | custom-call | flops 1000 | bytes 1097728 | tf_op jit(solution)/shard_map/halo/pack_x/pallas_call | solution.py:26
  6.2 3.9 %collective-permute-start = (f32[80,768]{1,0:T(8,128)}, f32[80,768]{1,0:T(8,128)S(1)}, u32[]{:S(2)}, u32[]{:S(2)}) collective-permute-start(f32[80,768]{1,0:T(8,128)} %get-tuple-element.10), channel_id=1, source_target_pairs={{0,16},{16,32},{32,48},{48,64},{64,80},{80,96},{96,112},{112,128},... | collective-permute-start | bytes 737288 | tf_op jit(solution)/shard_map/halo/ppermute | solution.py:376
  10.2 1.3 %collective-permute-start.1 = (f32[80,768]{1,0:T(8,128)}, f32[80,768]{1,0:T(8,128)S(1)}, u32[]{:S(2)}, u32[]{:S(2)}) collective-permute-start(f32[80,768]{1,0:T(8,128)} %get-tuple-element.11), channel_id=1, source_target_pairs={{16,0},{32,16},{48,32},{64,48},{80,64},{96,80},{112,96},{128,112},... | collective-permute-start | bytes 737288 | tf_op jit(solution)/shard_map/halo/ppermute | solution.py:376
  11.5 2.1 %collective-permute-done.left = f32[80,768]{1,0:T(8,128)S(1)} collective-permute-done((f32[80,768]{1,0:T(8,128)}, f32[80,768]{1,0:T(8,128)S(1)}, u32[]{:S(2)}, u32[]{:S(2)}) %collective-permute-start) | collective-permute-done | bytes 245792 | tf_op jit(solution)/shard_map/halo/ppermute | solution.py:376
  13.6 3.7 %collective-permute-done.1.right = f32[80,768]{1,0:T(8,128)S(1)} collective-permute-done((f32[80,768]{1,0:T(8,128)}, f32[80,768]{1,0:T(8,128)S(1)}, u32[]{:S(2)}, u32[]{:S(2)}) %collective-permute-start.1) | collective-permute-done | bytes 245792 | tf_op jit(solution)/shard_map/halo/ppermute | solution.py:376
  17.4 0.7 copy-done.1
  18.0 2.3 %pack_y.1 = (f32[96,1152]{1,0:T(8,128)}, f32[96,1152]{1,0:T(8,128)}, f32[8,512]{1,0:T(8,128)}) custom-call(f32[3,16,3072]{2,1,0:T(8,128)} %refs_1_.1, f32[8,512]{1,0:T(8,128)} %copy-done.2, f32[80,768]{1,0:T(8,128)} %copy-done, f32[80,768]{1,0:T(8,128)} %copy-done.1), custom_call_target="tpu_custom_call" | custom-call | flops 1000 | bytes 1998848 | tf_op jit(solution)/shard_map/halo/pack_y/pallas_call | solution.py:26
  20.3 7.2 %collective-permute-start.2 = (f32[96,1152]{1,0:T(8,128)}, f32[96,1152]{1,0:T(8,128)S(1)}, u32[]{:S(2)}, u32[]{:S(2)}) collective-permute-start(f32[96,1152]{1,0:T(8,128)} %get-tuple-element.13), channel_id=1, source_target_pairs={{0,1},{1,2},{2,3},{3,4},{4,5},{5,6},{6,7},{7,8},{8,9},{9,10},{10,1... | collective-permute-start | bytes 1327112 | tf_op jit(solution)/shard_map/halo/ppermute | solution.py:376
  27.5 1.9 %collective-permute-start.3 = (f32[96,1152]{1,0:T(8,128)}, f32[96,1152]{1,0:T(8,128)S(1)}, u32[]{:S(2)}, u32[]{:S(2)}) collective-permute-start(f32[96,1152]{1,0:T(8,128)} %get-tuple-element.14), channel_id=1, source_target_pairs={{1,0},{2,1},{3,2},{4,3},{5,4},{6,5},{7,6},{8,7},{9,8},{10,9},{11,1... | collective-permute-start | bytes 1327112 | tf_op jit(solution)/shard_map/halo/ppermute | solution.py:376
  29.4 3.6 %collective-permute-done.2.below = f32[96,1152]{1,0:T(8,128)S(1)} collective-permute-done((f32[96,1152]{1,0:T(8,128)}, f32[96,1152]{1,0:T(8,128)S(1)}, u32[]{:S(2)}, u32[]{:S(2)}) %collective-permute-start.2) | collective-permute-done | bytes 442400 | tf_op jit(solution)/shard_map/halo/ppermute | solution.py:376
  33.0 4.3 %collective-permute-done.3.above = f32[96,1152]{1,0:T(8,128)S(1)} collective-permute-done((f32[96,1152]{1,0:T(8,128)}, f32[96,1152]{1,0:T(8,128)S(1)}, u32[]{:S(2)}, u32[]{:S(2)}) %collective-permute-start.3) | collective-permute-done | bytes 442400 | tf_op jit(solution)/shard_map/halo/ppermute | solution.py:376
  37.3 0.8 copy-done.9
  38.1 15.7 %stiffness.1 = (f32[3,16,3072]{2,1,0:T(8,128)}, f32[256,192]{1,0:T(8,128)}) custom-call(f32[3,16,3072]{2,1,0:T(8,128)} %refs_1_.1, f32[80,768]{1,0:T(8,128)} %copy-done, f32[80,768]{1,0:T(8,128)} %copy-done.1, f32[8,512]{1,0:T(8,128)} %get-tuple-element.12.own, f32[96,1152]{1,0:T(8,128)} %copy-done.8, f32[96,1152]{1,0:T(8,128)} %copy-done.9), custom_call_target="tpu_custom_call" | custom-call | flops 2000000000 | bytes 2768896 | tf_op jit(solution)/shard_map/stiffness/stiffness/pallas_call | solution.py:26
  53.8 22.1 %all_to_all.15 = f32[32,8,192]{2,1,0:T(8,128)S(1)} all-to-all(f32[32,8,192]{2,1,0:T(8,128)} %bitcast.15), channel_id=1, replica_groups=mesh['slab'=32,'band'=16] {'slab'}, dimensions={0} | all-to-all | bytes 393216 | tf_op jit(solution)/shard_map/sums/all_to_all | solution.py:442
  76.0 21.9 %all_to_all.16 = f32[16,8,192]{2,1,0:T(8,128)S(1)} all-to-all(f32[16,8,192]{2,1,0:T(8,128)S(1)} %broadcast_in_dim.28), channel_id=1, replica_groups=mesh['slab'=32,'band'=16] {'band'}, dimensions={0} | all-to-all | bytes 196608 | tf_op jit(solution)/shard_map/sums/all_to_all | solution.py:381
  97.9 16.5 %all_to_all.17 = f32[32,8,192]{2,1,0:T(8,128)} all-to-all(f32[32,8,192]{2,1,0:T(8,128)S(1)} %broadcast_in_dim.29), channel_id=1, replica_groups=mesh['slab'=32,'band'=16] {'slab'}, dimensions={0} | all-to-all | bytes 393216 | tf_op jit(solution)/shard_map/sums/all_to_all | solution.py:381
  114.5 14.2 %rotation.1 = (f32[3,16,1024]{2,1,0:T(8,128)}, f32[3,16,1024]{2,1,0:T(8,128)}, f32[64,64]{1,0:T(8,128)}) custom-call(f32[256,192]{1,0:T(8,128)} %bitcast.16, f32[3,16,3072]{2,1,0:T(8,128)} %refs_1_.1, f32[3,16,3072]{2,1,0:T(8,128)} %get-tuple-element.16.refs_2_), custom_call_target="tpu_custom_call" | custom-call | flops 1000000000 | bytes 1785856 | tf_op jit(solution)/shard_map/rotation/rotation/pallas_call | solution.py:26
  (37 shorter events, 0.9 us)
Async XLA Ops:
  1.5 0.7 copy-start.3
  1.6 0.7 copy-start.6
  1.7 0.7 copy-start.4
  1.7 0.7 copy-start.5
  2.4 0.7 copy-start.7
  3.7 0.6 copy-start.2
  6.2 7.4 %collective-permute-start = (f32[80,768]{1,0:T(8,128)}, f32[80,768]{1,0:T(8,128)S(1)}, u32[]{:S(2)}, u32[]{:S(2)}) collective-permute-start(f32[80,768]{1,0:T(8,128)} %get-tuple-element.10), channel_id=1, source_target_pairs={{0,16},{16,32},{32,48},{48,64},{64,80},{80,96},{96,112},{112,128},... | collective-permute-start | bytes 737288 | tf_op jit(solution)/shard_map/halo/ppermute | solution.py:376
  10.2 7.2 %collective-permute-start.1 = (f32[80,768]{1,0:T(8,128)}, f32[80,768]{1,0:T(8,128)S(1)}, u32[]{:S(2)}, u32[]{:S(2)}) collective-permute-start(f32[80,768]{1,0:T(8,128)} %get-tuple-element.11), channel_id=1, source_target_pairs={{16,0},{32,16},{48,32},{64,48},{80,64},{96,80},{112,96},{128,112},... | collective-permute-start | bytes 737288 | tf_op jit(solution)/shard_map/halo/ppermute | solution.py:376
  13.6 3.7 %copy-start = (f32[80,768]{1,0:T(8,128)}, f32[80,768]{1,0:T(8,128)S(1)}, u32[]{:S(2)}) copy-start(f32[80,768]{1,0:T(8,128)S(1)} %collective-permute-done.left) | copy-start | bytes 737284
  17.4 0.7 copy-start.1
  20.3 12.7 %collective-permute-start.2 = (f32[96,1152]{1,0:T(8,128)}, f32[96,1152]{1,0:T(8,128)S(1)}, u32[]{:S(2)}, u32[]{:S(2)}) collective-permute-start(f32[96,1152]{1,0:T(8,128)} %get-tuple-element.13), channel_id=1, source_target_pairs={{0,1},{1,2},{2,3},{3,4},{4,5},{5,6},{6,7},{7,8},{8,9},{9,10},{10,1... | collective-permute-start | bytes 1327112 | tf_op jit(solution)/shard_map/halo/ppermute | solution.py:376
  27.5 9.8 %collective-permute-start.3 = (f32[96,1152]{1,0:T(8,128)}, f32[96,1152]{1,0:T(8,128)S(1)}, u32[]{:S(2)}, u32[]{:S(2)}) collective-permute-start(f32[96,1152]{1,0:T(8,128)} %get-tuple-element.14), channel_id=1, source_target_pairs={{1,0},{2,1},{3,2},{4,3},{5,4},{6,5},{7,6},{8,7},{9,8},{10,9},{11,1... | collective-permute-start | bytes 1327112 | tf_op jit(solution)/shard_map/halo/ppermute | solution.py:376
  33.0 4.3 %copy-start.8 = (f32[96,1152]{1,0:T(8,128)}, f32[96,1152]{1,0:T(8,128)S(1)}, u32[]{:S(2)}) copy-start(f32[96,1152]{1,0:T(8,128)S(1)} %collective-permute-done.2.below) | copy-start | bytes 1327108
  37.3 0.8 copy-start.9

commit v3 on v2

--- a/solution.py
+++ b/solution.py
@@ -21,11 +21,15 @@
 PARAMS = pltpu.CompilerParams(vmem_limit_bytes=56 * 1024 * 1024)
 
 
-def call(kernel, outs, scratch, args, flops, name):
+def hold(value):
+    return pltpu.with_memory_space_constraint(value, pltpu.VMEM)
+
+
+def call(kernel, outs, scratch, args, flops, name, near=True):
     size = sum(a.size for a in args) + sum(o[0] * o[1] * (o[2] if len(o) > 2 else 1) for o in outs)
     return pl.pallas_call(
         kernel,
-        out_shape=[jax.ShapeDtypeStruct(o, f32) for o in outs],
+        out_shape=[(pltpu.VMEM if near else jax.ShapeDtypeStruct)(o, f32) for o in outs],
         in_specs=[VMEM] * len(args),
         out_specs=[VMEM] * len(outs),
         scratch_shapes=scratch,
@@ -35,14 +39,36 @@
     )(*args)
 
 
-def pack_x(basis, geo, up, down):
-    for out, first, lane in ((up, SIDE - HALO, 256), (down, 0, 384)):
+def pack_x(basis, offsets, bond, bulk, springs, intact, up, down, geo, square, table):
+    square[...] = jnp.zeros((128, 128), f32)
+    for channel in range(3):
+        square[16 * channel : 16 * channel + 16, 0:16] = offsets[channel]
+    for channel, part in ((3, bond), (4, bulk), (5, springs)):
+        square[16 * channel : 16 * channel + 16, 0:16] = part[...]
+    table[...] = square[...].T
+    for y in range(SIDE):
+        for channel in range(6):
+            at = 16 * channel
+            geo[channel : channel + 1, 16 * y : 16 * y + 16] = table[y : y + 1, at : at + 16]
+    lists = intact[...].astype(f32)
+    gap = jnp.zeros((1, 4), f32)
+    fill = jnp.zeros((1, 3), f32)
+    for by in range(2):
+        most = lists[0, by : by + 1, 0:6]
+        rest = jnp.concatenate([lists[0, by : by + 1, 6:9], fill], axis=1)
+        for row, part in ((6, rest), (7, most)):
+            pattern = jnp.concatenate([part, gap, part], axis=1)
+            pattern = jnp.concatenate([pattern, pattern], axis=1)
+            pattern = jnp.concatenate([pattern, pattern], axis=1)
+            pattern = jnp.concatenate([pattern, pattern], axis=1)
+            geo[row : row + 1, 128 * by : 128 * by + 128] = pattern
+    for out, first in ((up, SIDE - HALO), (down, 0)):
         for c in range(3):
             for j in range(4):
                 row = j * 18 + c * 6
                 out[row : row + 6, :] = basis[c, first : first + 6, j * 768 : (j + 1) * 768]
         out[72:80, :] = jnp.zeros((8, 768), f32)
-        out[72:80, 0:128] = geo[:, lane : lane + 128]
+        out[72:80, 0:256] = geo[...]
 
 
 def pack_y(basis, geo, left, right, up, down, own):
@@ -50,8 +76,8 @@
     for y in range(SIDE):
         at = GROUP * y
         own[:, at : at + 16] = geo[:, 16 * y : 16 * y + 16]
-        own[:, at + 16 : at + 22] = left[72:80, 8 * y : 8 * y + 6]
-        own[:, at + 22 : at + 28] = right[72:80, 8 * y : 8 * y + 6]
+        own[:, at + 16 : at + 22] = left[72:80, 16 * y + 10 : 16 * y + 16]
+        own[:, at + 22 : at + 28] = right[72:80, 16 * y : 16 * y + 6]
     for out, first in ((up, SIDE - HALO), (down, 0)):
         pieces = ((2, 384, 768, 0), (3, 0, 768, 384)) if first else ((0, 0, 768, 0), (1, 0, 384, 768))
         for c in range(3):
@@ -80,6 +106,21 @@
         + jnp.dot(high, right_low, preferred_element_type=f32)
         + jnp.dot(low, right_high, preferred_element_type=f32)
     )
+
+
+def gram(a, b):
+    return lax.dot_general(
+        a, b, (((0,), (0,)), ((), ())), precision=highest, preferred_element_type=f32
+    )
+
+
+def prepare(basis, rows, mass):
+    for c in range(3):
+        for y in range(SIDE):
+            row = 256 * c + 16 * y
+            rows[row : row + 16, :] = basis[c, :, y * NCOL : (y + 1) * NCOL]
+    value = rows[...]
+    mass[...] = gram(value, value)
 
 
 def block_masks(s, table):
@@ -110,7 +151,7 @@
 
 
 def stiffness(
-    basis, left, right, own, below, above, images, grams,
+    rows, mass, left, right, own, below, above, images, grams,
     geo, geo_cols, geo_far, field, high, low, dil_high, dil_low, result,
 ):
     geo[...] = jnp.zeros((8, 1024), f32)
@@ -136,7 +177,7 @@
             j, t = divmod(y, 4)
             src = j * 18 + c * 6
             row = GROUP * y
-            field[c, row : row + 16, :] = basis[c, :, y * NCOL : (y + 1) * NCOL]
+            field[c, row : row + 16, :] = rows[256 * c + 16 * y : 256 * c + 16 * y + 16, :]
             field[c, row + 16 : row + 22, :] = left[src : src + 6, t * NCOL : (t + 1) * NCOL]
             field[c, row + 22 : row + 28, :] = right[src : src + 6, t * NCOL : (t + 1) * NCOL]
             field[c, row + 28 : row + 32, :] = jnp.zeros((4, NCOL), f32)
@@ -179,7 +220,7 @@
         dil_low[pl.ds(near, 64), :] = parts[1]
         return carry
 
-    lax.fori_loop(0, STRIPS, dilatations, 0)
+    lax.fori_loop(0, STRIPS, dilatations, 0, unroll=6)
 
     row = lax.broadcasted_iota(jnp.int32, (32, FAR), 0)
     lane = lax.broadcasted_iota(jnp.int32, (32, FAR), 1)
@@ -227,26 +268,16 @@
             result[i, pl.ds(at, 32), :] = image[32 * i : 32 * i + 32]
         return carry
 
-    lax.fori_loop(2, 10, forces, 0)
+    lax.fori_loop(2, 10, forces, 0, unroll=4)
 
     for c in range(3):
         for y in range(SIDE):
             images[c, :, y * NCOL : (y + 1) * NCOL] = result[c, 16 * y : 16 * y + 16, :]
 
-    rows = field[...].reshape(3, SIDE, GROUP, NCOL)[:, :, 0:16, :].reshape(768, NCOL)
-    image = result[...].reshape(768, NCOL)
-
-    def gram(a, b):
-        return lax.dot_general(
-            a, b, (((0,), (0,)), ((), ())), precision=highest, preferred_element_type=f32
-        )
-
-    mass = gram(rows, rows)
-    stiff = gram(rows, image)
-    mirror = gram(image, rows)
+    stiff = gram(rows[...], result[...].reshape(768, NCOL))
     at_row = lax.broadcasted_iota(jnp.int32, (NCOL, NCOL), 0)
     at_col = lax.broadcasted_iota(jnp.int32, (NCOL, NCOL), 1)
-    grams[0:192, :] = jnp.where(at_row >= at_col, mass, 0.5 * (stiff + mirror))
+    grams[0:192, :] = jnp.where(at_row >= at_col, mass[...], stiff)
     diagonal = jnp.sum(jnp.where(at_row == at_col, stiff, 0.0), axis=0, keepdims=True)
     grams[192:200, :] = jnp.broadcast_to(diagonal, (8, NCOL))
     grams[200:256, :] = jnp.zeros((56, NCOL), f32)
@@ -385,36 +416,23 @@
     slabs = lax.axis_size("slab")
     bands = lax.axis_size("band")
     total_rows = float(3 * SIDE * SIDE * slabs * bands)
-
-    with jax.named_scope("geometry"):
-        table = intact[0].astype(f32)
-        table = jnp.stack([jnp.pad(table[:, 6:9], ((0, 0), (0, 3))), table[:, 0:6]])
-        table = jnp.repeat(table, SIDE // 2, axis=1)
-        points = jnp.concatenate(
-            [offsets, bond_modulus[None], bulk_modulus[None], springs[None]], axis=0
-        ).transpose(0, 2, 1)
-
-        def lanes(part, width):
-            pads = width - part.shape[2]
-            part = jnp.concatenate(
-                [
-                    jnp.pad(part, ((0, 0), (0, 0), (0, pads))),
-                    jnp.pad(table, ((0, 0), (0, 0), (0, width - 6))),
-                ],
-                axis=0,
-            )
-            return part.reshape(8, SIDE * width)
-
-        geo = jnp.concatenate(
-            [lanes(points, 16), lanes(points[:, :, SIDE - HALO :], 8), lanes(points[:, :, :HALO], 8)],
-            axis=1,
-        )
+    basis = hold(basis)
 
     with jax.named_scope("halo"):
-        up, down = call(pack_x, [(80, 768)] * 2, [], (basis, geo), 1000, "pack_x")
+        up, down, geo = call(
+            pack_x,
+            [(80, 768)] * 2 + [(8, 256)],
+            [pltpu.VMEM((128, 128), f32)] * 2,
+            (basis, offsets, bond_modulus, bulk_modulus, springs, intact),
+            1000,
+            "pack_x",
+        )
         left, right = exchange(up, down, "slab")
+        rows, mass = call(
+            prepare, [(768, NCOL), (NCOL, NCOL)], [], (basis,), 3 * 10**8, "prepare"
+        )
         up, down, own = call(
-            pack_y, [(96, 1152)] * 2 + [(8, 512)], [], (basis, geo, left, right), 1000, "pack_y"
+            pack_y, [(96, 1152)] * 2 + [(8, 512)], [], (basis, hold(geo), hold(left), hold(right)), 1000, "pack_y"
         )
         below, above = exchange(up, down, "band")
 
@@ -433,7 +451,7 @@
                 pltpu.VMEM((1024, NCOL), bf16),
                 pltpu.VMEM((3, 256, NCOL), f32),
             ],
-            (basis, left, right, own, below, above),
+            (hold(rows), hold(mass), hold(left), hold(right), hold(own), hold(below), hold(above)),
             2 * 10**9,
             "stiffness",
         )
@@ -457,9 +475,10 @@
                 pltpu.VMEM((64, 256), f32),
                 pltpu.VMEM((128, 384), f32),
             ],
-            (grams, basis, images),
+            (hold(grams), basis, hold(images)),
             10**9,
             "rotation",
+            False,
         )
     return modes, mode_images, reduced
 

time: 129 us -> 112 us (0.87)
  Pallas kernels: 34 us -> 23 us
  local copies, waits for them, and re-layouts: 4.31 us -> 1.1 us
  waiting for transfers between devices: 13.8 us -> 12.4 us
    pallas_call x4 -> x5, Pallas kernels: 34 us -> 23 us  [call(): pl.pallas_call(kernel, out_shape=[(pltpu.VMEM if near else jax.ShapeDtype...]
    unnamed x23 -> x4, local copies, waits for them, and re-layouts: 3.42 us -> 1.07 us
    ppermute x4, waiting for transfers between devices: 13.8 us -> 12.4 us  [exchange(): return (lax.ppermute(up, axis, forward), lax.ppermute(down, axis, backward))]
  transfers between devices with their start and end apart: 4 -> 4, of which waited for: 4 -> 4; matrix products, arithmetic and copies ran while one was open for 0% -> 0% of each run, Pallas kernels for 0% -> 1%
where the time goes in v3:
time: 112 us; the launch traced here: 111 us
  blocking collectives  59.5 us (53%)
  Pallas kernels  23 us (21%)
  starting transfers between devices  14.4 us (13%)
  waiting for transfers between devices  12.4 us (11%)
    all_to_all x2, blocking collectives, spread(): lax.all_to_all(jnp.broadcast_to(value[None], (size,) + value.shape), axis...  37.8 us
    pallas_call x5, Pallas kernels, call(): pl.pallas_call(kernel, out_shape=[(pltpu.VMEM if near else jax.ShapeDtype...  23 us
    all_to_all x1, blocking collectives, local(): lax.all_to_all(grams.reshape(slabs, 256 // slabs, NCOL), 'slab', 0, 0, ti...  21.7 us
    ppermute x4, starting transfers between devices, exchange(): return (lax.ppermute(up, axis, forward), lax.ppermute(down, axis, backward))  14.4 us
    ppermute x4, waiting for transfers between devices, exchange(): return (lax.ppermute(up, axis, forward), lax.ppermute(down, axis, backward))  12.4 us
  transfers between devices with their start and end apart: 4, of which 4 were waited for; matrix products, arithmetic and copies ran while one was open for 0% of the time, Pallas kernels for 1%

profile of v3, /device:TPU:1, one launch (start us, length us, event | category | flops | bytes accessed | tf_op | source)
XLA Modules:
  0.0 111.2 jit_solution(6112323794812355396)
XLA Ops:
  0.6 0.0 copy-start
  0.6 1.1 copy-done
  1.7 1.2 %pack_x.1 = (f32[80,768]{1,0:T(8,128)S(1)}, f32[80,768]{1,0:T(8,128)S(1)}, f32[8,256]{1,0:T(8,128)S(1)}) custom-call(f32[3,16,3072]{2,1,0:T(8,128)S(1)} %copy-done, f32[3,16,16]{2,1,0:T(8,128)} %offsets.1, f32[16,16]{1,0:T(8,128)} %bond.1, f32[16,16]{1,0:T(8,128)} %bulk.1, f32[16,16]{1,0:T(8,128)} %springs.1, s32[1,2,9]{2,1,0:T(2,128)} %intact.1), custom_call_target="tpu_custom_call" | custom-call | flops 1000 | bytes 1095752 | tf_op jit(solution)/shard_map/halo/pack_x/pallas_call | solution.py:30
  2.9 4.0 %collective-permute-start = (f32[80,768]{1,0:T(8,128)S(1)}, f32[80,768]{1,0:T(8,128)S(1)}, u32[]{:S(2)}, u32[]{:S(2)}) collective-permute-start(f32[80,768]{1,0:T(8,128)S(1)} %get-tuple-element.15), channel_id=1, source_target_pairs={{0,16},{16,32},{32,48},{48,64},{64,80},{80,96},{96,112},{112,128},... | collective-permute-start | bytes 737288 | tf_op jit(solution)/shard_map/halo/ppermute | solution.py:407
  6.9 1.3 %collective-permute-start.1 = (f32[80,768]{1,0:T(8,128)S(1)}, f32[80,768]{1,0:T(8,128)S(1)}, u32[]{:S(2)}, u32[]{:S(2)}) collective-permute-start(f32[80,768]{1,0:T(8,128)S(1)} %get-tuple-element.16), channel_id=1, source_target_pairs={{16,0},{32,16},{48,32},{64,48},{80,64},{96,80},{112,96},{128,112},... | collective-permute-start | bytes 737288 | tf_op jit(solution)/shard_map/halo/ppermute | solution.py:407
  8.2 1.8 %collective-permute-done.left = f32[80,768]{1,0:T(8,128)S(1)} collective-permute-done((f32[80,768]{1,0:T(8,128)S(1)}, f32[80,768]{1,0:T(8,128)S(1)}, u32[]{:S(2)}, u32[]{:S(2)}) %collective-permute-start) | collective-permute-done | bytes 245792 | tf_op jit(solution)/shard_map/halo/ppermute | solution.py:407
  10.0 3.8 %collective-permute-done.1.right = f32[80,768]{1,0:T(8,128)S(1)} collective-permute-done((f32[80,768]{1,0:T(8,128)S(1)}, f32[80,768]{1,0:T(8,128)S(1)}, u32[]{:S(2)}, u32[]{:S(2)}) %collective-permute-start.1) | collective-permute-done | bytes 245792 | tf_op jit(solution)/shard_map/halo/ppermute | solution.py:407
  13.8 0.2 pack_y.1
  14.0 7.2 %collective-permute-start.2 = (f32[96,1152]{1,0:T(8,128)S(1)}, f32[96,1152]{1,0:T(8,128)S(1)}, u32[]{:S(2)}, u32[]{:S(2)}) collective-permute-start(f32[96,1152]{1,0:T(8,128)S(1)} %get-tuple-element.19), channel_id=1, source_target_pairs={{0,1},{1,2},{2,3},{3,4},{4,5},{5,6},{6,7},{7,8},{8,9},{9,10},{10,1... | collective-permute-start | bytes 1327112 | tf_op jit(solution)/shard_map/halo/ppermute | solution.py:407
  21.2 1.9 %collective-permute-start.3 = (f32[96,1152]{1,0:T(8,128)S(1)}, f32[96,1152]{1,0:T(8,128)S(1)}, u32[]{:S(2)}, u32[]{:S(2)}) collective-permute-start(f32[96,1152]{1,0:T(8,128)S(1)} %get-tuple-element.20), channel_id=1, source_target_pairs={{1,0},{2,1},{3,2},{4,3},{5,4},{6,5},{7,6},{8,7},{9,8},{10,9},{11,1... | collective-permute-start | bytes 1327112 | tf_op jit(solution)/shard_map/halo/ppermute | solution.py:407
  23.2 0.9 prepare.1
  24.1 2.4 %collective-permute-done.2.below = f32[96,1152]{1,0:T(8,128)S(1)} collective-permute-done((f32[96,1152]{1,0:T(8,128)S(1)}, f32[96,1152]{1,0:T(8,128)S(1)}, u32[]{:S(2)}, u32[]{:S(2)}) %collective-permute-start.2) | collective-permute-done | bytes 442400 | tf_op jit(solution)/shard_map/halo/ppermute | solution.py:407
  26.4 4.4 %collective-permute-done.3.above = f32[96,1152]{1,0:T(8,128)S(1)} collective-permute-done((f32[96,1152]{1,0:T(8,128)S(1)}, f32[96,1152]{1,0:T(8,128)S(1)}, u32[]{:S(2)}, u32[]{:S(2)}) %collective-permute-start.3) | collective-permute-done | bytes 442400 | tf_op jit(solution)/shard_map/halo/ppermute | solution.py:407
  30.8 7.8 %stiffness.1 = (f32[3,16,3072]{2,1,0:T(8,128)S(1)}, f32[256,192]{1,0:T(8,128)S(1)}) custom-call(f32[768,192]{1,0:T(8,128)S(1)} %get-tuple-element.13.rows, f32[192,192]{1,0:T(8,128)S(1)} %get-tuple-element.14.mass, f32[80,768]{1,0:T(8,128)S(1)} %collective-permute-done.left, f32[80,768]{1,0:T(8,128)S(1)} %collective-permute-done.1.right, ...), custom_call_target="tpu_custom_call" | custom-call | flops 2000000000 | bytes 2916352 | tf_op jit(solution)/shard_map/stiffness/stiffness/pallas_call | solution.py:30
  38.6 21.7 %all_to_all.15 = f32[32,8,192]{2,1,0:T(8,128)S(1)} all-to-all(f32[32,8,192]{2,1,0:T(8,128)S(1)} %bitcast.2), channel_id=1, replica_groups=mesh['slab'=32,'band'=16] {'slab'}, dimensions={0} | all-to-all | bytes 393216 | tf_op jit(solution)/shard_map/sums/all_to_all | solution.py:460
  60.4 0.0 copy-start.1
  60.4 22.3 %all_to_all.16 = f32[16,8,192]{2,1,0:T(8,128)S(1)} all-to-all(f32[16,8,192]{2,1,0:T(8,128)S(1)} %broadcast_in_dim.4), channel_id=1, replica_groups=mesh['slab'=32,'band'=16] {'band'}, dimensions={0} | all-to-all | bytes 196608 | tf_op jit(solution)/shard_map/sums/all_to_all | solution.py:412
  82.7 15.6 %all_to_all.17 = f32[32,8,192]{2,1,0:T(8,128)S(1)} all-to-all(f32[32,8,192]{2,1,0:T(8,128)S(1)} %broadcast_in_dim.5), channel_id=1, replica_groups=mesh['slab'=32,'band'=16] {'slab'}, dimensions={0} | all-to-all | bytes 393216 | tf_op jit(solution)/shard_map/sums/all_to_all | solution.py:412
  98.3 0.0 copy-done.1
  98.3 12.9 %rotation.1 = (f32[3,16,1024]{2,1,0:T(8,128)}, f32[3,16,1024]{2,1,0:T(8,128)}, f32[64,64]{1,0:T(8,128)}) custom-call(f32[256,192]{1,0:T(8,128)S(1)} %bitcast.3, f32[3,16,3072]{2,1,0:T(8,128)S(1)} %copy-done.1, f32[3,16,3072]{2,1,0:T(8,128)S(1)} %get-tuple-element.22.refs_2_), custom_call_target="tpu_custom_call" | custom-call | flops 1000000000 | bytes 1785856 | tf_op jit(solution)/shard_map/rotation/rotation/pallas_call | solution.py:30
  (4 shorter events, 0.1 us)
Async XLA Ops:
  0.6 1.1 copy-start
  2.9 7.1 %collective-permute-start = (f32[80,768]{1,0:T(8,128)S(1)}, f32[80,768]{1,0:T(8,128)S(1)}, u32[]{:S(2)}, u32[]{:S(2)}) collective-permute-start(f32[80,768]{1,0:T(8,128)S(1)} %get-tuple-element.15), channel_id=1, source_target_pairs={{0,16},{16,32},{32,48},{48,64},{64,80},{80,96},{96,112},{112,128},... | collective-permute-start | bytes 737288 | tf_op jit(solution)/shard_map/halo/ppermute | solution.py:407
  6.9 6.9 %collective-permute-start.1 = (f32[80,768]{1,0:T(8,128)S(1)}, f32[80,768]{1,0:T(8,128)S(1)}, u32[]{:S(2)}, u32[]{:S(2)}) collective-permute-start(f32[80,768]{1,0:T(8,128)S(1)} %get-tuple-element.16), channel_id=1, source_target_pairs={{16,0},{32,16},{48,32},{64,48},{80,64},{96,80},{112,96},{128,112},... | collective-permute-start | bytes 737288 | tf_op jit(solution)/shard_map/halo/ppermute | solution.py:407
  14.0 12.4 %collective-permute-start.2 = (f32[96,1152]{1,0:T(8,128)S(1)}, f32[96,1152]{1,0:T(8,128)S(1)}, u32[]{:S(2)}, u32[]{:S(2)}) collective-permute-start(f32[96,1152]{1,0:T(8,128)S(1)} %get-tuple-element.19), channel_id=1, source_target_pairs={{0,1},{1,2},{2,3},{3,4},{4,5},{5,6},{6,7},{7,8},{8,9},{9,10},{10,1... | collective-permute-start | bytes 1327112 | tf_op jit(solution)/shard_map/halo/ppermute | solution.py:407
  21.2 9.6 %collective-permute-start.3 = (f32[96,1152]{1,0:T(8,128)S(1)}, f32[96,1152]{1,0:T(8,128)S(1)}, u32[]{:S(2)}, u32[]{:S(2)}) collective-permute-start(f32[96,1152]{1,0:T(8,128)S(1)} %get-tuple-element.20), channel_id=1, source_target_pairs={{1,0},{2,1},{3,2},{4,3},{5,4},{6,5},{7,6},{8,7},{9,8},{10,9},{11,1... | collective-permute-start | bytes 1327112 | tf_op jit(solution)/shard_map/halo/ppermute | solution.py:407
  60.4 37.9 %copy-start.1 = (f32[3,16,3072]{2,1,0:T(8,128)S(1)}, f32[3,16,3072]{2,1,0:T(8,128)}, u32[]{:S(2)}) copy-start(f32[3,16,3072]{2,1,0:T(8,128)} %refs_1_.1) | copy-start | bytes 1769476

commit v4 on v3

--- a/solution.py
+++ b/solution.py
@@ -26,10 +26,11 @@
 
 
 def call(kernel, outs, scratch, args, flops, name, near=True):
-    size = sum(a.size for a in args) + sum(o[0] * o[1] * (o[2] if len(o) > 2 else 1) for o in outs)
+    outs = [(o, f32) if isinstance(o[0], int) else o for o in outs]
+    size = sum(a.size for a in args)
     return pl.pallas_call(
         kernel,
-        out_shape=[(pltpu.VMEM if near else jax.ShapeDtypeStruct)(o, f32) for o in outs],
+        out_shape=[(pltpu.VMEM if near else jax.ShapeDtypeStruct)(*o) for o in outs],
         in_specs=[VMEM] * len(args),
         out_specs=[VMEM] * len(outs),
         scratch_shapes=scratch,
@@ -150,15 +151,13 @@
     return vector, jnp.maximum(1.0 - square * (1.0 / 9.0), 0.0)
 
 
-def stiffness(
-    rows, mass, left, right, own, below, above, images, grams,
-    geo, geo_cols, geo_far, field, high, low, dil_high, dil_low, result,
-):
+def locate(own, below, above, geo, geo_cols, geo_far, strips):
     geo[...] = jnp.zeros((8, 1024), f32)
     geo[:, 256:768] = own[...]
     for part, lane in ((below, 64), (above, 768)):
-        geo[0:4, lane : lane + 192] = part[28:32, 0:192]
-        geo[4:8, lane : lane + 192] = part[60:64, 0:192]
+        if part is not None:
+            geo[0:4, lane : lane + 192] = part[28:32, 0:192]
+            geo[4:8, lane : lane + 192] = part[60:64, 0:192]
     lane = lax.broadcasted_iota(jnp.int32, (8, 1024), 1)
     channel = lax.broadcasted_iota(jnp.int32, (8, 1024), 0)
     xi = lane & 31
@@ -168,24 +167,127 @@
     placed = geo[...] + place
     geo[...] = placed
     geo_cols[...] = placed.T
-    for s in range(STRIPS):
+    for s in strips:
         start = GROUP * (2 * s + 1)
         geo_far[s] = geo[:, start : start + FAR]
 
+
+def rows_of(s):
+    near = pl.multiple_of(GROUP * (2 * s + 4), 64)
+    start = pl.multiple_of(GROUP * (2 * s + 1), 32)
+    return near, start
+
+
+def dilatation(s, geo_cols, geo_far, high, low, shift):
+    row = lax.broadcasted_iota(jnp.int32, (64, FAR), 0)
+    lane = lax.broadcasted_iota(jnp.int32, (64, FAR), 1)
+    home_row = row & 31
+    near, start = rows_of(s)
+    home = geo_cols[pl.ds(near, 64), :]
+    middle, before, after = block_masks(s, home[0:32])
+    vector, weight = bonds(geo_far[s], home)
+    weight = weight * jnp.where(home_row < 16, middle, jnp.where(home_row < 22, before, after))
+    far = pl.ds(pl.multiple_of(start - shift, 32), FAR)
+    total = jnp.zeros((64, NCOL), f32)
+    for j in range(3):
+        matrix = weight * vector[j]
+        matrix = jnp.where(lane == row + 96, -jnp.sum(matrix, axis=1, keepdims=True), matrix)
+        total = total + product(matrix, high[j, far, :], low[j, far, :])
+    return split(total * (home[:, 4:5] * (1.0 / 27.0)))
+
+
+def own_bonds(s, geo_cols, geo_far):
+    row = lax.broadcasted_iota(jnp.int32, (32, FAR), 0)
+    lane = lax.broadcasted_iota(jnp.int32, (32, FAR), 1)
+    at_self = lane == row + jnp.where(row < 16, 96, 112)
+    near, _ = rows_of(s)
+    first = geo_cols[pl.ds(near, 32), :]
+    second = geo_cols[pl.ds(near + 32, 16), :]
+    home = jnp.concatenate([first[0:16], second], axis=0)
+    middle, _, _ = block_masks(s, first)
+    vector, weight = bonds(geo_far[s], home)
+    return home, vector, weight * middle, at_self
+
+
+def bond_forces(s, tied, geo_far, high, low, shift):
+    home, vector, weight, at_self = tied
+    coupling = weight * ((home[:, 3:4] + geo_far[s, 3:4, :]) * (1.0 / 18.0))
+    spring = home[:, 5:6]
+    pairs = {}
+    for i in range(3):
+        side = coupling * vector[i]
+        for j in range(i, 3):
+            matrix = side * vector[j]
+            total = jnp.sum(matrix, axis=1, keepdims=True)
+            if i == j:
+                total = total + spring
+            pairs[i, j] = pairs[j, i] = jnp.where(at_self, total, -matrix)
+    _, start = rows_of(s)
+    far = pl.ds(pl.multiple_of(start - shift, 32), FAR)
+    image = jnp.zeros((96, NCOL), f32)
+    for j in range(3):
+        stacked = jnp.concatenate([pairs[i, j] for i in range(3)], axis=0)
+        image = image + product(stacked, high[j, far, :], low[j, far, :])
+    return image
+
+
+def dilatation_forces(s, tied, dil_high, dil_low):
+    _, vector, weight, at_self = tied
+    sides = []
+    for i in range(3):
+        matrix = weight * vector[i]
+        total = jnp.sum(matrix, axis=1, keepdims=True)
+        sides.append(-jnp.where(at_self, total, matrix))
+    _, start = rows_of(s)
+    far = pl.ds(start, FAR)
+    return product(jnp.concatenate(sides, axis=0), dil_high[far, :], dil_low[far, :])
+
+
+def inner(
+    rows, left, right, own, high, low, dil_high, dil_low, forces,
+    geo, geo_cols, geo_far, field,
+):
+    locate(own, None, None, geo, geo_cols, geo_far, range(4, 8))
     for c in range(3):
         for y in range(SIDE):
             j, t = divmod(y, 4)
             src = j * 18 + c * 6
             row = GROUP * y
-            field[c, row : row + 16, :] = rows[256 * c + 16 * y : 256 * c + 16 * y + 16, :]
+            point = 256 * c + 16 * y
+            field[c, row : row + 16, :] = rows[point : point + 16, :]
             field[c, row + 16 : row + 22, :] = left[src : src + 6, t * NCOL : (t + 1) * NCOL]
             field[c, row + 22 : row + 28, :] = right[src : src + 6, t * NCOL : (t + 1) * NCOL]
             field[c, row + 28 : row + 32, :] = jnp.zeros((4, NCOL), f32)
         for y in range(SIDE):
             row = GROUP * y
             parts = split(field[c, row : row + 32, :])
-            high[c, 256 + row : 288 + row, :] = parts[0]
-            low[c, 256 + row : 288 + row, :] = parts[1]
+            high[c, row : row + 32, :] = parts[0]
+            low[c, row : row + 32, :] = parts[1]
+
+    def middle(s, carry):
+        at = pl.ds(pl.multiple_of(64 * (s - 4), 64), 64)
+        parts = dilatation(s, geo_cols, geo_far, high, low, 256)
+        dil_high[at, :] = parts[0]
+        dil_low[at, :] = parts[1]
+        tied = own_bonds(s, geo_cols, geo_far)
+        image = bond_forces(s, tied, geo_far, high, low, 256)
+        at = pl.ds(pl.multiple_of(32 * (s - 4), 32), 32)
+        for i in range(3):
+            forces[i, at, :] = image[32 * i : 32 * i + 32]
+        return carry
+
+    lax.fori_loop(4, 8, middle, 0, unroll=2)
+
+
+def stiffness(
+    rows, mass, own, below, above, high_own, low_own, dil_high_own, dil_low_own, forces,
+    result, grams,
+    geo, geo_cols, geo_far, high, low, dil_high, dil_low,
+):
+    locate(own, below, above, geo, geo_cols, geo_far, range(STRIPS))
+    for c in range(3):
+        high[c, 256:768, :] = high_own[c]
+        low[c, 256:768, :] = low_own[c]
         for j in range(HALO):
             for part, first in ((below, 2), (above, 24)):
                 row = GROUP * (first + j)
@@ -195,86 +297,39 @@
         for row in (0, 960):
             for ref in (high, low):
                 ref[c, row : row + 64, :] = jnp.zeros((64, NCOL), bf16)
-
-    row = lax.broadcasted_iota(jnp.int32, (64, FAR), 0)
-    lane = lax.broadcasted_iota(jnp.int32, (64, FAR), 1)
-    at_self = lane == row + 96
-    home_row = row & 31
-
-    def dilatations(s, carry):
-        near = pl.multiple_of(GROUP * (2 * s + 4), 64)
-        start = pl.multiple_of(GROUP * (2 * s + 1), 32)
-        home = geo_cols[pl.ds(near, 64), :]
-        middle, before, after = block_masks(s, home[0:32])
-        vector, weight = bonds(geo_far[s], home)
-        weight = weight * jnp.where(home_row < 16, middle, jnp.where(home_row < 22, before, after))
-        total = jnp.zeros((64, NCOL), f32)
-        for j in range(3):
-            matrix = weight * vector[j]
-            matrix = jnp.where(at_self, -jnp.sum(matrix, axis=1, keepdims=True), matrix)
-            total = total + product(
-                matrix, high[j, pl.ds(start, FAR), :], low[j, pl.ds(start, FAR), :]
-            )
-        parts = split(total * (home[:, 4:5] * (1.0 / 27.0)))
+    dil_high[384:640, :] = dil_high_own[...]
+    dil_low[384:640, :] = dil_low_own[...]
+
+    def ends(i, carry):
+        s = i + 4 * (i // 4)
+        near, _ = rows_of(s)
+        parts = dilatation(s, geo_cols, geo_far, high, low, 0)
         dil_high[pl.ds(near, 64), :] = parts[0]
         dil_low[pl.ds(near, 64), :] = parts[1]
         return carry
 
-    lax.fori_loop(0, STRIPS, dilatations, 0, unroll=6)
-
-    row = lax.broadcasted_iota(jnp.int32, (32, FAR), 0)
-    lane = lax.broadcasted_iota(jnp.int32, (32, FAR), 1)
-    own_self = lane == row + jnp.where(row < 16, 96, 112)
-
-    def forces(s, carry):
-        near = pl.multiple_of(GROUP * (2 * s + 4), 64)
-        start = pl.multiple_of(GROUP * (2 * s + 1), 32)
-        first = geo_cols[pl.ds(near, 32), :]
-        second = geo_cols[pl.ds(near + 32, 16), :]
-        home = jnp.concatenate([first[0:16], second], axis=0)
-        middle, _, _ = block_masks(s, first)
-        far = geo_far[s]
-        vector, weight = bonds(far, home)
-        weight = weight * middle
-        coupling = weight * ((home[:, 3:4] + far[3:4, :]) * (1.0 / 18.0))
-        spring = home[:, 5:6]
-        pairs = {}
-        for i in range(3):
-            side = coupling * vector[i]
-            for j in range(i, 3):
-                matrix = side * vector[j]
-                total = jnp.sum(matrix, axis=1, keepdims=True)
-                if i == j:
-                    total = total + spring
-                pairs[i, j] = pairs[j, i] = jnp.where(own_self, total, -matrix)
-        image = jnp.zeros((96, NCOL), f32)
-        for j in range(3):
-            stacked = jnp.concatenate([pairs[i, j] for i in range(3)], axis=0)
-            image = image + product(
-                stacked, high[j, pl.ds(start, FAR), :], low[j, pl.ds(start, FAR), :]
-            )
-        sides = []
-        for i in range(3):
-            matrix = weight * vector[i]
-            total = jnp.sum(matrix, axis=1, keepdims=True)
-            sides.append(-jnp.where(own_self, total, matrix))
-        image = image + product(
-            jnp.concatenate(sides, axis=0),
-            dil_high[pl.ds(start, FAR), :],
-            dil_low[pl.ds(start, FAR), :],
-        )
-        at = pl.multiple_of(32 * (s - 2), 32)
-        for i in range(3):
-            result[i, pl.ds(at, 32), :] = image[32 * i : 32 * i + 32]
+    lax.fori_loop(0, 8, ends, 0, unroll=4)
+
+    def images(i, carry):
+        tasks = []
+        for s, whole in ((4 + i, False), (2 + i + 4 * (i // 2), True)):
+            tied = own_bonds(s, geo_cols, geo_far)
+            image = dilatation_forces(s, tied, dil_high, dil_low)
+            if whole:
+                image = image + bond_forces(s, tied, geo_far, high, low, 0)
+            else:
+                at = pl.ds(pl.multiple_of(32 * (s - 4), 32), 32)
+                image = image + jnp.concatenate([forces[k, at, :] for k in range(3)], axis=0)
+            tasks.append((s, image))
+        for s, image in tasks:
+            at = pl.multiple_of(32 * (s - 2), 32)
+            for k in range(3):
+                result[pl.ds(pl.multiple_of(at + 256 * k, 32), 32), :] = image[32 * k : 32 * k + 32]
         return carry
 
-    lax.fori_loop(2, 10, forces, 0, unroll=4)
-
-    for c in range(3):
-        for y in range(SIDE):
-            images[c, :, y * NCOL : (y + 1) * NCOL] = result[c, 16 * y : 16 * y + 16, :]
-
-    stiff = gram(rows[...], result[...].reshape(768, NCOL))
+    lax.fori_loop(0, 4, images, 0, unroll=2)
+
+    stiff = gram(rows[...], result[...])
     at_row = lax.broadcasted_iota(jnp.int32, (NCOL, NCOL), 0)
     at_col = lax.broadcasted_iota(jnp.int32, (NCOL, NCOL), 1)
     grams[0:192, :] = jnp.where(at_row >= at_col, mass[...], stiff)
@@ -349,7 +404,7 @@
             ref[row : row + 8, 128:256] = tiles[q][1]
 
 
-def rotation(scale, grams, basis, images, modes, mode_images, reduced, square, work, small, factor):
+def rotation(scale, grams, rows, images, modes, mode_images, reduced, square, work, small, factor):
     packed = grams[0:192, :] * scale
     diagonal = grams[192:193, :] * scale
     square[...] = jnp.zeros((256, 256), f32)
@@ -367,9 +422,9 @@
         reduced_rows = work[base : base + 64, :]
         for other in range(3):
             if other != block:
-                rows = slice(64 * other, 64 * other + 64)
-                work[rows, :] = work[rows, :] - jnp.dot(
-                    work[rows, base : base + 64],
+                part = slice(64 * other, 64 * other + 64)
+                work[part, :] = work[part, :] - jnp.dot(
+                    work[part, base : base + 64],
                     reduced_rows,
                     precision=highest,
                     preferred_element_type=f32,
@@ -380,24 +435,32 @@
     turned = square[...].T[0:64, 0:192]
     small[:, 0:64] = jnp.dot(turned, weighted, precision=highest, preferred_element_type=f32)
     small[:, 64:256] = turned
-    factor[...] = jnp.zeros((128, 384), f32)
 
     def keep(t, caught):
-        value = jnp.concatenate(caught, axis=1)[:, 64:256]
-        factor[8 * t : 8 * t + 8, 0:192] = value
-        factor[64 + 8 * t : 72 + 8 * t, 192:384] = value
+        factor[8 * t : 8 * t + 8, :] = jnp.concatenate(caught, axis=1)[:, 64:256]
 
     reduce_block(small, 0, 0, keep)
-    rotate = factor[0:64, 0:192]
+    rotate = factor[...]
+    blank = jnp.zeros((64, NCOL), f32)
+    even = split(jnp.concatenate([rotate, blank], axis=0))
+    odd = split(jnp.concatenate([blank, rotate], axis=0))
     across = (((1,), (1,)), ((), ()))
+
+    def dot(left, right):
+        return lax.dot_general(left, right, across, preferred_element_type=f32)
+
+    for source, out in ((rows, modes), (images, mode_images)):
+        value = source[...].reshape(24, 2, SIDE, NCOL)
+        total = jnp.zeros((384, 128), f32)
+        for at, (high, low) in ((0, even), (1, odd)):
+            first, second = split(value[:, at].reshape(384, NCOL))
+            total = total + dot(first, high) + dot(first, low) + dot(second, high)
+        for c in range(3):
+            for y in range(SIDE // 2):
+                row = 128 * c + 16 * y
+                out[c, :, 128 * y : 128 * y + 128] = total[row : row + 16]
     lifted = lax.dot_general(stiff, rotate, across, precision=highest, preferred_element_type=f32)
     reduced[...] = jnp.dot(rotate, lifted, precision=highest, preferred_element_type=f32)
-    both = factor[...]
-    for source, out in ((basis, modes), (images, mode_images)):
-        for y in range(SIDE // 2):
-            value = source[:, :, y * 384 : (y + 1) * 384].reshape(48, 384)
-            value = lax.dot_general(value, both, across, precision=highest, preferred_element_type=f32)
-            out[:, :, y * 128 : (y + 1) * 128] = value.reshape(3, SIDE, 128)
 
 
 def exchange(up, down, axis):
@@ -437,21 +500,27 @@
         below, above = exchange(up, down, "band")
 
     with jax.named_scope("stiffness"):
+        rows, mass, left, right, own = [hold(a) for a in (rows, mass, left, right, own)]
+        places = [
+            pltpu.VMEM((8, 1024), f32),
+            pltpu.VMEM((1024, 8), f32),
+            pltpu.VMEM((STRIPS, 8, FAR), f32),
+        ]
+        middle = call(
+            inner,
+            [((3, 512, NCOL), bf16)] * 2 + [((256, NCOL), bf16)] * 2 + [((3, 128, NCOL), f32)],
+            places + [pltpu.VMEM((3, 512, NCOL), f32)],
+            (rows, left, right, own),
+            10**9,
+            "inner",
+        )
         images, grams = call(
             stiffness,
-            [(3, SIDE, SIDE * NCOL), (256, NCOL)],
-            [
-                pltpu.VMEM((8, 1024), f32),
-                pltpu.VMEM((1024, 8), f32),
-                pltpu.VMEM((STRIPS, 8, FAR), f32),
-                pltpu.VMEM((3, 512, NCOL), f32),
-                pltpu.VMEM((3, 1024, NCOL), bf16),
-                pltpu.VMEM((3, 1024, NCOL), bf16),
-                pltpu.VMEM((1024, NCOL), bf16),
-                pltpu.VMEM((1024, NCOL), bf16),
-                pltpu.VMEM((3, 256, NCOL), f32),
-            ],
-            (hold(rows), hold(mass), hold(left), hold(right), hold(own), hold(below), hold(above)),
+            [(768, NCOL), (256, NCOL)],
+            places
+            + [pltpu.VMEM((3, 1024, NCOL), bf16)] * 2
+            + [pltpu.VMEM((1024, NCOL), bf16)] * 2,
+            (rows, mass, own, hold(below), hold(above), *[hold(a) for a in middle]),
             2 * 10**9,
             "stiffness",
         )
@@ -473,9 +542,9 @@
                 pltpu.VMEM((256, 256), f32),
                 pltpu.VMEM((192, 256), f32),
                 pltpu.VMEM((64, 256), f32),
-                pltpu.VMEM((128, 384), f32),
+                pltpu.VMEM((64, NCOL), f32),
             ],
-            (hold(grams), basis, hold(images)),
+            (hold(grams), hold(rows), hold(images)),
             10**9,
             "rotation",
             False,

time: 112 us -> 106 us (0.946)
  waiting for transfers between devices: 12.4 us -> 9.09 us
  Pallas kernels: 23 us -> 21.1 us
    ppermute x4, waiting for transfers between devices: 12.4 us -> 9.09 us  [exchange(): return (lax.ppermute(up, axis, forward), lax.ppermute(down, axis, backward))]
    pallas_call x5 -> x6, Pallas kernels: 23 us -> 21.1 us  [call(): pl.pallas_call(kernel, out_shape=[(pltpu.VMEM if near else jax.ShapeDtype...]
  transfers between devices with their start and end apart: 4 -> 4, of which waited for: 4 -> 3; matrix products, arithmetic and copies ran while one was open for 0% -> 0% of each run, Pallas kernels for 1% -> 4%
where the time goes in v4:
time: 106 us
  blocking collectives  59.4 us (56%)
  Pallas kernels  21.1 us (20%)
  starting transfers between devices  14.4 us (14%)
  waiting for transfers between devices  9.09 us (9%)
  local copies, waits for them, and re-layouts  1.09 us (1%)
    all_to_all x2, blocking collectives, spread(): lax.all_to_all(jnp.broadcast_to(value[None], (size,) + value.shape), axis...  37.7 us
    all_to_all x1, blocking collectives, local(): lax.all_to_all(grams.reshape(slabs, 256 // slabs, NCOL), 'slab', 0, 0, ti...  21.7 us
    pallas_call x6, Pallas kernels, call(): pl.pallas_call(kernel, out_shape=[(pltpu.VMEM if near else jax.ShapeDtype...  21.1 us
    ppermute x4, starting transfers between devices, exchange(): return (lax.ppermute(up, axis, forward), lax.ppermute(down, axis, backward))  14.4 us
    ppermute x4, waiting for transfers between devices, exchange(): return (lax.ppermute(up, axis, forward), lax.ppermute(down, axis, backward))  9.09 us
  transfers between devices with their start and end apart: 4, of which 3 were waited for; matrix products, arithmetic and copies ran while one was open for 0% of the time, Pallas kernels for 4%

profile of v4, /device:TPU:1, one launch (start us, length us, event | category | flops | bytes accessed | tf_op | source)
XLA Modules:
  0.0 105.9 jit_solution(12763022465921343347)
XLA Ops:
  0.6 0.0 copy-start
  0.6 1.1 copy-done
  1.7 1.2 %pack_x.1 = (f32[80,768]{1,0:T(8,128)S(1)}, f32[80,768]{1,0:T(8,128)S(1)}, f32[8,256]{1,0:T(8,128)S(1)}) custom-call(f32[3,16,3072]{2,1,0:T(8,128)S(1)} %copy-done, f32[3,16,16]{2,1,0:T(8,128)} %offsets.1, f32[16,16]{1,0:T(8,128)} %bond.1, f32[16,16]{1,0:T(8,128)} %bulk.1, f32[16,16]{1,0:T(8,128)} %springs.1, s32[1,2,9]{2,1,0:T(2,128)} %intact.1), custom_call_target="tpu_custom_call" | custom-call | flops 1000 | bytes 596040 | tf_op jit(solution)/shard_map/halo/pack_x/pallas_call | solution.py:31
  2.9 4.0 %collective-permute-start = (f32[80,768]{1,0:T(8,128)S(1)}, f32[80,768]{1,0:T(8,128)S(1)}, u32[]{:S(2)}, u32[]{:S(2)}) collective-permute-start(f32[80,768]{1,0:T(8,128)S(1)} %get-tuple-element.21), channel_id=1, source_target_pairs={{0,16},{16,32},{32,48},{48,64},{64,80},{80,96},{96,112},{112,128},... | collective-permute-start | bytes 737288 | tf_op jit(solution)/shard_map/halo/ppermute | solution.py:470
  6.9 1.3 %collective-permute-start.1 = (f32[80,768]{1,0:T(8,128)S(1)}, f32[80,768]{1,0:T(8,128)S(1)}, u32[]{:S(2)}, u32[]{:S(2)}) collective-permute-start(f32[80,768]{1,0:T(8,128)S(1)} %get-tuple-element.22), channel_id=1, source_target_pairs={{16,0},{32,16},{48,32},{64,48},{80,64},{96,80},{112,96},{128,112},... | collective-permute-start | bytes 737288 | tf_op jit(solution)/shard_map/halo/ppermute | solution.py:470
  8.2 1.8 %collective-permute-done.left = f32[80,768]{1,0:T(8,128)S(1)} collective-permute-done((f32[80,768]{1,0:T(8,128)S(1)}, f32[80,768]{1,0:T(8,128)S(1)}, u32[]{:S(2)}, u32[]{:S(2)}) %collective-permute-start) | collective-permute-done | bytes 245792 | tf_op jit(solution)/shard_map/halo/ppermute | solution.py:470
  10.0 3.8 %collective-permute-done.1.right = f32[80,768]{1,0:T(8,128)S(1)} collective-permute-done((f32[80,768]{1,0:T(8,128)S(1)}, f32[80,768]{1,0:T(8,128)S(1)}, u32[]{:S(2)}, u32[]{:S(2)}) %collective-permute-start.1) | collective-permute-done | bytes 245792 | tf_op jit(solution)/shard_map/halo/ppermute | solution.py:470
  13.8 0.2 pack_y.1
  14.0 7.2 %collective-permute-start.2 = (f32[96,1152]{1,0:T(8,128)S(1)}, f32[96,1152]{1,0:T(8,128)S(1)}, u32[]{:S(2)}, u32[]{:S(2)}) collective-permute-start(f32[96,1152]{1,0:T(8,128)S(1)} %get-tuple-element.24), channel_id=1, source_target_pairs={{0,1},{1,2},{2,3},{3,4},{4,5},{5,6},{6,7},{7,8},{8,9},{9,10},{10,1... | collective-permute-start | bytes 1327112 | tf_op jit(solution)/shard_map/halo/ppermute | solution.py:470
  21.2 1.9 %collective-permute-start.3 = (f32[96,1152]{1,0:T(8,128)S(1)}, f32[96,1152]{1,0:T(8,128)S(1)}, u32[]{:S(2)}, u32[]{:S(2)}) collective-permute-start(f32[96,1152]{1,0:T(8,128)S(1)} %get-tuple-element.25), channel_id=1, source_target_pairs={{1,0},{2,1},{3,2},{4,3},{5,4},{6,5},{7,6},{8,7},{9,8},{10,9},{11,1... | collective-permute-start | bytes 1327112 | tf_op jit(solution)/shard_map/halo/ppermute | solution.py:470
  23.1 0.9 prepare.1
  24.1 3.3 %inner.1 = (bf16[3,512,192]{2,1,0:T(8,128)(2,1)S(1)}, bf16[3,512,192]{2,1,0:T(8,128)(2,1)S(1)}, bf16[256,192]{1,0:T(8,128)(2,1)S(1)}, bf16[256,192]{1,0:T(8,128)(2,1)S(1)}, f32[3,128,192]{2,1,0:T(8,128)S(1)}) custom-call(f32[768,192]{1,0:T(8,128)S(1)} %get-tuple-element.18.rows.refs_1_, f32[80,768]{1,0:T(8,128)S(1)} %collective-permute-done.left, ...), custom_call_target="tpu_custom_call" | custom-call | flops 1000000000 | bytes 1097728 | tf_op jit(solution)/shard_map/stiffness/inner/pallas_call | solution.py:31
  27.4 0.0 collective-permute-done.2.below
  27.4 3.4 %collective-permute-done.3.above = f32[96,1152]{1,0:T(8,128)S(1)} collective-permute-done((f32[96,1152]{1,0:T(8,128)S(1)}, f32[96,1152]{1,0:T(8,128)S(1)}, u32[]{:S(2)}, u32[]{:S(2)}) %collective-permute-start.3) | collective-permute-done | bytes 442400 | tf_op jit(solution)/shard_map/halo/ppermute | solution.py:470
  30.8 5.8 %stiffness.1 = (f32[768,192]{1,0:T(8,128)S(1)}, f32[256,192]{1,0:T(8,128)S(1)}) custom-call(f32[768,192]{1,0:T(8,128)S(1)} %get-tuple-element.18.rows.refs_1_, f32[192,192]{1,0:T(8,128)S(1)} %get-tuple-element.19.mass, f32[8,512]{1,0:T(8,128)S(1)} %get-tuple-element.23.own, f32[96,1152]{1,0:T(8,128)S(1)} %collective-permute-done.2.below, ...), custom_call_target="tpu_custom_call" | custom-call | flops 2000000000 | bytes 4685824 | tf_op jit(solution)/shard_map/stiffness/stiffness/pallas_call | solution.py:31
  36.6 21.7 %all_to_all.15 = f32[32,8,192]{2,1,0:T(8,128)S(1)} all-to-all(f32[32,8,192]{2,1,0:T(8,128)S(1)} %bitcast.2), channel_id=1, replica_groups=mesh['slab'=32,'band'=16] {'slab'}, dimensions={0} | all-to-all | bytes 393216 | tf_op jit(solution)/shard_map/sums/all_to_all | solution.py:529
  58.4 22.1 %all_to_all.16 = f32[16,8,192]{2,1,0:T(8,128)S(1)} all-to-all(f32[16,8,192]{2,1,0:T(8,128)S(1)} %broadcast_in_dim.4), channel_id=1, replica_groups=mesh['slab'=32,'band'=16] {'band'}, dimensions={0} | all-to-all | bytes 196608 | tf_op jit(solution)/shard_map/sums/all_to_all | solution.py:475
  80.6 15.6 %all_to_all.17 = f32[32,8,192]{2,1,0:T(8,128)S(1)} all-to-all(f32[32,8,192]{2,1,0:T(8,128)S(1)} %broadcast_in_dim.5), channel_id=1, replica_groups=mesh['slab'=32,'band'=16] {'slab'}, dimensions={0} | all-to-all | bytes 393216 | tf_op jit(solution)/shard_map/sums/all_to_all | solution.py:475
  96.1 9.7 %rotation.1 = (f32[3,16,1024]{2,1,0:T(8,128)}, f32[3,16,1024]{2,1,0:T(8,128)}, f32[64,64]{1,0:T(8,128)}) custom-call(f32[256,192]{1,0:T(8,128)S(1)} %bitcast.3, f32[768,192]{1,0:T(8,128)S(1)} %get-tuple-element.18.rows.refs_1_, f32[768,192]{1,0:T(8,128)S(1)} %get-tuple-element.32.refs_2_), custom_call_target="tpu_custom_call" | custom-call | flops 1000000000 | bytes 1376256 | tf_op jit(solution)/shard_map/rotation/rotation/pallas_call | solution.py:31
  (4 shorter events, 0.1 us)
Async XLA Ops:
  0.6 1.1 %copy-start = (f32[3,16,3072]{2,1,0:T(8,128)S(1)}, f32[3,16,3072]{2,1,0:T(8,128)}, u32[]{:S(2)}) copy-start(f32[3,16,3072]{2,1,0:T(8,128)} %basis.5) | copy-start | bytes 1769476
  2.9 7.1 %collective-permute-start = (f32[80,768]{1,0:T(8,128)S(1)}, f32[80,768]{1,0:T(8,128)S(1)}, u32[]{:S(2)}, u32[]{:S(2)}) collective-permute-start(f32[80,768]{1,0:T(8,128)S(1)} %get-tuple-element.21), channel_id=1, source_target_pairs={{0,16},{16,32},{32,48},{48,64},{64,80},{80,96},{96,112},{112,128},... | collective-permute-start | bytes 737288 | tf_op jit(solution)/shard_map/halo/ppermute | solution.py:470
  6.9 6.9 %collective-permute-start.1 = (f32[80,768]{1,0:T(8,128)S(1)}, f32[80,768]{1,0:T(8,128)S(1)}, u32[]{:S(2)}, u32[]{:S(2)}) collective-permute-start(f32[80,768]{1,0:T(8,128)S(1)} %get-tuple-element.22), channel_id=1, source_target_pairs={{16,0},{32,16},{48,32},{64,48},{80,64},{96,80},{112,96},{128,112},... | collective-permute-start | bytes 737288 | tf_op jit(solution)/shard_map/halo/ppermute | solution.py:470
  14.0 13.4 %collective-permute-start.2 = (f32[96,1152]{1,0:T(8,128)S(1)}, f32[96,1152]{1,0:T(8,128)S(1)}, u32[]{:S(2)}, u32[]{:S(2)}) collective-permute-start(f32[96,1152]{1,0:T(8,128)S(1)} %get-tuple-element.24), channel_id=1, source_target_pairs={{0,1},{1,2},{2,3},{3,4},{4,5},{5,6},{6,7},{7,8},{8,9},{9,10},{10,1... | collective-permute-start | bytes 1327112 | tf_op jit(solution)/shard_map/halo/ppermute | solution.py:470
  21.2 9.6 %collective-permute-start.3 = (f32[96,1152]{1,0:T(8,128)S(1)}, f32[96,1152]{1,0:T(8,128)S(1)}, u32[]{:S(2)}, u32[]{:S(2)}) collective-permute-start(f32[96,1152]{1,0:T(8,128)S(1)} %get-tuple-element.25), channel_id=1, source_target_pairs={{1,0},{2,1},{3,2},{4,3},{5,4},{6,5},{7,6},{8,7},{9,8},{10,9},{11,1... | collective-permute-start | bytes 1327112 | tf_op jit(solution)/shard_map/halo/ppermute | solution.py:470

commit v5 on v4

--- a/solution.py
+++ b/solution.py
@@ -11,6 +11,7 @@
 SIDE = 16
 HALO = 6
 GROUP = 32
+RING = 28
 STRIPS = 12
 FAR = 256
 highest = lax.Precision.HIGHEST
@@ -65,11 +66,11 @@
             geo[row : row + 1, 128 * by : 128 * by + 128] = pattern
     for out, first in ((up, SIDE - HALO), (down, 0)):
         for c in range(3):
-            for j in range(4):
+            for j in range(8):
                 row = j * 18 + c * 6
-                out[row : row + 6, :] = basis[c, first : first + 6, j * 768 : (j + 1) * 768]
-        out[72:80, :] = jnp.zeros((8, 768), f32)
-        out[72:80, 0:256] = geo[...]
+                out[row : row + 6, :] = basis[c, first : first + 6, j * 384 : (j + 1) * 384]
+        out[144:152, 0:256] = geo[...]
+        out[144:152, 256:384] = jnp.zeros((8, 128), f32)
 
 
 def pack_y(basis, geo, left, right, up, down, own):
@@ -77,22 +78,21 @@
     for y in range(SIDE):
         at = GROUP * y
         own[:, at : at + 16] = geo[:, 16 * y : 16 * y + 16]
-        own[:, at + 16 : at + 22] = left[72:80, 16 * y + 10 : 16 * y + 16]
-        own[:, at + 22 : at + 28] = right[72:80, 16 * y : 16 * y + 6]
+        own[:, at + 16 : at + 22] = left[144:152, 16 * y + 10 : 16 * y + 16]
+        own[:, at + 22 : at + 28] = right[144:152, 16 * y : 16 * y + 6]
     for out, first in ((up, SIDE - HALO), (down, 0)):
-        pieces = ((2, 384, 768, 0), (3, 0, 768, 384)) if first else ((0, 0, 768, 0), (1, 0, 384, 768))
         for c in range(3):
-            row = GROUP * c
+            row = RING * c
             out[row : row + 16, :] = basis[c, :, first * NCOL : (first + HALO) * NCOL]
-            for j, start, stop, lane in pieces:
-                src = j * 18 + c * 6
-                width = stop - start
-                out[row + 16 : row + 22, lane : lane + width] = left[src : src + 6, start:stop]
-                out[row + 22 : row + 28, lane : lane + width] = right[src : src + 6, start:stop]
-            out[row + 28 : row + 32, :] = jnp.zeros((4, 1152), f32)
+            for j in range(HALO // 2):
+                src = (first // 2 + j) * 18 + c * 6
+                lanes = slice(384 * j, 384 * j + 384)
+                out[row + 16 : row + 22, lanes] = left[src : src + 6, :]
+                out[row + 22 : row + 28, lanes] = right[src : src + 6, :]
         lanes = slice(first * GROUP, (first + HALO) * GROUP)
-        out[28:32, 0:192] = own[0:4, lanes]
-        out[60:64, 0:192] = own[4:8, lanes]
+        out[84:88, :] = jnp.zeros((4, 1152), f32)
+        out[84:88, 0:192] = own[0:4, lanes]
+        out[84:88, 256:448] = own[4:8, lanes]
 
 
 def split(value):
@@ -156,8 +156,8 @@
     geo[:, 256:768] = own[...]
     for part, lane in ((below, 64), (above, 768)):
         if part is not None:
-            geo[0:4, lane : lane + 192] = part[28:32, 0:192]
-            geo[4:8, lane : lane + 192] = part[60:64, 0:192]
+            geo[0:4, lane : lane + 192] = part[84:88, 0:192]
+            geo[4:8, lane : lane + 192] = part[84:88, 256:448]
     lane = lax.broadcasted_iota(jnp.int32, (8, 1024), 1)
     channel = lax.broadcasted_iota(jnp.int32, (8, 1024), 0)
     xi = lane & 31
@@ -250,7 +250,7 @@
     locate(own, None, None, geo, geo_cols, geo_far, range(4, 8))
     for c in range(3):
         for y in range(SIDE):
-            j, t = divmod(y, 4)
+            j, t = divmod(y, 2)
             src = j * 18 + c * 6
             row = GROUP * y
             point = 256 * c + 16 * y
@@ -291,7 +291,7 @@
         for j in range(HALO):
             for part, first in ((below, 2), (above, 24)):
                 row = GROUP * (first + j)
-                parts = split(part[GROUP * c : GROUP * (c + 1), j * NCOL : (j + 1) * NCOL])
+                parts = split(part[RING * c : RING * c + GROUP, j * NCOL : (j + 1) * NCOL])
                 high[c, row : row + 32, :] = parts[0]
                 low[c, row : row + 32, :] = parts[1]
         for row in (0, 960):
@@ -332,14 +332,18 @@
     stiff = gram(rows[...], result[...])
     at_row = lax.broadcasted_iota(jnp.int32, (NCOL, NCOL), 0)
     at_col = lax.broadcasted_iota(jnp.int32, (NCOL, NCOL), 1)
-    grams[0:192, :] = jnp.where(at_row >= at_col, mass[...], stiff)
+    packed = jnp.where(at_row >= at_col, mass[...], stiff)
     diagonal = jnp.sum(jnp.where(at_row == at_col, stiff, 0.0), axis=0, keepdims=True)
-    grams[192:200, :] = jnp.broadcast_to(diagonal, (8, NCOL))
-    grams[200:256, :] = jnp.zeros((56, NCOL), f32)
+    grams[0:192, :] = packed[:, 0:128]
+    grams[192:288, 0:64] = packed[0:96, 128:192]
+    grams[192:288, 64:128] = packed[96:192, 128:192]
+    grams[288:320, :] = jnp.zeros((32, 128), f32)
+    grams[288:289, :] = diagonal[:, 0:128]
+    grams[289:290, 0:64] = diagonal[:, 128:192]
 
 
 def lanes_of(tile, column):
-    half = tile[column // 128]
+    half = tile[column // 128 - 2 + len(tile)]
     at = column % 128
     return jnp.broadcast_to(half[:, at : at + 1], (8, 128))
 
@@ -348,12 +352,12 @@
     return jnp.broadcast_to(value[row : row + 1, :], (8, 128))
 
 
-def reduce_block(ref, row0, col0, out):
+def reduce_block(ref, row0, col0, halves, out):
     at = lax.broadcasted_iota(jnp.int32, (8, 128), 0)
     tiles = []
     for q in range(8):
         row = row0 + 8 * q
-        tiles.append([ref[row : row + 8, 0:128], ref[row : row + 8, 128:256]])
+        tiles.append([ref[row : row + 8, 128 * h : 128 * h + 128] for h in halves])
     pivots = [lanes_of(tiles[0], col0 + j) for j in range(8)]
     for t in range(8):
         first = col0 + 8 * t
@@ -370,12 +374,11 @@
         for i in range(8):
             pivot = row_of(pivots[i], i)
             inverse = 1.0 / pivot
-            factor = pivots[i]
             chosen = at == i
+            factor = jnp.where(chosen, -inverse, pivots[i] * inverse)
 
             def step(value):
-                row = row_of(value, i) * inverse
-                return jnp.where(chosen, row, value - factor * row)
+                return jnp.where(chosen, 0.0, value) - factor * row_of(value, i)
 
             if out is not None:
                 root = lax.rsqrt(pivot)
@@ -400,15 +403,17 @@
     if out is None:
         for q in range(8):
             row = row0 + 8 * q
-            ref[row : row + 8, 0:128] = tiles[q][0]
-            ref[row : row + 8, 128:256] = tiles[q][1]
+            for h, value in zip(halves, tiles[q]):
+                ref[row : row + 8, 128 * h : 128 * h + 128] = value
 
 
 def rotation(scale, grams, rows, images, modes, mode_images, reduced, square, work, small, factor):
-    packed = grams[0:192, :] * scale
-    diagonal = grams[192:193, :] * scale
     square[...] = jnp.zeros((256, 256), f32)
-    square[0:192, 0:192] = packed
+    square[0:192, 0:128] = grams[0:192, :] * scale
+    square[0:96, 128:192] = grams[192:288, 0:64] * scale
+    square[96:192, 128:192] = grams[192:288, 64:128] * scale
+    packed = square[0:192, 0:192]
+    diagonal = jnp.concatenate([grams[288:289, :], grams[289:290, 0:64]], axis=1) * scale
     flipped = square[...].T[0:192, 0:192]
     at_row = lax.broadcasted_iota(jnp.int32, (NCOL, NCOL), 0)
     at_col = lax.broadcasted_iota(jnp.int32, (NCOL, NCOL), 1)
@@ -418,17 +423,18 @@
     work[:, 192:256] = mass[:, 0:64]
     for block in range(3):
         base = 64 * block
-        reduce_block(work, base, base, None)
-        reduced_rows = work[base : base + 64, :]
-        for other in range(3):
-            if other != block:
-                part = slice(64 * other, 64 * other + 64)
-                work[part, :] = work[part, :] - jnp.dot(
-                    work[part, base : base + 64],
-                    reduced_rows,
-                    precision=highest,
-                    preferred_element_type=f32,
-                )
+        halves = (1,) if block == 2 else (0, 1)
+        lanes = slice(128 * halves[0], 256)
+        reduce_block(work, base, base, halves, None)
+        rest = [slice(64 * other, 64 * other + 64) for other in range(3) if other != block]
+        change = jnp.dot(
+            jnp.concatenate([work[part, base : base + 64] for part in rest], axis=0),
+            work[base : base + 64, lanes],
+            precision=highest,
+            preferred_element_type=f32,
+        )
+        work[rest[0], lanes] = work[rest[0], lanes] - change[0:64]
+        work[rest[1], lanes] = work[rest[1], lanes] - change[64:128]
     solved = work[:, 192:256]
     weighted = jnp.dot(mass, solved, precision=highest, preferred_element_type=f32)
     square[0:192, 0:64] = solved
@@ -439,7 +445,7 @@
     def keep(t, caught):
         factor[8 * t : 8 * t + 8, :] = jnp.concatenate(caught, axis=1)[:, 64:256]
 
-    reduce_block(small, 0, 0, keep)
+    reduce_block(small, 0, 0, (0, 1), keep)
     rotate = factor[...]
     blank = jnp.zeros((64, NCOL), f32)
     even = split(jnp.concatenate([rotate, blank], axis=0))
@@ -479,12 +485,11 @@
     slabs = lax.axis_size("slab")
     bands = lax.axis_size("band")
     total_rows = float(3 * SIDE * SIDE * slabs * bands)
-    basis = hold(basis)
 
     with jax.named_scope("halo"):
         up, down, geo = call(
             pack_x,
-            [(80, 768)] * 2 + [(8, 256)],
+            [(152, 384)] * 2 + [(8, 256)],
             [pltpu.VMEM((128, 128), f32)] * 2,
             (basis, offsets, bond_modulus, bulk_modulus, springs, intact),
             1000,
@@ -492,10 +497,10 @@
         )
         left, right = exchange(up, down, "slab")
         rows, mass = call(
-            prepare, [(768, NCOL), (NCOL, NCOL)], [], (basis,), 3 * 10**8, "prepare"
+            prepare, [(768, NCOL), (NCOL, NCOL)], [], (hold(basis),), 3 * 10**8, "prepare"
         )
         up, down, own = call(
-            pack_y, [(96, 1152)] * 2 + [(8, 512)], [], (basis, hold(geo), hold(left), hold(right)), 1000, "pack_y"
+            pack_y, [(88, 1152)] * 2 + [(8, 512)], [], (hold(basis), hold(geo), hold(left), hold(right)), 1000, "pack_y"
         )
         below, above = exchange(up, down, "band")
 
@@ -516,7 +521,7 @@
         )
         images, grams = call(
             stiffness,
-            [(768, NCOL), (256, NCOL)],
+            [(768, NCOL), (320, 128)],
             places
             + [pltpu.VMEM((3, 1024, NCOL), bf16)] * 2
             + [pltpu.VMEM((1024, NCOL), bf16)] * 2,
@@ -526,10 +531,10 @@
         )
 
     with jax.named_scope("sums"):
-        part = lax.all_to_all(grams.reshape(slabs, 256 // slabs, NCOL), "slab", 0, 0, tiled=True)
+        part = lax.all_to_all(grams.reshape(slabs, 1, 40960 // slabs), "slab", 0, 0, tiled=True)
         part = spread(jnp.sum(part, axis=0), "band")
         part = spread(jnp.sum(part, axis=0), "slab")
-        grams = part.reshape(256, NCOL)
+        grams = part.reshape(320, 128)
 
     with jax.named_scope("rotation"):
         def kernel(*refs):

time: 106 us -> 99.8 us (0.942)
  blocking collectives: 59.4 us -> 54.1 us
    all_to_all x2, blocking collectives: 37.7 us -> 33 us  [spread(): lax.all_to_all(jnp.broadcast_to(value[None], (size,) + value.shape), axis...]
where the time goes in v5:
time: 99.8 us; the launch traced here: 99.5 us
  blocking collectives  54.1 us (54%)
  Pallas kernels  21.5 us (22%)
  starting transfers between devices  14.2 us (14%)
  waiting for transfers between devices  8.55 us (9%)
    all_to_all x2, blocking collectives, spread(): lax.all_to_all(jnp.broadcast_to(value[None], (size,) + value.shape), axis...  33 us
    pallas_call x6, Pallas kernels, call(): pl.pallas_call(kernel, out_shape=[(pltpu.VMEM if near else jax.ShapeDtype...  21.5 us
    all_to_all x1, blocking collectives, local(): lax.all_to_all(grams.reshape(slabs, 1, 40960 // slabs), 'slab', 0, 0, til...  21.1 us
    ppermute x4, starting transfers between devices, exchange(): return (lax.ppermute(up, axis, forward), lax.ppermute(down, axis, backward))  14.2 us
    ppermute x4, waiting for transfers between devices, exchange(): return (lax.ppermute(up, axis, forward), lax.ppermute(down, axis, backward))  8.55 us
  transfers between devices with their start and end apart: 4, of which 3 were waited for; matrix products, arithmetic and copies ran while one was open for 0% of the time, Pallas kernels for 4%

profile of v5, /device:TPU:1, one launch (start us, length us, event | category | flops | bytes accessed | tf_op | source)
XLA Modules:
  0.0 99.5 jit_solution(10604306329490349697)
XLA Ops:
  0.6 0.0 copy-start
  0.6 1.6 %pack_x.1 = (f32[152,384]{1,0:T(8,128)S(1)}, f32[152,384]{1,0:T(8,128)S(1)}, f32[8,256]{1,0:T(8,128)S(1)}) custom-call(f32[3,16,3072]{2,1,0:T(8,128)} %basis.5, f32[3,16,16]{2,1,0:T(8,128)} %offsets.1, f32[16,16]{1,0:T(8,128)} %bond.1, f32[16,16]{1,0:T(8,128)} %bulk.1, f32[16,16]{1,0:T(8,128)} %springs.1, s32[1,2,9]{2,1,0:T(2,128)} %intact.1), custom_call_target="tpu_custom_call" | custom-call | flops 1000 | bytes 596040 | tf_op jit(solution)/shard_map/halo/pack_x/pallas_call | solution.py:32
  2.2 4.0 %collective-permute-start = (f32[152,384]{1,0:T(8,128)S(1)}, f32[152,384]{1,0:T(8,128)S(1)}, u32[]{:S(2)}, u32[]{:S(2)}) collective-permute-start(f32[152,384]{1,0:T(8,128)S(1)} %get-tuple-element.21), channel_id=1, source_target_pairs={{0,16},{16,32},{32,48},{48,64},{64,80},{80,96},{96,112},{112,128},... | collective-permute-start | bytes 700424 | tf_op jit(solution)/shard_map/halo/ppermute | solution.py:476
  6.2 1.3 %collective-permute-start.1 = (f32[152,384]{1,0:T(8,128)S(1)}, f32[152,384]{1,0:T(8,128)S(1)}, u32[]{:S(2)}, u32[]{:S(2)}) collective-permute-start(f32[152,384]{1,0:T(8,128)S(1)} %get-tuple-element.22), channel_id=1, source_target_pairs={{16,0},{32,16},{48,32},{64,48},{80,64},{96,80},{112,96},{128,112},... | collective-permute-start | bytes 700424 | tf_op jit(solution)/shard_map/halo/ppermute | solution.py:476
  7.5 1.7 %collective-permute-done.left = f32[152,384]{1,0:T(8,128)S(1)} collective-permute-done((f32[152,384]{1,0:T(8,128)S(1)}, f32[152,384]{1,0:T(8,128)S(1)}, u32[]{:S(2)}, u32[]{:S(2)}) %collective-permute-start) | collective-permute-done | bytes 233504 | tf_op jit(solution)/shard_map/halo/ppermute | solution.py:476
  9.2 3.8 %collective-permute-done.1.right = f32[152,384]{1,0:T(8,128)S(1)} collective-permute-done((f32[152,384]{1,0:T(8,128)S(1)}, f32[152,384]{1,0:T(8,128)S(1)}, u32[]{:S(2)}, u32[]{:S(2)}) %collective-permute-start.1) | collective-permute-done | bytes 233504 | tf_op jit(solution)/shard_map/halo/ppermute | solution.py:476
  13.0 0.0 copy-done
  13.0 0.2 pack_y.1
  13.2 7.1 %collective-permute-start.2 = (f32[88,1152]{1,0:T(8,128)S(1)}, f32[88,1152]{1,0:T(8,128)S(1)}, u32[]{:S(2)}, u32[]{:S(2)}) collective-permute-start(f32[88,1152]{1,0:T(8,128)S(1)} %get-tuple-element.24), channel_id=1, source_target_pairs={{0,1},{1,2},{2,3},{3,4},{4,5},{5,6},{6,7},{7,8},{8,9},{9,10},{10,1... | collective-permute-start | bytes 1216520 | tf_op jit(solution)/shard_map/halo/ppermute | solution.py:476
  20.3 1.9 %collective-permute-start.3 = (f32[88,1152]{1,0:T(8,128)S(1)}, f32[88,1152]{1,0:T(8,128)S(1)}, u32[]{:S(2)}, u32[]{:S(2)}) collective-permute-start(f32[88,1152]{1,0:T(8,128)S(1)} %get-tuple-element.25), channel_id=1, source_target_pairs={{1,0},{2,1},{3,2},{4,3},{5,4},{6,5},{7,6},{8,7},{9,8},{10,9},{11,1... | collective-permute-start | bytes 1216520 | tf_op jit(solution)/shard_map/halo/ppermute | solution.py:476
  22.2 0.9 prepare.1
  23.1 3.3 %inner.1 = (bf16[3,512,192]{2,1,0:T(8,128)(2,1)S(1)}, bf16[3,512,192]{2,1,0:T(8,128)(2,1)S(1)}, bf16[256,192]{1,0:T(8,128)(2,1)S(1)}, bf16[256,192]{1,0:T(8,128)(2,1)S(1)}, f32[3,128,192]{2,1,0:T(8,128)S(1)}) custom-call(f32[768,192]{1,0:T(8,128)S(1)} %get-tuple-element.18.rows.refs_1_, f32[152,384]{1,0:T(8,128)S(1)} %collective-permute-done.left, ...), custom_call_target="tpu_custom_call" | custom-call | flops 1000000000 | bytes 1073152 | tf_op jit(solution)/shard_map/stiffness/inner/pallas_call | solution.py:32
  26.5 0.0 collective-permute-done.2.below
  26.5 3.0 %collective-permute-done.3.above = f32[88,1152]{1,0:T(8,128)S(1)} collective-permute-done((f32[88,1152]{1,0:T(8,128)S(1)}, f32[88,1152]{1,0:T(8,128)S(1)}, u32[]{:S(2)}, u32[]{:S(2)}) %collective-permute-start.3) | collective-permute-done | bytes 405536 | tf_op jit(solution)/shard_map/halo/ppermute | solution.py:476
  29.5 5.9 %stiffness.1 = (f32[768,192]{1,0:T(8,128)S(1)}, f32[320,128]{1,0:T(8,128)S(1)}) custom-call(f32[768,192]{1,0:T(8,128)S(1)} %get-tuple-element.18.rows.refs_1_, f32[192,192]{1,0:T(8,128)S(1)} %get-tuple-element.19.mass, f32[8,512]{1,0:T(8,128)S(1)} %get-tuple-element.23.own, f32[88,1152]{1,0:T(8,128)S(1)} %collective-permute-done.2.below, ...), custom_call_target="tpu_custom_call" | custom-call | flops 2000000000 | bytes 4612096 | tf_op jit(solution)/shard_map/stiffness/stiffness/pallas_call | solution.py:32
  35.4 21.1 %all_to_all.15 = f32[32,1,1280]{2,1,0:T(1,128)S(1)} all-to-all(f32[32,1,1280]{2,1,0:T(1,128)S(1)} %bitcast.2), channel_id=1, replica_groups=mesh['slab'=32,'band'=16] {'slab'}, dimensions={0} | all-to-all | bytes 327680 | tf_op jit(solution)/shard_map/sums/all_to_all | solution.py:534
  56.5 0.1 reduce_sum.18
  56.7 19.8 %all_to_all.16 = f32[16,1,1280]{2,1,0:T(1,128)S(1)} all-to-all(f32[16,1,1280]{2,1,0:T(1,128)S(1)} %broadcast_in_dim.4), channel_id=1, replica_groups=mesh['slab'=32,'band'=16] {'band'}, dimensions={0} | all-to-all | bytes 163840 | tf_op jit(solution)/shard_map/sums/all_to_all | solution.py:481
  76.4 0.1 reduce_sum.19
  76.5 0.1 broadcast_in_dim.5
  76.6 13.2 %all_to_all.17 = f32[32,1,1280]{2,1,0:T(1,128)S(1)} all-to-all(f32[32,1,1280]{2,1,0:T(1,128)S(1)} %broadcast_in_dim.5), channel_id=1, replica_groups=mesh['slab'=32,'band'=16] {'slab'}, dimensions={0} | all-to-all | bytes 327680 | tf_op jit(solution)/shard_map/sums/all_to_all | solution.py:481
  89.9 9.6 %rotation.1 = (f32[3,16,1024]{2,1,0:T(8,128)}, f32[3,16,1024]{2,1,0:T(8,128)}, f32[64,64]{1,0:T(8,128)}) custom-call(f32[320,128]{1,0:T(8,128)S(1)} %bitcast.3, f32[768,192]{1,0:T(8,128)S(1)} %get-tuple-element.18.rows.refs_1_, f32[768,192]{1,0:T(8,128)S(1)} %get-tuple-element.32.refs_2_), custom_call_target="tpu_custom_call" | custom-call | flops 1000000000 | bytes 1343488 | tf_op jit(solution)/shard_map/rotation/rotation/pallas_call | solution.py:32
  (1 shorter events, 0.0 us)
Async XLA Ops:
  0.6 12.4 %copy-start = (f32[3,16,3072]{2,1,0:T(8,128)S(1)}, f32[3,16,3072]{2,1,0:T(8,128)}, u32[]{:S(2)}) copy-start(f32[3,16,3072]{2,1,0:T(8,128)} %basis.5) | copy-start | bytes 1769476
  2.2 6.9 %collective-permute-start = (f32[152,384]{1,0:T(8,128)S(1)}, f32[152,384]{1,0:T(8,128)S(1)}, u32[]{:S(2)}, u32[]{:S(2)}) collective-permute-start(f32[152,384]{1,0:T(8,128)S(1)} %get-tuple-element.21), channel_id=1, source_target_pairs={{0,16},{16,32},{32,48},{48,64},{64,80},{80,96},{96,112},{112,128},... | collective-permute-start | bytes 700424 | tf_op jit(solution)/shard_map/halo/ppermute | solution.py:476
  6.2 6.8 %collective-permute-start.1 = (f32[152,384]{1,0:T(8,128)S(1)}, f32[152,384]{1,0:T(8,128)S(1)}, u32[]{:S(2)}, u32[]{:S(2)}) collective-permute-start(f32[152,384]{1,0:T(8,128)S(1)} %get-tuple-element.22), channel_id=1, source_target_pairs={{16,0},{32,16},{48,32},{64,48},{80,64},{96,80},{112,96},{128,112},... | collective-permute-start | bytes 700424 | tf_op jit(solution)/shard_map/halo/ppermute | solution.py:476
  13.2 13.3 %collective-permute-start.2 = (f32[88,1152]{1,0:T(8,128)S(1)}, f32[88,1152]{1,0:T(8,128)S(1)}, u32[]{:S(2)}, u32[]{:S(2)}) collective-permute-start(f32[88,1152]{1,0:T(8,128)S(1)} %get-tuple-element.24), channel_id=1, source_target_pairs={{0,1},{1,2},{2,3},{3,4},{4,5},{5,6},{6,7},{7,8},{8,9},{9,10},{10,1... | collective-permute-start | bytes 1216520 | tf_op jit(solution)/shard_map/halo/ppermute | solution.py:476
  20.3 9.2 %collective-permute-start.3 = (f32[88,1152]{1,0:T(8,128)S(1)}, f32[88,1152]{1,0:T(8,128)S(1)}, u32[]{:S(2)}, u32[]{:S(2)}) collective-permute-start(f32[88,1152]{1,0:T(8,128)S(1)} %get-tuple-element.25), channel_id=1, source_target_pairs={{1,0},{2,1},{3,2},{4,3},{5,4},{6,5},{7,6},{8,7},{9,8},{10,9},{11,1... | collective-permute-start | bytes 1216520 | tf_op jit(solution)/shard_map/halo/ppermute | solution.py:476

commit v6 on v5

--- a/solution.py
+++ b/solution.py
@@ -14,7 +14,6 @@
 RING = 28
 STRIPS = 12
 FAR = 256
-highest = lax.Precision.HIGHEST
 f32 = jnp.float32
 bf16 = jnp.bfloat16
 
@@ -101,27 +100,47 @@
 
 
 def product(left, right_high, right_low):
-    high, low = split(left)
-    return (
-        jnp.dot(high, right_high, preferred_element_type=f32)
-        + jnp.dot(high, right_low, preferred_element_type=f32)
-        + jnp.dot(low, right_high, preferred_element_type=f32)
-    )
-
-
-def gram(a, b):
-    return lax.dot_general(
-        a, b, (((0,), (0,)), ((), ())), precision=highest, preferred_element_type=f32
-    )
-
-
-def prepare(basis, rows, mass):
+    count = left.shape[0]
+    parts = split(left)
+    both = jnp.dot(jnp.concatenate(parts, axis=0), right_high, preferred_element_type=f32)
+    rest = jnp.dot(parts[0], right_low, preferred_element_type=f32)
+    return both[0:count] + both[count:] + rest
+
+
+def split3(value):
+    high, rest = split(value)
+    middle, low = split(value - high.astype(f32))
+    return high, middle, low
+
+
+def exact(left, right, across=False):
+    if left.dtype == f32:
+        left = jnp.concatenate(split3(left), axis=0)
+    count = left.shape[0] // 3
+    dims = (((1,), (1 if across else 0,)), ((), ()))
+    total = None
+    for k, part in reversed(list(enumerate(split3(right)))):
+        value = lax.dot_general(
+            left[0 : (3 - k) * count], part, dims, preferred_element_type=f32
+        )
+        for m in reversed(range(3 - k)):
+            piece = value[m * count : (m + 1) * count]
+            total = piece if total is None else total + piece
+    return total
+
+
+def prepare(basis, rows, turned, mass, wide):
+    wide[...] = jnp.zeros((768, 256), f32)
     for c in range(3):
         for y in range(SIDE):
             row = 256 * c + 16 * y
-            rows[row : row + 16, :] = basis[c, :, y * NCOL : (y + 1) * NCOL]
-    value = rows[...]
-    mass[...] = gram(value, value)
+            value = basis[c, :, y * NCOL : (y + 1) * NCOL]
+            rows[row : row + 16, :] = value
+            wide[row : row + 16, 0:NCOL] = value
+    parts = split3(wide[...].T[0:NCOL, :])
+    for k in range(3):
+        turned[k * NCOL : (k + 1) * NCOL, :] = parts[k]
+    mass[...] = exact(turned[...], rows[...])
 
 
 def block_masks(s, table):
@@ -280,7 +299,7 @@
 
 
 def stiffness(
-    rows, mass, own, below, above, high_own, low_own, dil_high_own, dil_low_own, forces,
+    turned, mass, own, below, above, high_own, low_own, dil_high_own, dil_low_own, forces,
     result, grams,
     geo, geo_cols, geo_far, high, low, dil_high, dil_low,
 ):
@@ -329,7 +348,7 @@
 
     lax.fori_loop(0, 4, images, 0, unroll=2)
 
-    stiff = gram(rows[...], result[...])
+    stiff = exact(turned[...], result[...])
     at_row = lax.broadcasted_iota(jnp.int32, (NCOL, NCOL), 0)
     at_col = lax.broadcasted_iota(jnp.int32, (NCOL, NCOL), 1)
     packed = jnp.where(at_row >= at_col, mass[...], stiff)
@@ -427,19 +446,17 @@
         lanes = slice(128 * halves[0], 256)
         reduce_block(work, base, base, halves, None)
         rest = [slice(64 * other, 64 * other + 64) for other in range(3) if other != block]
-        change = jnp.dot(
+        change = exact(
             jnp.concatenate([work[part, base : base + 64] for part in rest], axis=0),
             work[base : base + 64, lanes],
-            precision=highest,
-            preferred_element_type=f32,
         )
         work[rest[0], lanes] = work[rest[0], lanes] - change[0:64]
         work[rest[1], lanes] = work[rest[1], lanes] - change[64:128]
     solved = work[:, 192:256]
-    weighted = jnp.dot(mass, solved, precision=highest, preferred_element_type=f32)
+    weighted = exact(mass, solved)
     square[0:192, 0:64] = solved
     turned = square[...].T[0:64, 0:192]
-    small[:, 0:64] = jnp.dot(turned, weighted, precision=highest, preferred_element_type=f32)
+    small[:, 0:64] = exact(turned, weighted)
     small[:, 64:256] = turned
 
     def keep(t, caught):
@@ -459,14 +476,15 @@
         value = source[...].reshape(24, 2, SIDE, NCOL)
         total = jnp.zeros((384, 128), f32)
         for at, (high, low) in ((0, even), (1, odd)):
-            first, second = split(value[:, at].reshape(384, NCOL))
-            total = total + dot(first, high) + dot(first, low) + dot(second, high)
+            parts = split(value[:, at].reshape(384, NCOL))
+            both = dot(jnp.concatenate(parts, axis=0), high)
+            total = total + both[0:384] + both[384:] + dot(parts[0], low)
         for c in range(3):
             for y in range(SIDE // 2):
                 row = 128 * c + 16 * y
                 out[c, :, 128 * y : 128 * y + 128] = total[row : row + 16]
-    lifted = lax.dot_general(stiff, rotate, across, precision=highest, preferred_element_type=f32)
-    reduced[...] = jnp.dot(rotate, lifted, precision=highest, preferred_element_type=f32)
+    lifted = exact(stiff, rotate, True)
+    reduced[...] = exact(rotate, lifted)
 
 
 def exchange(up, down, axis):
@@ -496,8 +514,13 @@
             "pack_x",
         )
         left, right = exchange(up, down, "slab")
-        rows, mass = call(
-            prepare, [(768, NCOL), (NCOL, NCOL)], [], (hold(basis),), 3 * 10**8, "prepare"
+        rows, turned, mass = call(
+            prepare,
+            [(768, NCOL), ((3 * NCOL, 768), bf16), (NCOL, NCOL)],
+            [pltpu.VMEM((768, 256), f32)],
+            (hold(basis),),
+            3 * 10**8,
+            "prepare",
         )
         up, down, own = call(
             pack_y, [(88, 1152)] * 2 + [(8, 512)], [], (hold(basis), hold(geo), hold(left), hold(right)), 1000, "pack_y"
@@ -505,7 +528,9 @@
         below, above = exchange(up, down, "band")
 
     with jax.named_scope("stiffness"):
-        rows, mass, left, right, own = [hold(a) for a in (rows, mass, left, right, own)]
+        rows, turned, mass, left, right, own = [
+            hold(a) for a in (rows, turned, mass, left, right, own)
+        ]
         places = [
             pltpu.VMEM((8, 1024), f32),
             pltpu.VMEM((1024, 8), f32),
@@ -525,7 +550,7 @@
             places
             + [pltpu.VMEM((3, 1024, NCOL), bf16)] * 2
             + [pltpu.VMEM((1024, NCOL), bf16)] * 2,
-            (rows, mass, own, hold(below), hold(above), *[hold(a) for a in middle]),
+            (turned, mass, own, hold(below), hold(above), *[hold(a) for a in middle]),
             2 * 10**9,
             "stiffness",
         )

time: 99.8 us -> 100 us (level)
  no operation moved by 1% of the time
where the time goes in v6:
time: 100 us; the launch traced here: 99.9 us
  blocking collectives  54.3 us (54%)
  Pallas kernels  20.6 us (21%)
  starting transfers between devices  14.2 us (14%)
  waiting for transfers between devices  8.88 us (9%)
  local copies, waits for them, and re-layouts  1.03 us (1%)
    all_to_all x2, blocking collectives, spread(): lax.all_to_all(jnp.broadcast_to(value[None], (size,) + value.shape), axis...  33 us
    all_to_all x1, blocking collectives, local(): lax.all_to_all(grams.reshape(slabs, 1, 40960 // slabs), 'slab', 0, 0, til...  21.2 us
    pallas_call x6, Pallas kernels, call(): pl.pallas_call(kernel, out_shape=[(pltpu.VMEM if near else jax.ShapeDtype...  20.6 us
    ppermute x4, starting transfers between devices, exchange(): return (lax.ppermute(up, axis, forward), lax.ppermute(down, axis, backward))  14.2 us
    ppermute x4, waiting for transfers between devices, exchange(): return (lax.ppermute(up, axis, forward), lax.ppermute(down, axis, backward))  8.88 us
  transfers between devices with their start and end apart: 4, of which 3 were waited for; matrix products, arithmetic and copies ran while one was open for 0% of the time, Pallas kernels for 4%

profile of v6, /device:TPU:1, one launch (start us, length us, event | category | flops | bytes accessed | tf_op | source)
XLA Modules:
  0.0 99.9 jit_solution(10045440578849276020)
XLA Ops:
  0.6 0.0 copy-start
  0.6 1.6 %pack_x.1 = (f32[152,384]{1,0:T(8,128)S(1)}, f32[152,384]{1,0:T(8,128)S(1)}, f32[8,256]{1,0:T(8,128)S(1)}) custom-call(f32[3,16,3072]{2,1,0:T(8,128)} %basis.5, f32[3,16,16]{2,1,0:T(8,128)} %offsets.1, f32[16,16]{1,0:T(8,128)} %bond.1, f32[16,16]{1,0:T(8,128)} %bulk.1, f32[16,16]{1,0:T(8,128)} %springs.1, s32[1,2,9]{2,1,0:T(2,128)} %intact.1), custom_call_target="tpu_custom_call" | custom-call | flops 1000 | bytes 596040 | tf_op jit(solution)/shard_map/halo/pack_x/pallas_call | solution.py:31
  2.2 4.0 %collective-permute-start = (f32[152,384]{1,0:T(8,128)S(1)}, f32[152,384]{1,0:T(8,128)S(1)}, u32[]{:S(2)}, u32[]{:S(2)}) collective-permute-start(f32[152,384]{1,0:T(8,128)S(1)} %get-tuple-element.22), channel_id=1, source_target_pairs={{0,16},{16,32},{32,48},{48,64},{64,80},{80,96},{96,112},{112,128},... | collective-permute-start | bytes 700424 | tf_op jit(solution)/shard_map/halo/ppermute | solution.py:494
  6.2 1.3 %collective-permute-start.1 = (f32[152,384]{1,0:T(8,128)S(1)}, f32[152,384]{1,0:T(8,128)S(1)}, u32[]{:S(2)}, u32[]{:S(2)}) collective-permute-start(f32[152,384]{1,0:T(8,128)S(1)} %get-tuple-element.23), channel_id=1, source_target_pairs={{16,0},{32,16},{48,32},{64,48},{80,64},{96,80},{112,96},{128,112},... | collective-permute-start | bytes 700424 | tf_op jit(solution)/shard_map/halo/ppermute | solution.py:494
  7.5 1.7 %collective-permute-done.left = f32[152,384]{1,0:T(8,128)S(1)} collective-permute-done((f32[152,384]{1,0:T(8,128)S(1)}, f32[152,384]{1,0:T(8,128)S(1)}, u32[]{:S(2)}, u32[]{:S(2)}) %collective-permute-start) | collective-permute-done | bytes 233504 | tf_op jit(solution)/shard_map/halo/ppermute | solution.py:494
  9.2 3.8 %collective-permute-done.1.right = f32[152,384]{1,0:T(8,128)S(1)} collective-permute-done((f32[152,384]{1,0:T(8,128)S(1)}, f32[152,384]{1,0:T(8,128)S(1)}, u32[]{:S(2)}, u32[]{:S(2)}) %collective-permute-start.1) | collective-permute-done | bytes 233504 | tf_op jit(solution)/shard_map/halo/ppermute | solution.py:494
  13.0 0.0 copy-done
  13.0 0.2 pack_y.1
  13.2 7.1 %collective-permute-start.2 = (f32[88,1152]{1,0:T(8,128)S(1)}, f32[88,1152]{1,0:T(8,128)S(1)}, u32[]{:S(2)}, u32[]{:S(2)}) collective-permute-start(f32[88,1152]{1,0:T(8,128)S(1)} %get-tuple-element.25), channel_id=1, source_target_pairs={{0,1},{1,2},{2,3},{3,4},{4,5},{5,6},{6,7},{7,8},{8,9},{9,10},{10,1... | collective-permute-start | bytes 1216520 | tf_op jit(solution)/shard_map/halo/ppermute | solution.py:494
  20.3 1.9 %collective-permute-start.3 = (f32[88,1152]{1,0:T(8,128)S(1)}, f32[88,1152]{1,0:T(8,128)S(1)}, u32[]{:S(2)}, u32[]{:S(2)}) collective-permute-start(f32[88,1152]{1,0:T(8,128)S(1)} %get-tuple-element.26), channel_id=1, source_target_pairs={{1,0},{2,1},{3,2},{4,3},{5,4},{6,5},{7,6},{8,7},{9,8},{10,9},{11,1... | collective-permute-start | bytes 1216520 | tf_op jit(solution)/shard_map/halo/ppermute | solution.py:494
  22.2 0.9 prepare.1
  23.1 3.0 %inner.1 = (bf16[3,512,192]{2,1,0:T(8,128)(2,1)S(1)}, bf16[3,512,192]{2,1,0:T(8,128)(2,1)S(1)}, bf16[256,192]{1,0:T(8,128)(2,1)S(1)}, bf16[256,192]{1,0:T(8,128)(2,1)S(1)}, f32[3,128,192]{2,1,0:T(8,128)S(1)}) custom-call(f32[768,192]{1,0:T(8,128)S(1)} %get-tuple-element.27.rows.refs_1_, f32[152,384]{1,0:T(8,128)S(1)} %collective-permute-done.left, ...), custom_call_target="tpu_custom_call" | custom-call | flops 1000000000 | bytes 1073152 | tf_op jit(solution)/shard_map/stiffness/inner/pallas_call | solution.py:31
  26.1 0.0 collective-permute-done.2.below
  26.2 3.4 %collective-permute-done.3.above = f32[88,1152]{1,0:T(8,128)S(1)} collective-permute-done((f32[88,1152]{1,0:T(8,128)S(1)}, f32[88,1152]{1,0:T(8,128)S(1)}, u32[]{:S(2)}, u32[]{:S(2)}) %collective-permute-start.3) | collective-permute-done | bytes 405536 | tf_op jit(solution)/shard_map/halo/ppermute | solution.py:494
  29.5 5.3 %stiffness.1 = (f32[768,192]{1,0:T(8,128)S(1)}, f32[320,128]{1,0:T(8,128)S(1)}) custom-call(bf16[576,768]{1,0:T(8,128)(2,1)S(1)} %get-tuple-element.19.turned, f32[192,192]{1,0:T(8,128)S(1)} %get-tuple-element.20.mass, f32[8,512]{1,0:T(8,128)S(1)} %get-tuple-element.24.own, f32[88,1152]{1,0:T(8,128)S(1)} %collective-permute-done.2.below, ...), custom_call_target="tpu_custom_call" | custom-call | flops 2000000000 | bytes 5791744 | tf_op jit(solution)/shard_map/stiffness/stiffness/pallas_call | solution.py:31
  34.8 0.9 copy-done.1
  35.7 21.2 %all_to_all.15 = f32[32,1,1280]{2,1,0:T(1,128)S(1)} all-to-all(f32[32,1,1280]{2,1,0:T(1,128)S(1)} %bitcast.2), channel_id=1, replica_groups=mesh['slab'=32,'band'=16] {'slab'}, dimensions={0} | all-to-all | bytes 327680 | tf_op jit(solution)/shard_map/sums/all_to_all | solution.py:559
  56.9 0.1 reduce_sum.18
  57.1 19.8 %all_to_all.16 = f32[16,1,1280]{2,1,0:T(1,128)S(1)} all-to-all(f32[16,1,1280]{2,1,0:T(1,128)S(1)} %broadcast_in_dim.4), channel_id=1, replica_groups=mesh['slab'=32,'band'=16] {'band'}, dimensions={0} | all-to-all | bytes 163840 | tf_op jit(solution)/shard_map/sums/all_to_all | solution.py:499
  76.9 0.1 reduce_sum.19
  76.9 0.1 broadcast_in_dim.5
  77.0 13.2 %all_to_all.17 = f32[32,1,1280]{2,1,0:T(1,128)S(1)} all-to-all(f32[32,1,1280]{2,1,0:T(1,128)S(1)} %broadcast_in_dim.5), channel_id=1, replica_groups=mesh['slab'=32,'band'=16] {'slab'}, dimensions={0} | all-to-all | bytes 327680 | tf_op jit(solution)/shard_map/sums/all_to_all | solution.py:499
  90.3 0.0 copy-done.2
  90.3 9.6 %rotation.1 = (f32[3,16,1024]{2,1,0:T(8,128)}, f32[3,16,1024]{2,1,0:T(8,128)}, f32[64,64]{1,0:T(8,128)}) custom-call(f32[320,128]{1,0:T(8,128)S(1)} %bitcast.3, f32[768,192]{1,0:T(8,128)S(1)} %get-tuple-element.27.rows.refs_1_, f32[768,192]{1,0:T(8,128)S(1)} %copy-done.2), custom_call_target="tpu_custom_call" | custom-call | flops 1000000000 | bytes 1343488 | tf_op jit(solution)/shard_map/rotation/rotation/pallas_call | solution.py:31
  (3 shorter events, 0.0 us)
Async XLA Ops:
  0.6 12.4 %copy-start = (f32[3,16,3072]{2,1,0:T(8,128)S(1)}, f32[3,16,3072]{2,1,0:T(8,128)}, u32[]{:S(2)}) copy-start(f32[3,16,3072]{2,1,0:T(8,128)} %basis.5) | copy-start | bytes 1769476
  2.2 6.9 %collective-permute-start = (f32[152,384]{1,0:T(8,128)S(1)}, f32[152,384]{1,0:T(8,128)S(1)}, u32[]{:S(2)}, u32[]{:S(2)}) collective-permute-start(f32[152,384]{1,0:T(8,128)S(1)} %get-tuple-element.22), channel_id=1, source_target_pairs={{0,16},{16,32},{32,48},{48,64},{64,80},{80,96},{96,112},{112,128},... | collective-permute-start | bytes 700424 | tf_op jit(solution)/shard_map/halo/ppermute | solution.py:494
  6.2 6.8 %collective-permute-start.1 = (f32[152,384]{1,0:T(8,128)S(1)}, f32[152,384]{1,0:T(8,128)S(1)}, u32[]{:S(2)}, u32[]{:S(2)}) collective-permute-start(f32[152,384]{1,0:T(8,128)S(1)} %get-tuple-element.23), channel_id=1, source_target_pairs={{16,0},{32,16},{48,32},{64,48},{80,64},{96,80},{112,96},{128,112},... | collective-permute-start | bytes 700424 | tf_op jit(solution)/shard_map/halo/ppermute | solution.py:494
  13.2 12.9 %collective-permute-start.2 = (f32[88,1152]{1,0:T(8,128)S(1)}, f32[88,1152]{1,0:T(8,128)S(1)}, u32[]{:S(2)}, u32[]{:S(2)}) collective-permute-start(f32[88,1152]{1,0:T(8,128)S(1)} %get-tuple-element.25), channel_id=1, source_target_pairs={{0,1},{1,2},{2,3},{3,4},{4,5},{5,6},{6,7},{7,8},{8,9},{9,10},{10,1... | collective-permute-start | bytes 1216520 | tf_op jit(solution)/shard_map/halo/ppermute | solution.py:494
  20.3 9.2 %collective-permute-start.3 = (f32[88,1152]{1,0:T(8,128)S(1)}, f32[88,1152]{1,0:T(8,128)S(1)}, u32[]{:S(2)}, u32[]{:S(2)}) collective-permute-start(f32[88,1152]{1,0:T(8,128)S(1)} %get-tuple-element.26), channel_id=1, source_target_pairs={{1,0},{2,1},{3,2},{4,3},{5,4},{6,5},{7,6},{8,7},{9,8},{10,9},{11,1... | collective-permute-start | bytes 1216520 | tf_op jit(solution)/shard_map/halo/ppermute | solution.py:494
  34.8 0.9 copy-start.1
  35.7 54.6 %copy-start.2 = (f32[768,192]{1,0:T(8,128)S(1)}, f32[768,192]{1,0:T(8,128)}, u32[]{:S(2)}) copy-start(f32[768,192]{1,0:T(8,128)} %copy-done.1) | copy-start | bytes 1769476

commit v7 on v6

--- a/solution.py
+++ b/solution.py
@@ -18,14 +18,13 @@
 bf16 = jnp.bfloat16
 
 VMEM = pl.BlockSpec(memory_space=pltpu.VMEM)
-PARAMS = pltpu.CompilerParams(vmem_limit_bytes=56 * 1024 * 1024)
 
 
 def hold(value):
     return pltpu.with_memory_space_constraint(value, pltpu.VMEM)
 
 
-def call(kernel, outs, scratch, args, flops, name, near=True):
+def call(kernel, outs, scratch, args, flops, name, near=True, room=24):
     outs = [(o, f32) if isinstance(o[0], int) else o for o in outs]
     size = sum(a.size for a in args)
     return pl.pallas_call(
@@ -34,7 +33,7 @@
         in_specs=[VMEM] * len(args),
         out_specs=[VMEM] * len(outs),
         scratch_shapes=scratch,
-        compiler_params=PARAMS,
+        compiler_params=pltpu.CompilerParams(vmem_limit_bytes=room * 1024 * 1024),
         cost_estimate=pl.CostEstimate(flops=flops, bytes_accessed=4 * size, transcendentals=0),
         name=name,
     )(*args)
@@ -512,6 +511,7 @@
             (basis, offsets, bond_modulus, bulk_modulus, springs, intact),
             1000,
             "pack_x",
+            room=56,
         )
         left, right = exchange(up, down, "slab")
         rows, turned, mass = call(

time: 100 us -> 99.1 us (level)
  no operation moved by 1% of the time
where the time goes in v7:
time: 99.1 us; the launch traced here: 98.8 us
  blocking collectives  54.1 us (55%)
  Pallas kernels  20.5 us (21%)
  starting transfers between devices  14.2 us (14%)
  waiting for transfers between devices  8.88 us (9%)
    all_to_all x2, blocking collectives, spread(): lax.all_to_all(jnp.broadcast_to(value[None], (size,) + value.shape), axis...  33 us
    all_to_all x1, blocking collectives, local(): lax.all_to_all(grams.reshape(slabs, 1, 40960 // slabs), 'slab', 0, 0, til...  21.1 us
    pallas_call x6, Pallas kernels, call(): pl.pallas_call(kernel, out_shape=[(pltpu.VMEM if near else jax.ShapeDtype...  20.5 us
    ppermute x4, starting transfers between devices, exchange(): return (lax.ppermute(up, axis, forward), lax.ppermute(down, axis, backward))  14.2 us
    ppermute x4, waiting for transfers between devices, exchange(): return (lax.ppermute(up, axis, forward), lax.ppermute(down, axis, backward))  8.88 us
  transfers between devices with their start and end apart: 4, of which 3 were waited for; matrix products, arithmetic and copies ran while one was open for 0% of the time, Pallas kernels for 4%

profile of v7, /device:TPU:1, one launch (start us, length us, event | category | flops | bytes accessed | tf_op | source)
XLA Modules:
  0.0 98.8 jit_solution(17250859313010585863)
XLA Ops:
  0.6 0.0 copy-start
  0.6 1.6 %pack_x.1 = (f32[152,384]{1,0:T(8,128)S(1)}, f32[152,384]{1,0:T(8,128)S(1)}, f32[8,256]{1,0:T(8,128)S(1)}) custom-call(f32[3,16,3072]{2,1,0:T(8,128)} %basis.5, f32[3,16,16]{2,1,0:T(8,128)} %offsets.1, f32[16,16]{1,0:T(8,128)} %bond.1, f32[16,16]{1,0:T(8,128)} %bulk.1, f32[16,16]{1,0:T(8,128)} %springs.1, s32[1,2,9]{2,1,0:T(2,128)} %intact.1), custom_call_target="tpu_custom_call" | custom-call | flops 1000 | bytes 596040 | tf_op jit(solution)/shard_map/halo/pack_x/pallas_call | solution.py:30
  2.2 4.0 %collective-permute-start = (f32[152,384]{1,0:T(8,128)S(1)}, f32[152,384]{1,0:T(8,128)S(1)}, u32[]{:S(2)}, u32[]{:S(2)}) collective-permute-start(f32[152,384]{1,0:T(8,128)S(1)} %get-tuple-element.22), channel_id=1, source_target_pairs={{0,16},{16,32},{32,48},{48,64},{64,80},{80,96},{96,112},{112,128},... | collective-permute-start | bytes 700424 | tf_op jit(solution)/shard_map/halo/ppermute | solution.py:493
  6.2 1.3 %collective-permute-start.1 = (f32[152,384]{1,0:T(8,128)S(1)}, f32[152,384]{1,0:T(8,128)S(1)}, u32[]{:S(2)}, u32[]{:S(2)}) collective-permute-start(f32[152,384]{1,0:T(8,128)S(1)} %get-tuple-element.23), channel_id=1, source_target_pairs={{16,0},{32,16},{48,32},{64,48},{80,64},{96,80},{112,96},{128,112},... | collective-permute-start | bytes 700424 | tf_op jit(solution)/shard_map/halo/ppermute | solution.py:493
  7.5 1.7 %collective-permute-done.left = f32[152,384]{1,0:T(8,128)S(1)} collective-permute-done((f32[152,384]{1,0:T(8,128)S(1)}, f32[152,384]{1,0:T(8,128)S(1)}, u32[]{:S(2)}, u32[]{:S(2)}) %collective-permute-start) | collective-permute-done | bytes 233504 | tf_op jit(solution)/shard_map/halo/ppermute | solution.py:493
  9.2 3.8 %collective-permute-done.1.right = f32[152,384]{1,0:T(8,128)S(1)} collective-permute-done((f32[152,384]{1,0:T(8,128)S(1)}, f32[152,384]{1,0:T(8,128)S(1)}, u32[]{:S(2)}, u32[]{:S(2)}) %collective-permute-start.1) | collective-permute-done | bytes 233504 | tf_op jit(solution)/shard_map/halo/ppermute | solution.py:493
  13.0 0.0 copy-done
  13.0 0.2 pack_y.1
  13.2 7.1 %collective-permute-start.2 = (f32[88,1152]{1,0:T(8,128)S(1)}, f32[88,1152]{1,0:T(8,128)S(1)}, u32[]{:S(2)}, u32[]{:S(2)}) collective-permute-start(f32[88,1152]{1,0:T(8,128)S(1)} %get-tuple-element.25), channel_id=1, source_target_pairs={{0,1},{1,2},{2,3},{3,4},{4,5},{5,6},{6,7},{7,8},{8,9},{9,10},{10,1... | collective-permute-start | bytes 1216520 | tf_op jit(solution)/shard_map/halo/ppermute | solution.py:493
  20.3 1.9 %collective-permute-start.3 = (f32[88,1152]{1,0:T(8,128)S(1)}, f32[88,1152]{1,0:T(8,128)S(1)}, u32[]{:S(2)}, u32[]{:S(2)}) collective-permute-start(f32[88,1152]{1,0:T(8,128)S(1)} %get-tuple-element.26), channel_id=1, source_target_pairs={{1,0},{2,1},{3,2},{4,3},{5,4},{6,5},{7,6},{8,7},{9,8},{10,9},{11,1... | collective-permute-start | bytes 1216520 | tf_op jit(solution)/shard_map/halo/ppermute | solution.py:493
  22.2 0.9 prepare.1
  23.1 3.0 %inner.1 = (bf16[3,512,192]{2,1,0:T(8,128)(2,1)S(1)}, bf16[3,512,192]{2,1,0:T(8,128)(2,1)S(1)}, bf16[256,192]{1,0:T(8,128)(2,1)S(1)}, bf16[256,192]{1,0:T(8,128)(2,1)S(1)}, f32[3,128,192]{2,1,0:T(8,128)S(1)}) custom-call(f32[768,192]{1,0:T(8,128)S(1)} %get-tuple-element.27.rows.refs_1_, f32[152,384]{1,0:T(8,128)S(1)} %collective-permute-done.left, ...), custom_call_target="tpu_custom_call" | custom-call | flops 1000000000 | bytes 1073152 | tf_op jit(solution)/shard_map/stiffness/inner/pallas_call | solution.py:30
  26.1 0.0 collective-permute-done.2.below
  26.2 3.4 %collective-permute-done.3.above = f32[88,1152]{1,0:T(8,128)S(1)} collective-permute-done((f32[88,1152]{1,0:T(8,128)S(1)}, f32[88,1152]{1,0:T(8,128)S(1)}, u32[]{:S(2)}, u32[]{:S(2)}) %collective-permute-start.3) | collective-permute-done | bytes 405536 | tf_op jit(solution)/shard_map/halo/ppermute | solution.py:493
  29.5 5.3 %stiffness.1 = (f32[768,192]{1,0:T(8,128)S(1)}, f32[320,128]{1,0:T(8,128)S(1)}) custom-call(bf16[576,768]{1,0:T(8,128)(2,1)S(1)} %get-tuple-element.19.turned, f32[192,192]{1,0:T(8,128)S(1)} %get-tuple-element.20.mass, f32[8,512]{1,0:T(8,128)S(1)} %get-tuple-element.24.own, f32[88,1152]{1,0:T(8,128)S(1)} %collective-permute-done.2.below, ...), custom_call_target="tpu_custom_call" | custom-call | flops 2000000000 | bytes 5791744 | tf_op jit(solution)/shard_map/stiffness/stiffness/pallas_call | solution.py:30
  34.8 21.1 %all_to_all.15 = f32[32,1,1280]{2,1,0:T(1,128)S(1)} all-to-all(f32[32,1,1280]{2,1,0:T(1,128)S(1)} %bitcast.2), channel_id=1, replica_groups=mesh['slab'=32,'band'=16] {'slab'}, dimensions={0} | all-to-all | bytes 327680 | tf_op jit(solution)/shard_map/sums/all_to_all | solution.py:559
  55.9 0.1 reduce_sum.18
  56.1 19.8 %all_to_all.16 = f32[16,1,1280]{2,1,0:T(1,128)S(1)} all-to-all(f32[16,1,1280]{2,1,0:T(1,128)S(1)} %broadcast_in_dim.4), channel_id=1, replica_groups=mesh['slab'=32,'band'=16] {'band'}, dimensions={0} | all-to-all | bytes 163840 | tf_op jit(solution)/shard_map/sums/all_to_all | solution.py:498
  75.8 0.1 reduce_sum.19
  75.9 0.1 broadcast_in_dim.5
  76.0 13.2 %all_to_all.17 = f32[32,1,1280]{2,1,0:T(1,128)S(1)} all-to-all(f32[32,1,1280]{2,1,0:T(1,128)S(1)} %broadcast_in_dim.5), channel_id=1, replica_groups=mesh['slab'=32,'band'=16] {'slab'}, dimensions={0} | all-to-all | bytes 327680 | tf_op jit(solution)/shard_map/sums/all_to_all | solution.py:498
  89.2 9.6 %rotation.1 = (f32[3,16,1024]{2,1,0:T(8,128)}, f32[3,16,1024]{2,1,0:T(8,128)}, f32[64,64]{1,0:T(8,128)}) custom-call(f32[320,128]{1,0:T(8,128)S(1)} %bitcast.3, f32[768,192]{1,0:T(8,128)S(1)} %get-tuple-element.27.rows.refs_1_, f32[768,192]{1,0:T(8,128)S(1)} %get-tuple-element.34.refs_2_), custom_call_target="tpu_custom_call" | custom-call | flops 1000000000 | bytes 1343488 | tf_op jit(solution)/shard_map/rotation/rotation/pallas_call | solution.py:30
  (1 shorter events, 0.0 us)
Async XLA Ops:
  0.6 12.4 %copy-start = (f32[3,16,3072]{2,1,0:T(8,128)S(1)}, f32[3,16,3072]{2,1,0:T(8,128)}, u32[]{:S(2)}) copy-start(f32[3,16,3072]{2,1,0:T(8,128)} %basis.5) | copy-start | bytes 1769476
  2.2 6.9 %collective-permute-start = (f32[152,384]{1,0:T(8,128)S(1)}, f32[152,384]{1,0:T(8,128)S(1)}, u32[]{:S(2)}, u32[]{:S(2)}) collective-permute-start(f32[152,384]{1,0:T(8,128)S(1)} %get-tuple-element.22), channel_id=1, source_target_pairs={{0,16},{16,32},{32,48},{48,64},{64,80},{80,96},{96,112},{112,128},... | collective-permute-start | bytes 700424 | tf_op jit(solution)/shard_map/halo/ppermute | solution.py:493
  6.2 6.8 %collective-permute-start.1 = (f32[152,384]{1,0:T(8,128)S(1)}, f32[152,384]{1,0:T(8,128)S(1)}, u32[]{:S(2)}, u32[]{:S(2)}) collective-permute-start(f32[152,384]{1,0:T(8,128)S(1)} %get-tuple-element.23), channel_id=1, source_target_pairs={{16,0},{32,16},{48,32},{64,48},{80,64},{96,80},{112,96},{128,112},... | collective-permute-start | bytes 700424 | tf_op jit(solution)/shard_map/halo/ppermute | solution.py:493
  13.2 12.9 %collective-permute-start.2 = (f32[88,1152]{1,0:T(8,128)S(1)}, f32[88,1152]{1,0:T(8,128)S(1)}, u32[]{:S(2)}, u32[]{:S(2)}) collective-permute-start(f32[88,1152]{1,0:T(8,128)S(1)} %get-tuple-element.25), channel_id=1, source_target_pairs={{0,1},{1,2},{2,3},{3,4},{4,5},{5,6},{6,7},{7,8},{8,9},{9,10},{10,1... | collective-permute-start | bytes 1216520 | tf_op jit(solution)/shard_map/halo/ppermute | solution.py:493
  20.3 9.2 %collective-permute-start.3 = (f32[88,1152]{1,0:T(8,128)S(1)}, f32[88,1152]{1,0:T(8,128)S(1)}, u32[]{:S(2)}, u32[]{:S(2)}) collective-permute-start(f32[88,1152]{1,0:T(8,128)S(1)} %get-tuple-element.26), channel_id=1, source_target_pairs={{1,0},{2,1},{3,2},{4,3},{5,4},{6,5},{7,6},{8,7},{9,8},{10,9},{11,1... | collective-permute-start | bytes 1216520 | tf_op jit(solution)/shard_map/halo/ppermute | solution.py:493

commit v8 on v7

--- a/solution.py
+++ b/solution.py
@@ -393,7 +393,7 @@
             pivot = row_of(pivots[i], i)
             inverse = 1.0 / pivot
             chosen = at == i
-            factor = jnp.where(chosen, -inverse, pivots[i] * inverse)
+            factor = jnp.where(chosen, -1.0, pivots[i]) * inverse
 
             def step(value):
                 return jnp.where(chosen, 0.0, value) - factor * row_of(value, i)
@@ -425,7 +425,9 @@
                 ref[row : row + 8, 128 * h : 128 * h + 128] = value
 
 
-def rotation(scale, grams, rows, images, modes, mode_images, reduced, square, work, small, factor):
+def rotation(
+    scale, grams, rows, images, modes, mode_images, reduced, square, work, small, factor, moved,
+):
     square[...] = jnp.zeros((256, 256), f32)
     square[0:192, 0:128] = grams[0:192, :] * scale
     square[0:96, 128:192] = grams[192:288, 0:64] * scale
@@ -456,34 +458,40 @@
     square[0:192, 0:64] = solved
     turned = square[...].T[0:64, 0:192]
     small[:, 0:64] = exact(turned, weighted)
-    small[:, 64:256] = turned
+    at_row = lax.broadcasted_iota(jnp.int32, (64, 64), 0)
+    at_col = lax.broadcasted_iota(jnp.int32, (64, 64), 1)
+    small[:, 64:128] = jnp.where(at_row == at_col, 1.0, 0.0)
+    energy = exact(turned, exact(stiff, solved))
+    for k, source in enumerate((rows, images)):
+        value = source[...].reshape(24, 2, SIDE, NCOL)
+        value = jnp.concatenate([value[:, h].reshape(384, NCOL) for h in range(2)], axis=0)
+        value = exact(value, solved)
+        parts = split(jnp.concatenate([value[0:384], value[384:768]], axis=1))
+        moved[k, 0:384, :] = parts[0]
+        moved[k, 384:768, :] = parts[1]
+    upper = lax.broadcasted_iota(jnp.int32, (8, 128), 1) < 64
 
     def keep(t, caught):
-        factor[8 * t : 8 * t + 8, :] = jnp.concatenate(caught, axis=1)[:, 64:256]
-
-    reduce_block(small, 0, 0, (0, 1), keep)
-    rotate = factor[...]
-    blank = jnp.zeros((64, NCOL), f32)
-    even = split(jnp.concatenate([rotate, blank], axis=0))
-    odd = split(jnp.concatenate([blank, rotate], axis=0))
+        value = caught[0]
+        factor[8 * t : 8 * t + 8, :] = jnp.where(upper, pltpu.roll(value, 64, 1), 0.0)
+        factor[64 + 8 * t : 72 + 8 * t, :] = jnp.where(upper, 0.0, value)
+
+    reduce_block(small, 0, 0, (0,), keep)
+    high, low = split(factor[...])
     across = (((1,), (1,)), ((), ()))
 
     def dot(left, right):
         return lax.dot_general(left, right, across, preferred_element_type=f32)
 
-    for source, out in ((rows, modes), (images, mode_images)):
-        value = source[...].reshape(24, 2, SIDE, NCOL)
-        total = jnp.zeros((384, 128), f32)
-        for at, (high, low) in ((0, even), (1, odd)):
-            parts = split(value[:, at].reshape(384, NCOL))
-            both = dot(jnp.concatenate(parts, axis=0), high)
-            total = total + both[0:384] + both[384:] + dot(parts[0], low)
+    for k, out in enumerate((modes, mode_images)):
+        both = dot(moved[k], high)
+        total = both[0:384] + both[384:] + dot(moved[k, 0:384], low)
         for c in range(3):
             for y in range(SIDE // 2):
                 row = 128 * c + 16 * y
                 out[c, :, 128 * y : 128 * y + 128] = total[row : row + 16]
-    lifted = exact(stiff, rotate, True)
-    reduced[...] = exact(rotate, lifted)
+    inverse = factor[0:64, 0:64]
+    reduced[...] = exact(exact(inverse, energy), inverse, True)
 
 
 def exchange(up, down, axis):
@@ -571,8 +579,9 @@
             [
                 pltpu.VMEM((256, 256), f32),
                 pltpu.VMEM((192, 256), f32),
-                pltpu.VMEM((64, 256), f32),
-                pltpu.VMEM((64, NCOL), f32),
+                pltpu.VMEM((64, 128), f32),
+                pltpu.VMEM((128, 128), f32),
+                pltpu.VMEM((2, 768, 128), bf16),
             ],
             (hold(grams), hold(rows), hold(images)),
             10**9,

time: 99.1 us -> 98.7 us (level)
  no operation moved by 1% of the time
where the time goes in v8:
time: 98.7 us; the launch traced here: 98.4 us
  blocking collectives  54.1 us (55%)
  Pallas kernels  20.1 us (20%)
  starting transfers between devices  14.2 us (14%)
  waiting for transfers between devices  8.88 us (9%)
    all_to_all x2, blocking collectives, spread(): lax.all_to_all(jnp.broadcast_to(value[None], (size,) + value.shape), axis...  33 us
    all_to_all x1, blocking collectives, local(): lax.all_to_all(grams.reshape(slabs, 1, 40960 // slabs), 'slab', 0, 0, til...  21.1 us
    pallas_call x6, Pallas kernels, call(): pl.pallas_call(kernel, out_shape=[(pltpu.VMEM if near else jax.ShapeDtype...  20.1 us
    ppermute x4, starting transfers between devices, exchange(): return (lax.ppermute(up, axis, forward), lax.ppermute(down, axis, backward))  14.2 us
    ppermute x4, waiting for transfers between devices, exchange(): return (lax.ppermute(up, axis, forward), lax.ppermute(down, axis, backward))  8.88 us
  transfers between devices with their start and end apart: 4, of which 3 were waited for; matrix products, arithmetic and copies ran while one was open for 0% of the time, Pallas kernels for 4%

profile of v8, /device:TPU:1, one launch (start us, length us, event | category | flops | bytes accessed | tf_op | source)
XLA Modules:
  0.0 98.4 jit_solution(18329727352672597822)
XLA Ops:
  0.6 0.0 copy-start
  0.6 1.6 %pack_x.1 = (f32[152,384]{1,0:T(8,128)S(1)}, f32[152,384]{1,0:T(8,128)S(1)}, f32[8,256]{1,0:T(8,128)S(1)}) custom-call(f32[3,16,3072]{2,1,0:T(8,128)} %basis.5, f32[3,16,16]{2,1,0:T(8,128)} %offsets.1, f32[16,16]{1,0:T(8,128)} %bond.1, f32[16,16]{1,0:T(8,128)} %bulk.1, f32[16,16]{1,0:T(8,128)} %springs.1, s32[1,2,9]{2,1,0:T(2,128)} %intact.1), custom_call_target="tpu_custom_call" | custom-call | flops 1000 | bytes 596040 | tf_op jit(solution)/shard_map/halo/pack_x/pallas_call | solution.py:30
  2.2 4.0 %collective-permute-start = (f32[152,384]{1,0:T(8,128)S(1)}, f32[152,384]{1,0:T(8,128)S(1)}, u32[]{:S(2)}, u32[]{:S(2)}) collective-permute-start(f32[152,384]{1,0:T(8,128)S(1)} %get-tuple-element.22), channel_id=1, source_target_pairs={{0,16},{16,32},{32,48},{48,64},{64,80},{80,96},{96,112},{112,128},... | collective-permute-start | bytes 700424 | tf_op jit(solution)/shard_map/halo/ppermute | solution.py:501
  6.2 1.3 %collective-permute-start.1 = (f32[152,384]{1,0:T(8,128)S(1)}, f32[152,384]{1,0:T(8,128)S(1)}, u32[]{:S(2)}, u32[]{:S(2)}) collective-permute-start(f32[152,384]{1,0:T(8,128)S(1)} %get-tuple-element.23), channel_id=1, source_target_pairs={{16,0},{32,16},{48,32},{64,48},{80,64},{96,80},{112,96},{128,112},... | collective-permute-start | bytes 700424 | tf_op jit(solution)/shard_map/halo/ppermute | solution.py:501
  7.5 1.7 %collective-permute-done.left = f32[152,384]{1,0:T(8,128)S(1)} collective-permute-done((f32[152,384]{1,0:T(8,128)S(1)}, f32[152,384]{1,0:T(8,128)S(1)}, u32[]{:S(2)}, u32[]{:S(2)}) %collective-permute-start) | collective-permute-done | bytes 233504 | tf_op jit(solution)/shard_map/halo/ppermute | solution.py:501
  9.2 3.8 %collective-permute-done.1.right = f32[152,384]{1,0:T(8,128)S(1)} collective-permute-done((f32[152,384]{1,0:T(8,128)S(1)}, f32[152,384]{1,0:T(8,128)S(1)}, u32[]{:S(2)}, u32[]{:S(2)}) %collective-permute-start.1) | collective-permute-done | bytes 233504 | tf_op jit(solution)/shard_map/halo/ppermute | solution.py:501
  13.0 0.0 copy-done
  13.0 0.2 pack_y.1
  13.2 7.1 %collective-permute-start.2 = (f32[88,1152]{1,0:T(8,128)S(1)}, f32[88,1152]{1,0:T(8,128)S(1)}, u32[]{:S(2)}, u32[]{:S(2)}) collective-permute-start(f32[88,1152]{1,0:T(8,128)S(1)} %get-tuple-element.25), channel_id=1, source_target_pairs={{0,1},{1,2},{2,3},{3,4},{4,5},{5,6},{6,7},{7,8},{8,9},{9,10},{10,1... | collective-permute-start | bytes 1216520 | tf_op jit(solution)/shard_map/halo/ppermute | solution.py:501
  20.3 1.9 %collective-permute-start.3 = (f32[88,1152]{1,0:T(8,128)S(1)}, f32[88,1152]{1,0:T(8,128)S(1)}, u32[]{:S(2)}, u32[]{:S(2)}) collective-permute-start(f32[88,1152]{1,0:T(8,128)S(1)} %get-tuple-element.26), channel_id=1, source_target_pairs={{1,0},{2,1},{3,2},{4,3},{5,4},{6,5},{7,6},{8,7},{9,8},{10,9},{11,1... | collective-permute-start | bytes 1216520 | tf_op jit(solution)/shard_map/halo/ppermute | solution.py:501
  22.2 0.9 prepare.1
  23.1 3.0 %inner.1 = (bf16[3,512,192]{2,1,0:T(8,128)(2,1)S(1)}, bf16[3,512,192]{2,1,0:T(8,128)(2,1)S(1)}, bf16[256,192]{1,0:T(8,128)(2,1)S(1)}, bf16[256,192]{1,0:T(8,128)(2,1)S(1)}, f32[3,128,192]{2,1,0:T(8,128)S(1)}) custom-call(f32[768,192]{1,0:T(8,128)S(1)} %get-tuple-element.27.rows.refs_1_, f32[152,384]{1,0:T(8,128)S(1)} %collective-permute-done.left, ...), custom_call_target="tpu_custom_call" | custom-call | flops 1000000000 | bytes 1073152 | tf_op jit(solution)/shard_map/stiffness/inner/pallas_call | solution.py:30
  26.1 0.0 collective-permute-done.2.below
  26.2 3.4 %collective-permute-done.3.above = f32[88,1152]{1,0:T(8,128)S(1)} collective-permute-done((f32[88,1152]{1,0:T(8,128)S(1)}, f32[88,1152]{1,0:T(8,128)S(1)}, u32[]{:S(2)}, u32[]{:S(2)}) %collective-permute-start.3) | collective-permute-done | bytes 405536 | tf_op jit(solution)/shard_map/halo/ppermute | solution.py:501
  29.5 5.3 %stiffness.1 = (f32[768,192]{1,0:T(8,128)S(1)}, f32[320,128]{1,0:T(8,128)S(1)}) custom-call(bf16[576,768]{1,0:T(8,128)(2,1)S(1)} %get-tuple-element.19.turned, f32[192,192]{1,0:T(8,128)S(1)} %get-tuple-element.20.mass, f32[8,512]{1,0:T(8,128)S(1)} %get-tuple-element.24.own, f32[88,1152]{1,0:T(8,128)S(1)} %collective-permute-done.2.below, ...), custom_call_target="tpu_custom_call" | custom-call | flops 2000000000 | bytes 5791744 | tf_op jit(solution)/shard_map/stiffness/stiffness/pallas_call | solution.py:30
  34.8 21.1 %all_to_all.15 = f32[32,1,1280]{2,1,0:T(1,128)S(1)} all-to-all(f32[32,1,1280]{2,1,0:T(1,128)S(1)} %bitcast.2), channel_id=1, replica_groups=mesh['slab'=32,'band'=16] {'slab'}, dimensions={0} | all-to-all | bytes 327680 | tf_op jit(solution)/shard_map/sums/all_to_all | solution.py:567
  55.9 0.1 reduce_sum.18
  56.1 19.8 %all_to_all.16 = f32[16,1,1280]{2,1,0:T(1,128)S(1)} all-to-all(f32[16,1,1280]{2,1,0:T(1,128)S(1)} %broadcast_in_dim.4), channel_id=1, replica_groups=mesh['slab'=32,'band'=16] {'band'}, dimensions={0} | all-to-all | bytes 163840 | tf_op jit(solution)/shard_map/sums/all_to_all | solution.py:506
  75.8 0.1 reduce_sum.19
  75.9 0.1 broadcast_in_dim.5
  76.0 13.2 %all_to_all.17 = f32[32,1,1280]{2,1,0:T(1,128)S(1)} all-to-all(f32[32,1,1280]{2,1,0:T(1,128)S(1)} %broadcast_in_dim.5), channel_id=1, replica_groups=mesh['slab'=32,'band'=16] {'slab'}, dimensions={0} | all-to-all | bytes 327680 | tf_op jit(solution)/shard_map/sums/all_to_all | solution.py:506
  89.2 9.2 %rotation.1 = (f32[3,16,1024]{2,1,0:T(8,128)}, f32[3,16,1024]{2,1,0:T(8,128)}, f32[64,64]{1,0:T(8,128)}) custom-call(f32[320,128]{1,0:T(8,128)S(1)} %bitcast.3, f32[768,192]{1,0:T(8,128)S(1)} %get-tuple-element.27.rows.refs_1_, f32[768,192]{1,0:T(8,128)S(1)} %get-tuple-element.34.refs_2_), custom_call_target="tpu_custom_call" | custom-call | flops 1000000000 | bytes 1343488 | tf_op jit(solution)/shard_map/rotation/rotation/pallas_call | solution.py:30
  (1 shorter events, 0.0 us)
Async XLA Ops:
  0.6 12.4 %copy-start = (f32[3,16,3072]{2,1,0:T(8,128)S(1)}, f32[3,16,3072]{2,1,0:T(8,128)}, u32[]{:S(2)}) copy-start(f32[3,16,3072]{2,1,0:T(8,128)} %basis.5) | copy-start | bytes 1769476
  2.2 6.9 %collective-permute-start = (f32[152,384]{1,0:T(8,128)S(1)}, f32[152,384]{1,0:T(8,128)S(1)}, u32[]{:S(2)}, u32[]{:S(2)}) collective-permute-start(f32[152,384]{1,0:T(8,128)S(1)} %get-tuple-element.22), channel_id=1, source_target_pairs={{0,16},{16,32},{32,48},{48,64},{64,80},{80,96},{96,112},{112,128},... | collective-permute-start | bytes 700424 | tf_op jit(solution)/shard_map/halo/ppermute | solution.py:501
  6.2 6.8 %collective-permute-start.1 = (f32[152,384]{1,0:T(8,128)S(1)}, f32[152,384]{1,0:T(8,128)S(1)}, u32[]{:S(2)}, u32[]{:S(2)}) collective-permute-start(f32[152,384]{1,0:T(8,128)S(1)} %get-tuple-element.23), channel_id=1, source_target_pairs={{16,0},{32,16},{48,32},{64,48},{80,64},{96,80},{112,96},{128,112},... | collective-permute-start | bytes 700424 | tf_op jit(solution)/shard_map/halo/ppermute | solution.py:501
  13.2 12.9 %collective-permute-start.2 = (f32[88,1152]{1,0:T(8,128)S(1)}, f32[88,1152]{1,0:T(8,128)S(1)}, u32[]{:S(2)}, u32[]{:S(2)}) collective-permute-start(f32[88,1152]{1,0:T(8,128)S(1)} %get-tuple-element.25), channel_id=1, source_target_pairs={{0,1},{1,2},{2,3},{3,4},{4,5},{5,6},{6,7},{7,8},{8,9},{9,10},{10,1... | collective-permute-start | bytes 1216520 | tf_op jit(solution)/shard_map/halo/ppermute | solution.py:501
  20.3 9.2 %collective-permute-start.3 = (f32[88,1152]{1,0:T(8,128)S(1)}, f32[88,1152]{1,0:T(8,128)S(1)}, u32[]{:S(2)}, u32[]{:S(2)}) collective-permute-start(f32[88,1152]{1,0:T(8,128)S(1)} %get-tuple-element.26), channel_id=1, source_target_pairs={{1,0},{2,1},{3,2},{4,3},{5,4},{6,5},{7,6},{8,7},{9,8},{10,9},{11,1... | collective-permute-start | bytes 1216520 | tf_op jit(solution)/shard_map/halo/ppermute | solution.py:501

commit v9 on v8

--- a/solution.py
+++ b/solution.py
@@ -465,7 +465,7 @@
     for k, source in enumerate((rows, images)):
         value = source[...].reshape(24, 2, SIDE, NCOL)
         value = jnp.concatenate([value[:, h].reshape(384, NCOL) for h in range(2)], axis=0)
-        value = exact(value, solved)
+        value = product(value, *split(solved))
         parts = split(jnp.concatenate([value[0:384], value[384:768]], axis=1))
         moved[k, 0:384, :] = parts[0]
         moved[k, 384:768, :] = parts[1]

time: 98.7 us -> 98.4 us (level)
  no operation moved by 1% of the time
where the time goes in v9:
time: 98.4 us; the launch traced here: 98.1 us
  blocking collectives  54.1 us (55%)
  Pallas kernels  19.8 us (20%)
  starting transfers between devices  14.2 us (14%)
  waiting for transfers between devices  8.88 us (9%)
    all_to_all x2, blocking collectives, spread(): lax.all_to_all(jnp.broadcast_to(value[None], (size,) + value.shape), axis...  33 us
    all_to_all x1, blocking collectives, local(): lax.all_to_all(grams.reshape(slabs, 1, 40960 // slabs), 'slab', 0, 0, til...  21.1 us
    pallas_call x6, Pallas kernels, call(): pl.pallas_call(kernel, out_shape=[(pltpu.VMEM if near else jax.ShapeDtype...  19.8 us
    ppermute x4, starting transfers between devices, exchange(): return (lax.ppermute(up, axis, forward), lax.ppermute(down, axis, backward))  14.2 us
    ppermute x4, waiting for transfers between devices, exchange(): return (lax.ppermute(up, axis, forward), lax.ppermute(down, axis, backward))  8.88 us
  transfers between devices with their start and end apart: 4, of which 3 were waited for; matrix products, arithmetic and copies ran while one was open for 0% of the time, Pallas kernels for 4%

profile of v9, /device:TPU:1, one launch (start us, length us, event | category | flops | bytes accessed | tf_op | source)
XLA Modules:
  0.0 98.1 jit_solution(5179532006627587878)
XLA Ops:
  0.6 0.0 copy-start
  0.6 1.6 %pack_x.1 = (f32[152,384]{1,0:T(8,128)S(1)}, f32[152,384]{1,0:T(8,128)S(1)}, f32[8,256]{1,0:T(8,128)S(1)}) custom-call(f32[3,16,3072]{2,1,0:T(8,128)} %basis.5, f32[3,16,16]{2,1,0:T(8,128)} %offsets.1, f32[16,16]{1,0:T(8,128)} %bond.1, f32[16,16]{1,0:T(8,128)} %bulk.1, f32[16,16]{1,0:T(8,128)} %springs.1, s32[1,2,9]{2,1,0:T(2,128)} %intact.1), custom_call_target="tpu_custom_call" | custom-call | flops 1000 | bytes 596040 | tf_op jit(solution)/shard_map/halo/pack_x/pallas_call | solution.py:30
  2.2 4.0 %collective-permute-start = (f32[152,384]{1,0:T(8,128)S(1)}, f32[152,384]{1,0:T(8,128)S(1)}, u32[]{:S(2)}, u32[]{:S(2)}) collective-permute-start(f32[152,384]{1,0:T(8,128)S(1)} %get-tuple-element.22), channel_id=1, source_target_pairs={{0,16},{16,32},{32,48},{48,64},{64,80},{80,96},{96,112},{112,128},... | collective-permute-start | bytes 700424 | tf_op jit(solution)/shard_map/halo/ppermute | solution.py:501
  6.2 1.3 %collective-permute-start.1 = (f32[152,384]{1,0:T(8,128)S(1)}, f32[152,384]{1,0:T(8,128)S(1)}, u32[]{:S(2)}, u32[]{:S(2)}) collective-permute-start(f32[152,384]{1,0:T(8,128)S(1)} %get-tuple-element.23), channel_id=1, source_target_pairs={{16,0},{32,16},{48,32},{64,48},{80,64},{96,80},{112,96},{128,112},... | collective-permute-start | bytes 700424 | tf_op jit(solution)/shard_map/halo/ppermute | solution.py:501
  7.5 1.7 %collective-permute-done.left = f32[152,384]{1,0:T(8,128)S(1)} collective-permute-done((f32[152,384]{1,0:T(8,128)S(1)}, f32[152,384]{1,0:T(8,128)S(1)}, u32[]{:S(2)}, u32[]{:S(2)}) %collective-permute-start) | collective-permute-done | bytes 233504 | tf_op jit(solution)/shard_map/halo/ppermute | solution.py:501
  9.2 3.8 %collective-permute-done.1.right = f32[152,384]{1,0:T(8,128)S(1)} collective-permute-done((f32[152,384]{1,0:T(8,128)S(1)}, f32[152,384]{1,0:T(8,128)S(1)}, u32[]{:S(2)}, u32[]{:S(2)}) %collective-permute-start.1) | collective-permute-done | bytes 233504 | tf_op jit(solution)/shard_map/halo/ppermute | solution.py:501
  13.0 0.0 copy-done
  13.0 0.2 pack_y.1
  13.2 7.1 %collective-permute-start.2 = (f32[88,1152]{1,0:T(8,128)S(1)}, f32[88,1152]{1,0:T(8,128)S(1)}, u32[]{:S(2)}, u32[]{:S(2)}) collective-permute-start(f32[88,1152]{1,0:T(8,128)S(1)} %get-tuple-element.25), channel_id=1, source_target_pairs={{0,1},{1,2},{2,3},{3,4},{4,5},{5,6},{6,7},{7,8},{8,9},{9,10},{10,1... | collective-permute-start | bytes 1216520 | tf_op jit(solution)/shard_map/halo/ppermute | solution.py:501
  20.3 1.9 %collective-permute-start.3 = (f32[88,1152]{1,0:T(8,128)S(1)}, f32[88,1152]{1,0:T(8,128)S(1)}, u32[]{:S(2)}, u32[]{:S(2)}) collective-permute-start(f32[88,1152]{1,0:T(8,128)S(1)} %get-tuple-element.26), channel_id=1, source_target_pairs={{1,0},{2,1},{3,2},{4,3},{5,4},{6,5},{7,6},{8,7},{9,8},{10,9},{11,1... | collective-permute-start | bytes 1216520 | tf_op jit(solution)/shard_map/halo/ppermute | solution.py:501
  22.2 0.9 prepare.1
  23.1 3.0 %inner.1 = (bf16[3,512,192]{2,1,0:T(8,128)(2,1)S(1)}, bf16[3,512,192]{2,1,0:T(8,128)(2,1)S(1)}, bf16[256,192]{1,0:T(8,128)(2,1)S(1)}, bf16[256,192]{1,0:T(8,128)(2,1)S(1)}, f32[3,128,192]{2,1,0:T(8,128)S(1)}) custom-call(f32[768,192]{1,0:T(8,128)S(1)} %get-tuple-element.27.rows.refs_1_, f32[152,384]{1,0:T(8,128)S(1)} %collective-permute-done.left, ...), custom_call_target="tpu_custom_call" | custom-call | flops 1000000000 | bytes 1073152 | tf_op jit(solution)/shard_map/stiffness/inner/pallas_call | solution.py:30
  26.1 0.0 collective-permute-done.2.below
  26.2 3.4 %collective-permute-done.3.above = f32[88,1152]{1,0:T(8,128)S(1)} collective-permute-done((f32[88,1152]{1,0:T(8,128)S(1)}, f32[88,1152]{1,0:T(8,128)S(1)}, u32[]{:S(2)}, u32[]{:S(2)}) %collective-permute-start.3) | collective-permute-done | bytes 405536 | tf_op jit(solution)/shard_map/halo/ppermute | solution.py:501
  29.5 5.3 %stiffness.1 = (f32[768,192]{1,0:T(8,128)S(1)}, f32[320,128]{1,0:T(8,128)S(1)}) custom-call(bf16[576,768]{1,0:T(8,128)(2,1)S(1)} %get-tuple-element.19.turned, f32[192,192]{1,0:T(8,128)S(1)} %get-tuple-element.20.mass, f32[8,512]{1,0:T(8,128)S(1)} %get-tuple-element.24.own, f32[88,1152]{1,0:T(8,128)S(1)} %collective-permute-done.2.below, ...), custom_call_target="tpu_custom_call" | custom-call | flops 2000000000 | bytes 5791744 | tf_op jit(solution)/shard_map/stiffness/stiffness/pallas_call | solution.py:30
  34.8 21.1 %all_to_all.15 = f32[32,1,1280]{2,1,0:T(1,128)S(1)} all-to-all(f32[32,1,1280]{2,1,0:T(1,128)S(1)} %bitcast.2), channel_id=1, replica_groups=mesh['slab'=32,'band'=16] {'slab'}, dimensions={0} | all-to-all | bytes 327680 | tf_op jit(solution)/shard_map/sums/all_to_all | solution.py:567
  55.9 0.1 reduce_sum.18
  56.1 19.8 %all_to_all.16 = f32[16,1,1280]{2,1,0:T(1,128)S(1)} all-to-all(f32[16,1,1280]{2,1,0:T(1,128)S(1)} %broadcast_in_dim.4), channel_id=1, replica_groups=mesh['slab'=32,'band'=16] {'band'}, dimensions={0} | all-to-all | bytes 163840 | tf_op jit(solution)/shard_map/sums/all_to_all | solution.py:506
  75.8 0.1 reduce_sum.19
  75.9 0.1 broadcast_in_dim.5
  76.0 13.2 %all_to_all.17 = f32[32,1,1280]{2,1,0:T(1,128)S(1)} all-to-all(f32[32,1,1280]{2,1,0:T(1,128)S(1)} %broadcast_in_dim.5), channel_id=1, replica_groups=mesh['slab'=32,'band'=16] {'slab'}, dimensions={0} | all-to-all | bytes 327680 | tf_op jit(solution)/shard_map/sums/all_to_all | solution.py:506
  89.2 8.9 %rotation.1 = (f32[3,16,1024]{2,1,0:T(8,128)}, f32[3,16,1024]{2,1,0:T(8,128)}, f32[64,64]{1,0:T(8,128)}) custom-call(f32[320,128]{1,0:T(8,128)S(1)} %bitcast.3, f32[768,192]{1,0:T(8,128)S(1)} %get-tuple-element.27.rows.refs_1_, f32[768,192]{1,0:T(8,128)S(1)} %get-tuple-element.34.refs_2_), custom_call_target="tpu_custom_call" | custom-call | flops 1000000000 | bytes 1343488 | tf_op jit(solution)/shard_map/rotation/rotation/pallas_call | solution.py:30
  (1 shorter events, 0.0 us)
Async XLA Ops:
  0.6 12.4 %copy-start = (f32[3,16,3072]{2,1,0:T(8,128)S(1)}, f32[3,16,3072]{2,1,0:T(8,128)}, u32[]{:S(2)}) copy-start(f32[3,16,3072]{2,1,0:T(8,128)} %basis.5) | copy-start | bytes 1769476
  2.2 6.9 %collective-permute-start = (f32[152,384]{1,0:T(8,128)S(1)}, f32[152,384]{1,0:T(8,128)S(1)}, u32[]{:S(2)}, u32[]{:S(2)}) collective-permute-start(f32[152,384]{1,0:T(8,128)S(1)} %get-tuple-element.22), channel_id=1, source_target_pairs={{0,16},{16,32},{32,48},{48,64},{64,80},{80,96},{96,112},{112,128},... | collective-permute-start | bytes 700424 | tf_op jit(solution)/shard_map/halo/ppermute | solution.py:501
  6.2 6.8 %collective-permute-start.1 = (f32[152,384]{1,0:T(8,128)S(1)}, f32[152,384]{1,0:T(8,128)S(1)}, u32[]{:S(2)}, u32[]{:S(2)}) collective-permute-start(f32[152,384]{1,0:T(8,128)S(1)} %get-tuple-element.23), channel_id=1, source_target_pairs={{16,0},{32,16},{48,32},{64,48},{80,64},{96,80},{112,96},{128,112},... | collective-permute-start | bytes 700424 | tf_op jit(solution)/shard_map/halo/ppermute | solution.py:501
  13.2 12.9 %collective-permute-start.2 = (f32[88,1152]{1,0:T(8,128)S(1)}, f32[88,1152]{1,0:T(8,128)S(1)}, u32[]{:S(2)}, u32[]{:S(2)}) collective-permute-start(f32[88,1152]{1,0:T(8,128)S(1)} %get-tuple-element.25), channel_id=1, source_target_pairs={{0,1},{1,2},{2,3},{3,4},{4,5},{5,6},{6,7},{7,8},{8,9},{9,10},{10,1... | collective-permute-start | bytes 1216520 | tf_op jit(solution)/shard_map/halo/ppermute | solution.py:501
  20.3 9.2 %collective-permute-start.3 = (f32[88,1152]{1,0:T(8,128)S(1)}, f32[88,1152]{1,0:T(8,128)S(1)}, u32[]{:S(2)}, u32[]{:S(2)}) collective-permute-start(f32[88,1152]{1,0:T(8,128)S(1)} %get-tuple-element.26), channel_id=1, source_target_pairs={{1,0},{2,1},{3,2},{4,3},{5,4},{6,5},{7,6},{8,7},{9,8},{10,9},{11,1... | collective-permute-start | bytes 1216520 | tf_op jit(solution)/shard_map/halo/ppermute | solution.py:501

commit v10 on v9

--- a/solution.py
+++ b/solution.py
@@ -326,7 +326,7 @@
         dil_low[pl.ds(near, 64), :] = parts[1]
         return carry
 
-    lax.fori_loop(0, 8, ends, 0, unroll=4)
+    lax.fori_loop(0, 8, ends, 0, unroll=8)
 
     def images(i, carry):
         tasks = []
@@ -345,7 +345,7 @@
                 result[pl.ds(pl.multiple_of(at + 256 * k, 32), 32), :] = image[32 * k : 32 * k + 32]
         return carry
 
-    lax.fori_loop(0, 4, images, 0, unroll=2)
+    lax.fori_loop(0, 4, images, 0, unroll=4)
 
     stiff = exact(turned[...], result[...])
     at_row = lax.broadcasted_iota(jnp.int32, (NCOL, NCOL), 0)

time: 98.4 us -> 98.8 us (level)
  no operation moved by 1% of the time
where the time goes in v10:
time: 98.8 us; the launch traced here: 98.5 us
  blocking collectives  54.1 us (55%)
  Pallas kernels  20.2 us (20%)
  starting transfers between devices  14.2 us (14%)
  waiting for transfers between devices  8.88 us (9%)
    all_to_all x2, blocking collectives, spread(): lax.all_to_all(jnp.broadcast_to(value[None], (size,) + value.shape), axis...  33 us
    all_to_all x1, blocking collectives, local(): lax.all_to_all(grams.reshape(slabs, 1, 40960 // slabs), 'slab', 0, 0, til...  21.1 us
    pallas_call x6, Pallas kernels, call(): pl.pallas_call(kernel, out_shape=[(pltpu.VMEM if near else jax.ShapeDtype...  20.2 us
    ppermute x4, starting transfers between devices, exchange(): return (lax.ppermute(up, axis, forward), lax.ppermute(down, axis, backward))  14.2 us
    ppermute x4, waiting for transfers between devices, exchange(): return (lax.ppermute(up, axis, forward), lax.ppermute(down, axis, backward))  8.88 us
  transfers between devices with their start and end apart: 4, of which 3 were waited for; matrix products, arithmetic and copies ran while one was open for 0% of the time, Pallas kernels for 4%

profile of v10, /device:TPU:1, one launch (start us, length us, event | category | flops | bytes accessed | tf_op | source)
XLA Modules:
  0.0 98.5 jit_solution(16553080805587318950)
XLA Ops:
  0.6 0.0 copy-start
  0.6 1.6 %pack_x.1 = (f32[152,384]{1,0:T(8,128)S(1)}, f32[152,384]{1,0:T(8,128)S(1)}, f32[8,256]{1,0:T(8,128)S(1)}) custom-call(f32[3,16,3072]{2,1,0:T(8,128)} %basis.5, f32[3,16,16]{2,1,0:T(8,128)} %offsets.1, f32[16,16]{1,0:T(8,128)} %bond.1, f32[16,16]{1,0:T(8,128)} %bulk.1, f32[16,16]{1,0:T(8,128)} %springs.1, s32[1,2,9]{2,1,0:T(2,128)} %intact.1), custom_call_target="tpu_custom_call" | custom-call | flops 1000 | bytes 596040 | tf_op jit(solution)/shard_map/halo/pack_x/pallas_call | solution.py:30
  2.2 4.0 %collective-permute-start = (f32[152,384]{1,0:T(8,128)S(1)}, f32[152,384]{1,0:T(8,128)S(1)}, u32[]{:S(2)}, u32[]{:S(2)}) collective-permute-start(f32[152,384]{1,0:T(8,128)S(1)} %get-tuple-element.22), channel_id=1, source_target_pairs={{0,16},{16,32},{32,48},{48,64},{64,80},{80,96},{96,112},{112,128},... | collective-permute-start | bytes 700424 | tf_op jit(solution)/shard_map/halo/ppermute | solution.py:501
  6.2 1.3 %collective-permute-start.1 = (f32[152,384]{1,0:T(8,128)S(1)}, f32[152,384]{1,0:T(8,128)S(1)}, u32[]{:S(2)}, u32[]{:S(2)}) collective-permute-start(f32[152,384]{1,0:T(8,128)S(1)} %get-tuple-element.23), channel_id=1, source_target_pairs={{16,0},{32,16},{48,32},{64,48},{80,64},{96,80},{112,96},{128,112},... | collective-permute-start | bytes 700424 | tf_op jit(solution)/shard_map/halo/ppermute | solution.py:501
  7.5 1.7 %collective-permute-done.left = f32[152,384]{1,0:T(8,128)S(1)} collective-permute-done((f32[152,384]{1,0:T(8,128)S(1)}, f32[152,384]{1,0:T(8,128)S(1)}, u32[]{:S(2)}, u32[]{:S(2)}) %collective-permute-start) | collective-permute-done | bytes 233504 | tf_op jit(solution)/shard_map/halo/ppermute | solution.py:501
  9.2 3.8 %collective-permute-done.1.right = f32[152,384]{1,0:T(8,128)S(1)} collective-permute-done((f32[152,384]{1,0:T(8,128)S(1)}, f32[152,384]{1,0:T(8,128)S(1)}, u32[]{:S(2)}, u32[]{:S(2)}) %collective-permute-start.1) | collective-permute-done | bytes 233504 | tf_op jit(solution)/shard_map/halo/ppermute | solution.py:501
  13.0 0.0 copy-done
  13.0 0.2 pack_y.1
  13.2 7.1 %collective-permute-start.2 = (f32[88,1152]{1,0:T(8,128)S(1)}, f32[88,1152]{1,0:T(8,128)S(1)}, u32[]{:S(2)}, u32[]{:S(2)}) collective-permute-start(f32[88,1152]{1,0:T(8,128)S(1)} %get-tuple-element.25), channel_id=1, source_target_pairs={{0,1},{1,2},{2,3},{3,4},{4,5},{5,6},{6,7},{7,8},{8,9},{9,10},{10,1... | collective-permute-start | bytes 1216520 | tf_op jit(solution)/shard_map/halo/ppermute | solution.py:501
  20.3 1.9 %collective-permute-start.3 = (f32[88,1152]{1,0:T(8,128)S(1)}, f32[88,1152]{1,0:T(8,128)S(1)}, u32[]{:S(2)}, u32[]{:S(2)}) collective-permute-start(f32[88,1152]{1,0:T(8,128)S(1)} %get-tuple-element.26), channel_id=1, source_target_pairs={{1,0},{2,1},{3,2},{4,3},{5,4},{6,5},{7,6},{8,7},{9,8},{10,9},{11,1... | collective-permute-start | bytes 1216520 | tf_op jit(solution)/shard_map/halo/ppermute | solution.py:501
  22.2 0.9 prepare.1
  23.1 3.0 %inner.1 = (bf16[3,512,192]{2,1,0:T(8,128)(2,1)S(1)}, bf16[3,512,192]{2,1,0:T(8,128)(2,1)S(1)}, bf16[256,192]{1,0:T(8,128)(2,1)S(1)}, bf16[256,192]{1,0:T(8,128)(2,1)S(1)}, f32[3,128,192]{2,1,0:T(8,128)S(1)}) custom-call(f32[768,192]{1,0:T(8,128)S(1)} %get-tuple-element.27.rows.refs_1_, f32[152,384]{1,0:T(8,128)S(1)} %collective-permute-done.left, ...), custom_call_target="tpu_custom_call" | custom-call | flops 1000000000 | bytes 1073152 | tf_op jit(solution)/shard_map/stiffness/inner/pallas_call | solution.py:30
  26.1 0.0 collective-permute-done.2.below
  26.2 3.4 %collective-permute-done.3.above = f32[88,1152]{1,0:T(8,128)S(1)} collective-permute-done((f32[88,1152]{1,0:T(8,128)S(1)}, f32[88,1152]{1,0:T(8,128)S(1)}, u32[]{:S(2)}, u32[]{:S(2)}) %collective-permute-start.3) | collective-permute-done | bytes 405536 | tf_op jit(solution)/shard_map/halo/ppermute | solution.py:501
  29.5 5.6 %stiffness.1 = (f32[768,192]{1,0:T(8,128)S(1)}, f32[320,128]{1,0:T(8,128)S(1)}) custom-call(bf16[576,768]{1,0:T(8,128)(2,1)S(1)} %get-tuple-element.19.turned, f32[192,192]{1,0:T(8,128)S(1)} %get-tuple-element.20.mass, f32[8,512]{1,0:T(8,128)S(1)} %get-tuple-element.24.own, f32[88,1152]{1,0:T(8,128)S(1)} %collective-permute-done.2.below, ...), custom_call_target="tpu_custom_call" | custom-call | flops 2000000000 | bytes 5791744 | tf_op jit(solution)/shard_map/stiffness/stiffness/pallas_call | solution.py:30
  35.2 21.1 %all_to_all.15 = f32[32,1,1280]{2,1,0:T(1,128)S(1)} all-to-all(f32[32,1,1280]{2,1,0:T(1,128)S(1)} %bitcast.2), channel_id=1, replica_groups=mesh['slab'=32,'band'=16] {'slab'}, dimensions={0} | all-to-all | bytes 327680 | tf_op jit(solution)/shard_map/sums/all_to_all | solution.py:567
  56.3 0.1 reduce_sum.18
  56.4 19.8 %all_to_all.16 = f32[16,1,1280]{2,1,0:T(1,128)S(1)} all-to-all(f32[16,1,1280]{2,1,0:T(1,128)S(1)} %broadcast_in_dim.4), channel_id=1, replica_groups=mesh['slab'=32,'band'=16] {'band'}, dimensions={0} | all-to-all | bytes 163840 | tf_op jit(solution)/shard_map/sums/all_to_all | solution.py:506
  76.2 0.1 reduce_sum.19
  76.3 0.1 broadcast_in_dim.5
  76.3 13.3 %all_to_all.17 = f32[32,1,1280]{2,1,0:T(1,128)S(1)} all-to-all(f32[32,1,1280]{2,1,0:T(1,128)S(1)} %broadcast_in_dim.5), channel_id=1, replica_groups=mesh['slab'=32,'band'=16] {'slab'}, dimensions={0} | all-to-all | bytes 327680 | tf_op jit(solution)/shard_map/sums/all_to_all | solution.py:506
  89.6 8.9 %rotation.1 = (f32[3,16,1024]{2,1,0:T(8,128)}, f32[3,16,1024]{2,1,0:T(8,128)}, f32[64,64]{1,0:T(8,128)}) custom-call(f32[320,128]{1,0:T(8,128)S(1)} %bitcast.3, f32[768,192]{1,0:T(8,128)S(1)} %get-tuple-element.27.rows.refs_1_, f32[768,192]{1,0:T(8,128)S(1)} %get-tuple-element.34.refs_2_), custom_call_target="tpu_custom_call" | custom-call | flops 1000000000 | bytes 1343488 | tf_op jit(solution)/shard_map/rotation/rotation/pallas_call | solution.py:30
  (1 shorter events, 0.0 us)
Async XLA Ops:
  0.6 12.4 %copy-start = (f32[3,16,3072]{2,1,0:T(8,128)S(1)}, f32[3,16,3072]{2,1,0:T(8,128)}, u32[]{:S(2)}) copy-start(f32[3,16,3072]{2,1,0:T(8,128)} %basis.5) | copy-start | bytes 1769476
  2.2 6.9 %collective-permute-start = (f32[152,384]{1,0:T(8,128)S(1)}, f32[152,384]{1,0:T(8,128)S(1)}, u32[]{:S(2)}, u32[]{:S(2)}) collective-permute-start(f32[152,384]{1,0:T(8,128)S(1)} %get-tuple-element.22), channel_id=1, source_target_pairs={{0,16},{16,32},{32,48},{48,64},{64,80},{80,96},{96,112},{112,128},... | collective-permute-start | bytes 700424 | tf_op jit(solution)/shard_map/halo/ppermute | solution.py:501
  6.2 6.8 %collective-permute-start.1 = (f32[152,384]{1,0:T(8,128)S(1)}, f32[152,384]{1,0:T(8,128)S(1)}, u32[]{:S(2)}, u32[]{:S(2)}) collective-permute-start(f32[152,384]{1,0:T(8,128)S(1)} %get-tuple-element.23), channel_id=1, source_target_pairs={{16,0},{32,16},{48,32},{64,48},{80,64},{96,80},{112,96},{128,112},... | collective-permute-start | bytes 700424 | tf_op jit(solution)/shard_map/halo/ppermute | solution.py:501
  13.2 12.9 %collective-permute-start.2 = (f32[88,1152]{1,0:T(8,128)S(1)}, f32[88,1152]{1,0:T(8,128)S(1)}, u32[]{:S(2)}, u32[]{:S(2)}) collective-permute-start(f32[88,1152]{1,0:T(8,128)S(1)} %get-tuple-element.25), channel_id=1, source_target_pairs={{0,1},{1,2},{2,3},{3,4},{4,5},{5,6},{6,7},{7,8},{8,9},{9,10},{10,1... | collective-permute-start | bytes 1216520 | tf_op jit(solution)/shard_map/halo/ppermute | solution.py:501
  20.3 9.2 %collective-permute-start.3 = (f32[88,1152]{1,0:T(8,128)S(1)}, f32[88,1152]{1,0:T(8,128)S(1)}, u32[]{:S(2)}, u32[]{:S(2)}) collective-permute-start(f32[88,1152]{1,0:T(8,128)S(1)} %get-tuple-element.26), channel_id=1, source_target_pairs={{1,0},{2,1},{3,2},{4,3},{5,4},{6,5},{7,6},{8,7},{9,8},{10,9},{11,1... | collective-permute-start | bytes 1216520 | tf_op jit(solution)/shard_map/halo/ppermute | solution.py:501
